TPU v7x, 32 devices: a whole 2x2x4 slice. The times are simulated.
32 devices in a mesh: dp: 4 (over z), ctx: 2 (over core), tensor: 4 (over y, x).
Axes of the slice: x: 2, y: 2, z: 4, core: 2. Of those that a mesh axis runs over, the one named last changes fastest.
Arguments:
- tokens: bfloat16 [8, 2, 2, 256, 768], P('dp', 'ctx', None, 'tensor'), may hold values from -6 to 6
- cotangent: bfloat16 [8, 2, 2, 256, 768], P('dp', 'ctx', None, 'tensor'), may hold values from -6 to 6
- document_lengths: int32 [8, 8], P('dp'), may hold values from 1 to 512, 1024 in all within a row
- dealing: int32 [8, 7], P('dp'), may hold values from 0 to 6, each once within a row
- query_weight: bfloat16 [768, 768], P(('dp', 'ctx'), 'tensor'), may hold values from -0.21875 to 0.21875
- query_master: float32 [768, 768], P(('dp', 'ctx'), 'tensor'), may hold values from -0.21875 to 0.21875
- query_moment: float32 [768, 768], P(('dp', 'ctx'), 'tensor'), may hold values from -16 to 16
- query_variance: float32 [768, 768], P(('dp', 'ctx'), 'tensor'), may hold values from 5 to 500
- keyvalue_weight: bfloat16 [2, 768, 768], P(None, ('dp', 'ctx'), 'tensor'), may hold values from -0.21875 to 0.21875
- keyvalue_master: float32 [2, 768, 768], P(None, ('dp', 'ctx'), 'tensor'), may hold values from -0.21875 to 0.21875
- keyvalue_moment: float32 [2, 768, 768], P(None, ('dp', 'ctx'), 'tensor'), may hold values from -16 to 16
- keyvalue_variance: float32 [2, 768, 768], P(None, ('dp', 'ctx'), 'tensor'), may hold values from 5 to 500
- output_weight: bfloat16 [768, 768], P('tensor', ('dp', 'ctx')), may hold values from -1.75 to 1.75
- output_master: float32 [768, 768], P('tensor', ('dp', 'ctx')), may hold values from -1.75 to 1.75
- output_moment: float32 [768, 768], P('tensor', ('dp', 'ctx')), may hold values from -16 to 16
- output_variance: float32 [768, 768], P('tensor', ('dp', 'ctx')), may hold values from 5 to 500
- gateup_weight: bfloat16 [2, 768, 2048], P(None, ('dp', 'ctx'), 'tensor'), may hold values from -0.21875 to 0.21875
- gateup_master: float32 [2, 768, 2048], P(None, ('dp', 'ctx'), 'tensor'), may hold values from -0.21875 to 0.21875
- gateup_moment: float32 [2, 768, 2048], P(None, ('dp', 'ctx'), 'tensor'), may hold values from -16 to 16
- gateup_variance: float32 [2, 768, 2048], P(None, ('dp', 'ctx'), 'tensor'), may hold values from 5 to 500
- down_weight: bfloat16 [2048, 768], P('tensor', ('dp', 'ctx')), may hold values from -0.125 to 0.125
- down_master: float32 [2048, 768], P('tensor', ('dp', 'ctx')), may hold values from -0.125 to 0.125
- down_moment: float32 [2048, 768], P('tensor', ('dp', 'ctx')), may hold values from -16 to 16
- down_variance: float32 [2048, 768], P('tensor', ('dp', 'ctx')), may hold values from 5 to 500
- norm_gain: bfloat16 [2, 768], P(None, ('dp', 'ctx')), may hold values from 0.5 to 1.5
- gain_master: float32 [2, 768], P(None, ('dp', 'ctx', 'tensor')), may hold values from 0.5 to 1.5
- gain_moment: float32 [2, 768], P(None, ('dp', 'ctx', 'tensor')), may hold values from -16 to 16
- gain_variance: float32 [2, 768], P(None, ('dp', 'ctx', 'tensor')), may hold values from 5 to 500
Outputs:
- block_output: bfloat16 [8, 2, 2, 256, 768], P('dp', 'ctx', None, 'tensor')
- input_grad: float32 [8, 2, 2, 256, 768], P('dp', 'ctx', None, 'tensor')
- query_grad: float32 [768, 768], P(('dp', 'ctx'), 'tensor')
- master_query: float32 [768, 768], P(('dp', 'ctx'), 'tensor')
- moment_query: float32 [768, 768], P(('dp', 'ctx'), 'tensor')
- variance_query: float32 [768, 768], P(('dp', 'ctx'), 'tensor')
- keyvalue_grad: float32 [2, 768, 768], P(None, ('dp', 'ctx'), 'tensor')
- master_keyvalue: float32 [2, 768, 768], P(None, ('dp', 'ctx'), 'tensor')
- moment_keyvalue: float32 [2, 768, 768], P(None, ('dp', 'ctx'), 'tensor')
- variance_keyvalue: float32 [2, 768, 768], P(None, ('dp', 'ctx'), 'tensor')
- output_grad: float32 [768, 768], P('tensor', ('dp', 'ctx'))
- master_output: float32 [768, 768], P('tensor', ('dp', 'ctx'))
- moment_output: float32 [768, 768], P('tensor', ('dp', 'ctx'))
- variance_output: float32 [768, 768], P('tensor', ('dp', 'ctx'))
- gateup_grad: float32 [2, 768, 2048], P(None, ('dp', 'ctx'), 'tensor')
- master_gateup: float32 [2, 768, 2048], P(None, ('dp', 'ctx'), 'tensor')
- moment_gateup: float32 [2, 768, 2048], P(None, ('dp', 'ctx'), 'tensor')
- variance_gateup: float32 [2, 768, 2048], P(None, ('dp', 'ctx'), 'tensor')
- down_grad: float32 [2048, 768], P('tensor', ('dp', 'ctx'))
- master_down: float32 [2048, 768], P('tensor', ('dp', 'ctx'))
- moment_down: float32 [2048, 768], P('tensor', ('dp', 'ctx'))
- variance_down: float32 [2048, 768], P('tensor', ('dp', 'ctx'))
- gain_grad: float32 [2, 768], P(None, ('dp', 'ctx', 'tensor'))
- master_gain: float32 [2, 768], P(None, ('dp', 'ctx', 'tensor'))
- moment_gain: float32 [2, 768], P(None, ('dp', 'ctx', 'tensor'))
- variance_gain: float32 [2, 768], P(None, ('dp', 'ctx', 'tensor'))
Inputs may be any that keep to these rules, and one draw needn't show every extreme that they name: `document_lengths`: in each row the entries sum to 1024; entries 0 to 6 are the documents' lengths, the last is the padding at the row's end. Each row is a permutation of 0 to 6: document dealing[r, 0] comes first in row r, then dealing[r, 1], and so on.
All inputs are finite; a program needn't handle non-finite values.
Results may differ from a plain program's by a relative error of at most 0.02.
Values may be sent and summed in bfloat16 or wider, within the bound.
No kernel may reach another device: no remote copies, remote signals or barrier semaphores. Data moves between devices by JAX's collectives and lax.ppermute only.
A program may use at most 128 MiB of HBM per device.

v0:
```python
import jax
import jax.numpy as jnp
from jax import lax
from jax.sharding import PartitionSpec as P

H = 12
KVH = 12
HD = 64
STEP = 10


EPSILON = 1e-05
BETA_ONE = 0.9
BETA_TWO = 0.95
ADAM_EPSILON = 1e-08
WEIGHT_DECAY = 0.1
LEARNING_RATE = 0.01
OUTPUT_RATE = 0.08
GAIN_RATE = 0.4
ROTARY_BASE = 10000.0
NEGATIVE = -1e30


def cut_along(array, dim, size):
    shape = array.shape
    blocks = array.reshape(*shape[:dim], size, shape[dim] // size, *shape[dim + 1 :])
    return jnp.moveaxis(blocks, dim, 0)


def summed_on_arrival(array, axis, dim):
    blocks = cut_along(array, dim, lax.axis_size(axis))
    arrived = lax.all_to_all(blocks, axis, split_axis=0, concat_axis=0, tiled=True)
    return arrived.astype(jnp.float32).sum(axis=0)


def normed(hidden, gain):
    return hidden * lax.rsqrt(jnp.mean(hidden * hidden, axis=-1, keepdims=True) + EPSILON) * gain


def angles(position, head_width):
    half_width = head_width // 2
    inverse = ROTARY_BASE ** (-(jnp.arange(half_width, dtype=jnp.float32) * 2.0 / head_width))
    phase = position.astype(jnp.float32)[..., None] * inverse
    return (jnp.cos(phase), jnp.sin(phase))


def rotate(values, cosine, sine):
    half_width = values.shape[-1] // 2
    former = values[..., :half_width]
    latter = values[..., half_width:]
    cosine = cosine[..., None, :]
    sine = sine[..., None, :]
    return jnp.concatenate(
        [former * cosine - latter * sine, latter * cosine + former * sine], axis=-1
    )


def document_ends(lengths, dealing):
    documents = dealing.shape[-1]
    picked = (dealing[..., :, None] == jnp.arange(documents, dtype=jnp.int32)).astype(jnp.int32)
    placed = jnp.sum(picked * lengths[..., None, :documents], axis=-1)
    return jnp.cumsum(placed, axis=-1)


def locate(position, ends):
    after = position[..., None] >= ends
    segment = jnp.sum(after.astype(jnp.int32), axis=-1)
    begin = jnp.max(jnp.where(after, ends, 0), axis=-1)
    return (segment, position - begin)


def matmul(left, right):
    return jnp.dot(left, right, preferred_element_type=jnp.float32)


def times_transposed(left, right):
    return lax.dot_general(
        left, right, (((1,), (1,)), ((), ())), preferred_element_type=jnp.float32
    )


def transposed_times(left, right):
    return lax.dot_general(
        left, right, (((0,), (0,)), ((), ())), preferred_element_type=jnp.float32
    )


def adam_step(gradient, master, moment, variance, decay, rate):
    moment_new = BETA_ONE * moment + (1.0 - BETA_ONE) * gradient
    variance_new = BETA_TWO * variance + (1.0 - BETA_TWO) * gradient * gradient
    first_fix = 1.0 - BETA_ONE**STEP
    second_fix = 1.0 - BETA_TWO**STEP
    stepped = (
        moment_new / first_fix / (jnp.sqrt(variance_new / second_fix) + ADAM_EPSILON)
        + decay * master
    )
    return (master - rate * stepped, moment_new, variance_new)


def per_device(
    tokens,
    cotangent,
    document_lengths,
    dealing,
    query_weight,
    query_master,
    query_moment,
    query_variance,
    keyvalue_weight,
    keyvalue_master,
    keyvalue_moment,
    keyvalue_variance,
    output_weight,
    output_master,
    output_moment,
    output_variance,
    gateup_weight,
    gateup_master,
    gateup_moment,
    gateup_variance,
    down_weight,
    down_master,
    down_moment,
    down_variance,
    norm_gain,
    gain_master,
    gain_moment,
    gain_variance,
):
    feature_width = tokens.shape[-1]
    row_count = tokens.shape[0]
    piece_size = tokens.shape[3]
    part_count = lax.axis_size("tensor")
    quarter_size = piece_size * part_count
    local_rows = row_count * 2 * piece_size
    query_block = 2 * quarter_size
    all_rows = part_count * local_rows
    own_context = lax.axis_index("ctx")
    own_part = lax.axis_index("tensor")
    group_size = H // KVH
    score_scale = HD ** (-0.5)
    query_full, keyvalue_full, output_full, gateup_full, down_full, gain_full = (
        lax.all_gather(query_weight, ("dp", "ctx"), axis=0, tiled=True),
        lax.all_gather(keyvalue_weight, ("dp", "ctx"), axis=1, tiled=True),
        lax.all_gather(output_weight, ("dp", "ctx"), axis=1, tiled=True),
        lax.all_gather(gateup_weight, ("dp", "ctx"), axis=1, tiled=True),
        lax.all_gather(down_weight, ("dp", "ctx"), axis=1, tiled=True),
        lax.all_gather(norm_gain, ("dp", "ctx"), axis=1, tiled=True),
    )
    gains = gain_full.astype(jnp.float32)
    key_width = keyvalue_full.shape[2]
    query_width = query_full.shape[1]
    local_heads = key_width // HD
    ends = document_ends(document_lengths, dealing)
    context_axis = jnp.arange(2, dtype=jnp.int32)[:, None, None, None]
    part_axis = jnp.arange(part_count, dtype=jnp.int32)[None, :, None, None]
    side_axis = jnp.arange(2, dtype=jnp.int32)[None, None, :, None]
    inner_axis = jnp.arange(piece_size, dtype=jnp.int32)[None, None, None, :]
    quarter_index = jnp.where(side_axis == 0, context_axis, 3 - context_axis)
    key_points = quarter_index * quarter_size + part_axis * piece_size + inner_axis
    query_points = lax.dynamic_index_in_dim(key_points, own_context, 0, keepdims=False)
    query_segment, query_position = locate(query_points[:, None], ends[None, :, None, None, :])
    key_segment = locate(key_points[:, :, None], ends[None, None, :, None, None, :])[0]
    own_points = lax.dynamic_index_in_dim(query_points, own_part, 0, keepdims=False)
    keep_mask = (
        (own_points[None] < ends[:, -1][:, None, None]).astype(jnp.float32).reshape(local_rows, 1)
    )
    cosine, sine = angles(query_position.reshape(all_rows), HD)
    query_flat = query_points.reshape(query_block)
    key_flat = key_points.reshape(2 * query_block)
    hidden_in = tokens.reshape(local_rows, feature_width).astype(jnp.float32)
    first_norm = normed(hidden_in, gains[0]).astype(jnp.bfloat16)
    spread_one = lax.all_gather(first_norm[None], "tensor", axis=0, tiled=True).reshape(
        all_rows, feature_width
    )
    query_raw = matmul(spread_one, query_full)
    key_raw = matmul(spread_one, keyvalue_full[0])
    value_low = matmul(spread_one, keyvalue_full[1]).astype(jnp.bfloat16)
    query_low = rotate(query_raw.reshape(all_rows, -1, HD), cosine, sine).astype(jnp.bfloat16)
    key_low = (
        rotate(key_raw.reshape(all_rows, local_heads, HD), cosine, sine)
        .reshape(all_rows, key_width)
        .astype(jnp.bfloat16)
    )
    pair_local = jnp.stack([key_low, value_low], 0).reshape(
        2, 1, part_count, row_count, 2 * piece_size, key_width
    )
    key_value = lax.all_gather(pair_local, "ctx", axis=1, tiled=True)
    query_rows = query_low.reshape(part_count, row_count, 2 * piece_size, query_width)

    def row_inputs(row_number):
        queries = lax.dynamic_index_in_dim(query_rows, row_number, 1, keepdims=False).reshape(
            query_block, local_heads, group_size, HD
        )
        pair_row = lax.dynamic_index_in_dim(key_value, row_number, 3, keepdims=False)
        keys_row = pair_row[0].reshape(2 * query_block, local_heads, HD)
        values_row = pair_row[1].reshape(2 * query_block, local_heads, HD)
        query_seg = lax.dynamic_index_in_dim(query_segment, row_number, 1, keepdims=False).reshape(
            query_block
        )
        key_seg = lax.dynamic_index_in_dim(key_segment, row_number, 2, keepdims=False).reshape(
            2 * query_block
        )
        allowed = (query_seg[:, None] == key_seg[None, :]) & (
            query_flat[:, None] >= key_flat[None, :]
        )
        scores = (
            jnp.einsum("qkgd,tkd->kgqt", queries, keys_row, preferred_element_type=jnp.float32)
            * score_scale
        )
        scores = jnp.where(allowed, scores, NEGATIVE)
        return (queries, keys_row, values_row, allowed, scores)

    def attend(row_number):
        queries, keys_row, values_row, allowed, scores = row_inputs(row_number)
        highest = jnp.max(scores, axis=-1, keepdims=True)
        logsum = highest + jnp.log(jnp.sum(jnp.exp(scores - highest), axis=-1, keepdims=True))
        weights_row = jnp.exp(scores - logsum).astype(jnp.bfloat16)
        mixture = jnp.einsum(
            "kgqt,tkd->qkgd", weights_row, values_row, preferred_element_type=jnp.float32
        )
        return (mixture.reshape(query_block, query_width).astype(jnp.bfloat16), logsum)

    mixtures, logsums = lax.map(attend, jnp.arange(row_count, dtype=jnp.int32))
    mixed_heads = jnp.moveaxis(
        mixtures.reshape(row_count, part_count, 2 * piece_size, query_width), 1, 0
    ).reshape(all_rows, query_width)
    attended = lax.psum_scatter(
        matmul(mixed_heads, output_full), "tensor", scatter_dimension=0, tiled=True
    )
    middle = hidden_in + attended
    second_norm = normed(middle, gains[1]).astype(jnp.bfloat16)
    spread_two = lax.all_gather(second_norm[None], "tensor", axis=0, tiled=True).reshape(
        all_rows, feature_width
    )
    gating = matmul(spread_two, gateup_full[0])
    upward = matmul(spread_two, gateup_full[1])
    active = (jax.nn.silu(gating) * upward).astype(jnp.bfloat16)
    fed = lax.psum_scatter(
        matmul(active, down_full).astype(jnp.bfloat16), "tensor", scatter_dimension=0, tiled=True
    ).astype(jnp.float32)
    block_output = (middle + fed).astype(jnp.bfloat16).reshape(tokens.shape)
    query_full, keyvalue_full, output_full, gateup_full, down_full, gain_full = (
        lax.all_gather(query_weight, ("dp", "ctx"), axis=0, tiled=True),
        lax.all_gather(keyvalue_weight, ("dp", "ctx"), axis=1, tiled=True),
        lax.all_gather(output_weight, ("dp", "ctx"), axis=1, tiled=True),
        lax.all_gather(gateup_weight, ("dp", "ctx"), axis=1, tiled=True),
        lax.all_gather(down_weight, ("dp", "ctx"), axis=1, tiled=True),
        lax.all_gather(norm_gain, ("dp", "ctx"), axis=1, tiled=True),
    )
    gains = gain_full.astype(jnp.float32)
    grad_out = cotangent.reshape(local_rows, feature_width).astype(jnp.float32) * keep_mask
    spread_grad = lax.all_gather(
        grad_out.astype(jnp.bfloat16)[None], "tensor", axis=0, tiled=True
    ).reshape(all_rows, feature_width)
    grad_active = times_transposed(spread_grad, down_full)
    down_sum = transposed_times(active, spread_grad)
    sigmoid_gate = jax.nn.sigmoid(gating)
    grad_gating = (
        grad_active * upward * sigmoid_gate * (1.0 + gating * (1.0 - sigmoid_gate))
    ).astype(jnp.bfloat16)
    grad_upward = (grad_active * gating * sigmoid_gate).astype(jnp.bfloat16)
    gateup_sum = jnp.stack(
        [transposed_times(spread_two, grad_gating), transposed_times(spread_two, grad_upward)]
    )
    grad_second = lax.psum_scatter(
        times_transposed(grad_gating, gateup_full[0])
        + times_transposed(grad_upward, gateup_full[1]),
        "tensor",
        scatter_dimension=0,
        tiled=True,
    )
    pull_second = jax.vjp(normed, middle, gains[1])[1]
    grad_mid_norm, gain_two = pull_second(grad_second)
    grad_middle = grad_out + grad_mid_norm
    spread_mid = lax.all_gather(
        grad_middle.astype(jnp.bfloat16)[None], "tensor", axis=0, tiled=True
    ).reshape(all_rows, feature_width)
    grad_heads = times_transposed(spread_mid, output_full).astype(jnp.bfloat16)
    output_sum = transposed_times(mixed_heads, spread_mid)
    grad_heads_rows = grad_heads.reshape(part_count, row_count, 2 * piece_size, query_width)

    def attend_back(row_number):
        queries, keys_row, values_row, allowed, scores = row_inputs(row_number)
        logsum = lax.dynamic_index_in_dim(logsums, row_number, 0, keepdims=False)
        probability = jnp.where(allowed, jnp.exp(scores - logsum), 0.0)
        grad_rows = lax.dynamic_index_in_dim(
            grad_heads_rows, row_number, 1, keepdims=False
        ).reshape(query_block, local_heads, group_size, HD)
        grad_probs = jnp.einsum(
            "qkgd,tkd->kgqt", grad_rows, values_row, preferred_element_type=jnp.float32
        )
        inner_sum = jnp.sum(probability * grad_probs, axis=-1, keepdims=True)
        grad_scores = (probability * (grad_probs - inner_sum) * score_scale).astype(jnp.bfloat16)
        grad_queries = jnp.einsum(
            "kgqt,tkd->qkgd", grad_scores, keys_row, preferred_element_type=jnp.float32
        )
        grad_keys = jnp.einsum(
            "kgqt,qkgd->tkd", grad_scores, queries, preferred_element_type=jnp.float32
        )
        grad_values = jnp.einsum(
            "kgqt,qkgd->tkd",
            probability.astype(jnp.bfloat16),
            grad_rows,
            preferred_element_type=jnp.float32,
        )
        pair_grad = jnp.stack([grad_keys, grad_values]).reshape(
            2, 2, part_count * 2 * piece_size, key_width
        )
        return (grad_queries.reshape(query_block, query_width), pair_grad)

    grad_query_rows, grad_pairs = lax.map(attend_back, jnp.arange(row_count, dtype=jnp.int32))
    own_pairs = lax.psum_scatter(
        grad_pairs.astype(jnp.bfloat16), "ctx", scatter_dimension=2, tiled=True
    ).astype(jnp.float32)
    own_pairs = jnp.moveaxis(
        own_pairs.reshape(row_count, 2, part_count, 2 * piece_size, key_width), 0, 2
    ).reshape(2, all_rows, local_heads, HD)
    grad_query_flat = jnp.moveaxis(
        grad_query_rows.reshape(row_count, part_count, 2 * piece_size, query_width), 1, 0
    ).reshape(all_rows, -1, HD)
    grad_query = (
        rotate(grad_query_flat, cosine, -sine).reshape(all_rows, query_width).astype(jnp.bfloat16)
    )
    grad_key = rotate(own_pairs[0], cosine, -sine).reshape(all_rows, key_width).astype(jnp.bfloat16)
    grad_value = own_pairs[1].reshape(all_rows, key_width).astype(jnp.bfloat16)
    query_sum = transposed_times(spread_one, grad_query)
    keyvalue_sum = jnp.stack(
        [transposed_times(spread_one, grad_key), transposed_times(spread_one, grad_value)]
    )
    grad_first = lax.psum_scatter(
        (
            times_transposed(grad_query, query_full)
            + times_transposed(grad_key, keyvalue_full[0])
            + times_transposed(grad_value, keyvalue_full[1])
        ).astype(jnp.bfloat16),
        "tensor",
        scatter_dimension=0,
        tiled=True,
    ).astype(jnp.float32)
    pull_first = jax.vjp(normed, hidden_in, gains[0])[1]
    grad_in_norm, gain_one = pull_first(grad_first)
    input_grad = (grad_middle + grad_in_norm).reshape(tokens.shape)
    query_grad, keyvalue_grad, output_grad, gateup_grad, down_grad = (
        summed_on_arrival(query_sum.astype(jnp.bfloat16), ("dp", "ctx"), 0),
        summed_on_arrival(keyvalue_sum.astype(jnp.bfloat16), ("dp", "ctx"), 1),
        summed_on_arrival(output_sum.astype(jnp.bfloat16), ("dp", "ctx"), 1),
        summed_on_arrival(gateup_sum.astype(jnp.bfloat16), ("dp", "ctx"), 1),
        summed_on_arrival(down_sum.astype(jnp.bfloat16), ("dp", "ctx"), 1),
    )
    gain_grad = lax.psum_scatter(
        jnp.stack([gain_one, gain_two]), ("dp", "ctx", "tensor"), scatter_dimension=1, tiled=True
    )
    query_new = adam_step(
        query_grad, query_master, query_moment, query_variance, WEIGHT_DECAY, LEARNING_RATE
    )
    keyvalue_new = adam_step(
        keyvalue_grad,
        keyvalue_master,
        keyvalue_moment,
        keyvalue_variance,
        WEIGHT_DECAY,
        LEARNING_RATE,
    )
    output_new = adam_step(
        output_grad, output_master, output_moment, output_variance, WEIGHT_DECAY, OUTPUT_RATE
    )
    gateup_new = adam_step(
        gateup_grad, gateup_master, gateup_moment, gateup_variance, WEIGHT_DECAY, LEARNING_RATE
    )
    down_new = adam_step(
        down_grad, down_master, down_moment, down_variance, WEIGHT_DECAY, LEARNING_RATE
    )
    gain_new = adam_step(gain_grad, gain_master, gain_moment, gain_variance, 0.0, GAIN_RATE)
    return (
        block_output,
        input_grad,
        query_grad,
        query_new[0],
        query_new[1],
        query_new[2],
        keyvalue_grad,
        keyvalue_new[0],
        keyvalue_new[1],
        keyvalue_new[2],
        output_grad,
        output_new[0],
        output_new[1],
        output_new[2],
        gateup_grad,
        gateup_new[0],
        gateup_new[1],
        gateup_new[2],
        down_grad,
        down_new[0],
        down_new[1],
        down_new[2],
        gain_grad,
        gain_new[0],
        gain_new[1],
        gain_new[2],
    )


def solution(mesh):
    return jax.shard_map(
        per_device,
        mesh=mesh,
        in_specs=(
            P("dp", "ctx", None, "tensor", None),
            P("dp", "ctx", None, "tensor", None),
            P("dp", None),
            P("dp", None),
            P(("dp", "ctx"), "tensor"),
            P(("dp", "ctx"), "tensor"),
            P(("dp", "ctx"), "tensor"),
            P(("dp", "ctx"), "tensor"),
            P(None, ("dp", "ctx"), "tensor"),
            P(None, ("dp", "ctx"), "tensor"),
            P(None, ("dp", "ctx"), "tensor"),
            P(None, ("dp", "ctx"), "tensor"),
            P("tensor", ("dp", "ctx")),
            P("tensor", ("dp", "ctx")),
            P("tensor", ("dp", "ctx")),
            P("tensor", ("dp", "ctx")),
            P(None, ("dp", "ctx"), "tensor"),
            P(None, ("dp", "ctx"), "tensor"),
            P(None, ("dp", "ctx"), "tensor"),
            P(None, ("dp", "ctx"), "tensor"),
            P("tensor", ("dp", "ctx")),
            P("tensor", ("dp", "ctx")),
            P("tensor", ("dp", "ctx")),
            P("tensor", ("dp", "ctx")),
            P(None, ("dp", "ctx")),
            P(None, ("dp", "ctx", "tensor")),
            P(None, ("dp", "ctx", "tensor")),
            P(None, ("dp", "ctx", "tensor")),
        ),
        out_specs=(
            P("dp", "ctx", None, "tensor", None),
            P("dp", "ctx", None, "tensor", None),
            P(("dp", "ctx"), "tensor"),
            P(("dp", "ctx"), "tensor"),
            P(("dp", "ctx"), "tensor"),
            P(("dp", "ctx"), "tensor"),
            P(None, ("dp", "ctx"), "tensor"),
            P(None, ("dp", "ctx"), "tensor"),
            P(None, ("dp", "ctx"), "tensor"),
            P(None, ("dp", "ctx"), "tensor"),
            P("tensor", ("dp", "ctx")),
            P("tensor", ("dp", "ctx")),
            P("tensor", ("dp", "ctx")),
            P("tensor", ("dp", "ctx")),
            P(None, ("dp", "ctx"), "tensor"),
            P(None, ("dp", "ctx"), "tensor"),
            P(None, ("dp", "ctx"), "tensor"),
            P(None, ("dp", "ctx"), "tensor"),
            P("tensor", ("dp", "ctx")),
            P("tensor", ("dp", "ctx")),
            P("tensor", ("dp", "ctx")),
            P("tensor", ("dp", "ctx")),
            P(None, ("dp", "ctx", "tensor")),
            P(None, ("dp", "ctx", "tensor")),
            P(None, ("dp", "ctx", "tensor")),
            P(None, ("dp", "ctx", "tensor")),
        ),
        check_vma=False,
    )
```

profile of v0, /device:TPU:0, one launch (start us, length us, event | category | flops | bytes accessed | tf_op | source)
XLA Modules:
  0.0 575.3 jit_solution(8230138873698333674)
XLA Ops:
  9.9 13.5 %all-gather.2 = bf16[8,96,2]{1,2,0:T(2,128)(2,1)S(1)} all-gather(bf16[1,96,2]{1,2,0:T(2,128)(2,1)} %bitcast.402), channel_id=1, replica_groups=mesh['dp'=4,'ctx'=2,'tensor'=4] {'dp','ctx'}, dimensions={0}, use_global_device_ids=true | all-gather | bytes 3456 | tf_op jit(solution)/shard_map/all_gather | solution.py:148
  28.5 14.7 %all_gather.43 = bf16[768,192]{1,0:T(8,128)(2,1)S(1)} all-gather(bf16[96,192]{1,0:T(8,128)(2,1)} %param.36), channel_id=1, replica_groups=mesh['dp'=4,'ctx'=2,'tensor'=4] {'dp','ctx'}, dimensions={0}, use_global_device_ids=true | all-gather | bytes 331776 | tf_op jit(solution)/shard_map/all_gather | solution.py:143
  43.4 16.2 %all_gather.41 = bf16[2,768,192]{2,1,0:T(8,128)(2,1)S(1)} all-gather(bf16[2,96,192]{2,1,0:T(8,128)(2,1)S(1)} %copy-done.60), channel_id=1, replica_groups=mesh['dp'=4,'ctx'=2,'tensor'=4] {'dp','ctx'}, dimensions={1}, use_global_device_ids=true | all-gather | bytes 663552 | tf_op jit(solution)/shard_map/all_gather | solution.py:144
  61.1 2.9 convolution_convert_fusion.7
  69.6 14.7 %all_gather.44 = bf16[192,768]{0,1:T(8,128)(2,1)S(1)} all-gather(bf16[192,96]{0,1:T(8,128)(2,1)S(1)} %copy.304), channel_id=1, replica_groups=mesh['dp'=4,'ctx'=2,'tensor'=4] {'dp','ctx'}, dimensions={1}, use_global_device_ids=true | all-gather | bytes 331776 | tf_op jit(solution)/shard_map/all_gather | solution.py:145
  84.7 21.0 %while.28 = (s32[]{:T(128)}, bf16[2,512,192]{1,2,0:T(8,128)(2,1)S(1)}, f32[2,3,1,512,1]{3,1,4,2,0:T(4,128)S(1)}, s32[2]{0:T(128)S(1)}, bf16[2,2,4,2,128,192]{4,2...) while((s32[]{:T(128)}, ...), condition=%wide.wide.region_9.10_spmd.clone, body=%wide.wide.region_6.9_spmd.clone.sunk | while | flops 421625344 | bytes 26583340 | solution.py:224
  106.7 2.3 fusion.75
  109.7 41.8 %reduce-scatter.7.cloned.1.call-done = f32[256,768]{1,0:T(8,128)} async-done(((f32[1024,768]{1,0:T(8,128)}), f32[256,768]{1,0:T(8,128)}) %reduce-scatter.7.cloned.1.call-update) | async-done | bytes 786448 | tf_op jit(solution)/shard_map/reduce_scatter | solution.py:228
  154.9 15.7 %all_gather.47 = bf16[512,768]{0,1:T(8,128)(2,1)S(1)} all-gather(bf16[512,96]{0,1:T(8,128)(2,1)S(1)} %copy-done.61), channel_id=1, replica_groups=mesh['dp'=4,'ctx'=2,'tensor'=4] {'dp','ctx'}, dimensions={1}, use_global_device_ids=true | all-gather | bytes 884736 | tf_op jit(solution)/shard_map/all_gather | solution.py:147
  170.7 13.9 %all-gather.18.cloned.1.call-done = bf16[1024,768]{1,0:T(8,128)(2,1)} async-done(((bf16[256,768]{1,0:T(8,128)(2,1)}), bf16[1024,768]{1,0:T(8,128)(2,1)}) %all-gather.18.cloned.1.call-update) | async-done | bytes 1572880 | tf_op jit(solution)/shard_map/all_gather | solution.py:233
  184.6 4.1 fusion.47
  188.7 2.3 fusion.46
  191.0 26.7 %all-gather.16.cloned.1.call-done = bf16[4,256,768]{2,1,0:T(8,128)(2,1)} async-done(((bf16[1,256,768]{2,1,0:T(8,128)(2,1)}), bf16[4,256,768]{2,1,0:T(8,128)(2,1)}) %all-gather.16.cloned.1.call-update) | async-done | bytes 1572880 | tf_op jit(solution)/shard_map/all_gather | solution.py:253
  217.7 5.6 multiply_convert_fusion
  224.6 2.7 convolution_add_fusion
  227.4 3.4 convolution_convert_fusion
  230.8 40.4 %reduce-scatter.11.cloned.1.call-done = f32[256,768]{1,0:T(8,128)} async-done(((f32[1024,768]{1,0:T(8,128)}), f32[256,768]{1,0:T(8,128)}) %reduce-scatter.11.cloned.1.call-update) | async-done | bytes 786448 | tf_op jit(solution)/shard_map/reduce_scatter | solution.py:266
  272.7 32.5 %reduce-scatter.9.cloned.1.call-done = bf16[256,768]{1,0:T(8,128)(2,1)} async-done(((bf16[1024,768]{1,0:T(8,128)(2,1)}), bf16[256,768]{1,0:T(8,128)(2,1)}) %reduce-scatter.9.cloned.1.call-update) | async-done | bytes 393232 | tf_op jit(solution)/shard_map/reduce_scatter | solution.py:239
  305.1 2.5 fusion.68
  308.2 30.5 %all-gather.20.cloned.1.call-done = bf16[1024,768]{1,0:T(8,128)(2,1)} async-done(((bf16[256,768]{1,0:T(8,128)(2,1)}), bf16[1024,768]{1,0:T(8,128)(2,1)}) %all-gather.20.cloned.1.call-update) | async-done | bytes 1572880 | tf_op jit(solution)/shard_map/all_gather | solution.py:276
  338.7 2.1 convolution_convert_fusion.6
  341.2 55.4 %while.29 = (s32[]{:T(128)}, f32[2,512,192]{1,2,0:T(8,128)}, bf16[2,2,2,512,192]{3,4,1,0,2:T(8,128)(2,1)}, s32[2]{0:T(128)S(1)}, bf16[2,2,4,2,128,192]{4,2,1,5,3...) while((s32[]{:T(128)}, f32[2,512,192]{1,2,0:T(8,128)}, ...), condition=%wide.wide.region_17.18_spmd.clone, body=%wide.wide.region_15.17_spmd.clone.sunk | while | flops 1038482944 | bytes 127232600 | solution.py:312
  349.1 2.6 copy-done
  351.8 2.8 fusion.184
  354.6 2.2 stack.43
  356.8 4.7 fusion.181
  361.5 2.2 fusion.182
  376.8 2.6 copy-done
  379.4 2.8 fusion.184
  382.3 2.2 stack.43
  384.5 4.7 fusion.181
  389.2 2.2 fusion.182
  396.7 2.8 convolution_convert_fusion.1
  400.7 4.9 all-to-all-start.4
  407.2 2.5 fusion.33
  412.2 14.3 %all-to-all-done.4 = bf16[8,512,96]{1,2,0:T(8,128)(2,1)S(1)} async-done(((bf16[8,512,96]{1,2,0:T(8,128)(2,1)}), bf16[8,512,96]{1,2,0:T(8,128)(2,1)S(1)}, u32[]{:S(2)}, u32[]{:S(2)}) %all-to-all-start.4) | async-done | bytes 786464 | tf_op jit(solution)/shard_map/all_to_all | solution.py:32
  426.5 4.3 all-to-all-start.3
  439.3 2.3 fusion.76
  454.5 2.2 convolution_convert_fusion.9
  459.0 9.7 %all-to-all-done.3 = bf16[8,2,96,512]{3,2,1,0:T(8,128)(2,1)} async-done(((bf16[8,2,96,512]{3,2,1,0:T(8,128)(2,1)}), bf16[8,2,96,512]{3,2,1,0:T(8,128)(2,1)}, u32[]{:S(2)}, u32[]{:S(2)}) %all-to-all-start.3) | async-done | bytes 1572896 | tf_op jit(solution)/shard_map/all_to_all | solution.py:32
  468.7 3.7 all-to-all-start.2
  477.7 7.1 %all-to-all-done.2 = bf16[8,192,96]{2,1,0:T(8,128)(2,1)S(1)} async-done(((bf16[8,192,96]{2,1,0:T(8,128)(2,1)}), bf16[8,192,96]{2,1,0:T(8,128)(2,1)S(1)}, u32[]{:S(2)}, u32[]{:S(2)}) %all-to-all-start.2) | async-done | bytes 294944 | tf_op jit(solution)/shard_map/all_to_all | solution.py:32
  484.8 3.5 all-to-all-start
  491.6 9.1 %all-to-all-done = bf16[8,96,192]{1,2,0:T(8,128)(2,1)S(1)} async-done(((bf16[8,96,192]{1,2,0:T(8,128)(2,1)}), bf16[8,96,192]{1,2,0:T(8,128)(2,1)S(1)}, u32[]{:S(2)}, u32[]{:S(2)}) %all-to-all-start) | async-done | bytes 294944 | tf_op jit(solution)/shard_map/all_to_all | solution.py:32
  500.7 3.5 all-to-all-start.1
  509.7 15.5 %all-to-all-done.1 = bf16[8,2,96,192]{3,2,1,0:T(8,128)(2,1)S(1)} async-done(((bf16[8,2,96,192]{3,2,1,0:T(8,128)(2,1)}), bf16[8,2,96,192]{3,2,1,0:T(8,128)(2,1)S(1)}, u32[]{:S(2)}, u32[]{:S(2)}) %all-to-all-start.1) | async-done | bytes 589856 | tf_op jit(solution)/shard_map/all_to_all | solution.py:32
  527.7 37.0 %all-reduce = f32[2,768]{1,0:T(2,128)S(1)} all-reduce(f32[2,768]{1,0:T(2,128)S(1)} %pad_maximum_fusion.5), channel_id=9, replica_groups=mesh['dp'=4,'ctx'=2,'tensor'=4] {'dp','ctx','tensor'}, use_global_device_ids=true, to_apply=%region_28.29.clone | all-reduce | flops 1536 | bytes 12288
  565.4 2.1 fusion.43
  (415 shorter events, 107.9 us)
Async XLA Ops:
  8.0 35.3 %copy-start.60 = (bf16[2,96,192]{2,1,0:T(8,128)(2,1)S(1)}, bf16[2,96,192]{2,1,0:T(8,128)(2,1)}, u32[]{:S(2)}) copy-start(bf16[2,96,192]{2,1,0:T(8,128)(2,1)} %param.40) | copy-start | bytes 221188
  8.0 53.0 %all-gather.10.cloned.1.call-start = ((), (), s32[]{:S(2)}) async-start(), calls=%async_computation.10 | async-start | bytes 1966080 | tf_op jit(solution)/shard_map/all_gather | solution.py:173
  9.9 49.7 %copy-start.73 = (f32[256]{0:T(256)}, f32[256]{0:T(256)S(1)}, u32[]{:S(2)}) copy-start(f32[256]{0:T(256)S(1)} %rsqrt.22) | copy-start | bytes 3076
  26.1 58.6 %all-gather.12.cloned.1.call-start = ((), (), s32[]{:S(2)}) async-start(), calls=%async_computation.11 | async-start | bytes 2359296 | tf_op jit(solution)/shard_map/all_gather | solution.py:188
  28.2 41.0 %copy-start.70 = (s32[4,2,64]{2,1,0:T(2,128)}, s32[4,2,64]{2,1,0:T(2,128)S(1)}, u32[]{:S(2)}) copy-start(s32[4,2,64]{2,1,0:T(2,128)S(1)} %dynamic-slice_bitcast_fusion.1) | copy-start | bytes 6148
  43.2 17.9 %copy-start.14 = (bf16[768,192]{1,0:T(8,128)(2,1)}, bf16[768,192]{1,0:T(8,128)(2,1)S(1)}, u32[]{:S(2)}) copy-start(bf16[768,192]{1,0:T(8,128)(2,1)S(1)} %all_gather.43) | copy-start | bytes 884740
  69.2 82.3 %reduce-scatter.7.cloned.1.call-start = ((), (), s32[]{:S(2)}) async-start(), calls=%async_computation.12 | async-start | bytes 3932160 | tf_op jit(solution)/shard_map/reduce_scatter | solution.py:228
  109.0 42.5 %copy-start.7 = (bf16[2,1,2,64,768]{4,3,2,1,0:T(8,128)(2,1)S(1)}, bf16[2,1,2,64,768]{4,3,2,1,0:T(8,128)(2,1)}, u32[]{:S(2)}) copy-start(bf16[2,1,2,64,768]{4,3,2,1,0:T(8,128)(2,1)} %param.32) | copy-start | bytes 1179652
  109.0 45.0 %copy-start.31 = (bf16[2,1,2,64,768]{4,3,2,1,0:T(8,128)(2,1)S(1)}, bf16[2,1,2,64,768]{4,3,2,1,0:T(8,128)(2,1)}, u32[]{:S(2)}) copy-start(bf16[2,1,2,64,768]{4,3,2,1,0:T(8,128)(2,1)} %param.33) | copy-start | bytes 1179652
  109.0 61.7 %all-gather.14.cloned.1.call-start = ((), (), s32[]{:S(2)}) async-start(), calls=%async_computation.13 | async-start | bytes 1769472 | tf_op jit(solution)/shard_map/all_gather | solution.py:146
  109.6 45.3 %copy-start.61 = (bf16[512,96]{0,1:T(8,128)(2,1)S(1)}, bf16[512,96]{0,1:T(8,128)(2,1)}, u32[]{:S(2)}) copy-start(bf16[512,96]{0,1:T(8,128)(2,1)} %param.52) | copy-start | bytes 294916
  109.6 75.0 %all-gather.18.cloned.1.call-start = ((), (), s32[]{:S(2)}) async-start(), calls=%async_computation.19 | async-start | bytes 1966080 | tf_op jit(solution)/shard_map/all_gather | solution.py:233
  153.7 64.0 %all-gather.16.cloned.1.call-start = ((), (), s32[]{:S(2)}) async-start(), calls=%async_computation.15 | async-start | bytes 1966080 | tf_op jit(solution)/shard_map/all_gather | solution.py:253
  154.9 116.4 %reduce-scatter.11.cloned.1.call-start = ((), (), s32[]{:S(2)}) async-start(), calls=%async_computation.16 | async-start | bytes 3932160 | tf_op jit(solution)/shard_map/reduce_scatter | solution.py:266
  227.3 77.8 %reduce-scatter.9.cloned.1.call-start = ((), (), s32[]{:S(2)}) async-start(), calls=%async_computation.14 | async-start | bytes 1966080 | tf_op jit(solution)/shard_map/reduce_scatter | solution.py:239
  230.8 74.4 %copy-start.32 = (bf16[2,1,2,64,768]{4,3,2,1,0:T(8,128)(2,1)S(1)}, bf16[2,1,2,64,768]{4,3,2,1,0:T(8,128)(2,1)}, u32[]{:S(2)}) copy-start(bf16[2,1,2,64,768]{4,3,2,1,0:T(8,128)(2,1)} %param.33) | copy-start | bytes 1179652
  230.8 108.0 %all-gather.20.cloned.1.call-start = ((), (), s32[]{:S(2)}) async-start(), calls=%async_computation.20 | async-start | bytes 1966080 | tf_op jit(solution)/shard_map/all_gather | solution.py:276
  271.2 33.9 %copy-start.20 = (f32[256,768]{1,0:T(8,128)S(1)}, f32[256,768]{1,0:T(8,128)}, u32[]{:S(2)}) copy-start(f32[256,768]{1,0:T(8,128)} %reduce-scatter.11.cloned.1.call-done) | copy-start | bytes 2359300
  272.7 35.5 %copy-start.71 = (s32[4,2,64]{2,1,0:T(2,128)S(1)}, s32[4,2,64]{2,1,0:T(2,128)}, u32[]{:S(2)}) copy-start(s32[4,2,64]{2,1,0:T(2,128)} %get-tuple-element.1058) | copy-start | bytes 6148
  307.6 134.0 %reduce-scatter.13.cloned.1.call-start = ((), (), s32[]{:S(2)}) async-start(), calls=%async_computation.17 | async-start | bytes 2359296 | tf_op jit(solution)/shard_map/reduce_scatter | solution.py:313
  400.7 25.9 %all-to-all-start.4 = ((bf16[8,512,96]{1,2,0:T(8,128)(2,1)}), bf16[8,512,96]{1,2,0:T(8,128)(2,1)S(1)}, u32[]{:S(2)}, u32[]{:S(2)}) async-start(bf16[8,512,96]{1,2,0:T(8,128)(2,1)} %bitcast.46), calls=%async_computation.9 | async-start | bytes 1572864 | tf_op jit(solution)/shard_map/all_to_all | solution.py:32
  412.2 18.7 %copy-start.62 = (f32[96,192]{1,0:T(8,128)S(1)}, f32[96,192]{1,0:T(8,128)}, u32[]{:S(2)}) copy-start(f32[96,192]{1,0:T(8,128)} %param.37) | copy-start | bytes 221188
  412.2 19.4 %copy-start.63 = (f32[96,192]{1,0:T(8,128)S(1)}, f32[96,192]{1,0:T(8,128)}, u32[]{:S(2)}) copy-start(f32[96,192]{1,0:T(8,128)} %param.38) | copy-start | bytes 221188
  412.2 20.2 %copy-start.64 = (f32[96,192]{1,0:T(8,128)S(1)}, f32[96,192]{1,0:T(8,128)}, u32[]{:S(2)}) copy-start(f32[96,192]{1,0:T(8,128)} %param.39) | copy-start | bytes 221188
  412.2 20.9 %copy-start.2 = (bf16[4,256,768]{2,1,0:T(8,128)(2,1)S(1)}, bf16[4,256,768]{2,1,0:T(8,128)(2,1)}, u32[]{:S(2)}) copy-start(bf16[4,256,768]{2,1,0:T(8,128)(2,1)} %all-gather.10.cloned.1.call-done) | copy-start | bytes 4718596
  426.5 42.1 %all-to-all-start.3 = ((bf16[8,2,96,512]{3,2,1,0:T(8,128)(2,1)}), bf16[8,2,96,512]{3,2,1,0:T(8,128)(2,1)}, u32[]{:S(2)}, u32[]{:S(2)}) async-start(bf16[8,2,96,512]{3,2,1,0:T(8,128)(2,1)} %copy.324), calls=%async_computation.8 | async-start | bytes 3145728 | tf_op jit(solution)/shard_map/all_to_all | solution.py:32
  430.8 95.4 %reduce-scatter.15.cloned.1.call-start = ((), (), s32[]{:S(2)}) async-start(), calls=%async_computation.18 | async-start | bytes 1966080 | tf_op jit(solution)/shard_map/reduce_scatter | solution.py:331
  456.6 15.7 %copy-start.54 = (f32[512,96]{0,1:T(8,128)S(1)}, f32[512,96]{0,1:T(8,128)}, u32[]{:S(2)}) copy-start(f32[512,96]{0,1:T(8,128)} %param.53) | copy-start | bytes 589828
  456.6 15.7 %copy-start.55 = (f32[512,96]{0,1:T(8,128)S(1)}, f32[512,96]{0,1:T(8,128)}, u32[]{:S(2)}) copy-start(f32[512,96]{0,1:T(8,128)} %param.54) | copy-start | bytes 589828
  456.7 15.7 %copy-start.56 = (f32[512,96]{0,1:T(8,128)S(1)}, f32[512,96]{0,1:T(8,128)}, u32[]{:S(2)}) copy-start(f32[512,96]{0,1:T(8,128)} %param.55) | copy-start | bytes 589828
  459.0 16.0 %copy-start.18 = (bf16[1024,3,64]{0,2,1:T(8,128)(2,1)S(1)}, bf16[1024,3,64]{0,2,1:T(8,128)(2,1)}, u32[]{:S(2)}) copy-start(bf16[1024,3,64]{0,2,1:T(8,128)(2,1)} %copy-done.17) | copy-start | bytes 1179652
  468.7 16.1 %all-to-all-start.2 = ((bf16[8,192,96]{2,1,0:T(8,128)(2,1)}), bf16[8,192,96]{2,1,0:T(8,128)(2,1)S(1)}, u32[]{:S(2)}, u32[]{:S(2)}) async-start(bf16[8,192,96]{2,1,0:T(8,128)(2,1)} %bitcast.276), calls=%async_computation.7 | async-start | bytes 786432 | tf_op jit(solution)/shard_map/all_to_all | solution.py:32
  474.9 29.3 %copy-start.35 = (f32[2,96,512]{2,1,0:T(8,128)}, f32[2,96,512]{2,1,0:T(8,128)S(1)}, u32[]{:S(2)}) copy-start(f32[2,96,512]{2,1,0:T(8,128)S(1)} %convert_reduce_fusion) | copy-start | bytes 1179652
  484.8 15.9 %all-to-all-start = ((bf16[8,96,192]{1,2,0:T(8,128)(2,1)}), bf16[8,96,192]{1,2,0:T(8,128)(2,1)S(1)}, u32[]{:S(2)}, u32[]{:S(2)}) async-start(bf16[8,96,192]{1,2,0:T(8,128)(2,1)} %copy.314), calls=%async_computation.5 | async-start | bytes 786432 | tf_op jit(solution)/shard_map/all_to_all | solution.py:32
  500.7 24.5 %all-to-all-start.1 = ((bf16[8,2,96,192]{3,2,1,0:T(8,128)(2,1)}), bf16[8,2,96,192]{3,2,1,0:T(8,128)(2,1)S(1)}, u32[]{:S(2)}, u32[]{:S(2)}) async-start(bf16[8,2,96,192]{3,2,1,0:T(8,128)(2,1)} %copy.321), calls=%async_computation.6 | async-start | bytes 1572864 | tf_op jit(solution)/shard_map/all_to_all | solution.py:32
  505.6 19.7 %copy-start.57 = (f32[2,96,192]{2,1,0:T(8,128)S(1)}, f32[2,96,192]{2,1,0:T(8,128)}, u32[]{:S(2)}) copy-start(f32[2,96,192]{2,1,0:T(8,128)} %param.41) | copy-start | bytes 442372
  505.6 19.7 %copy-start.58 = (f32[2,96,192]{2,1,0:T(8,128)S(1)}, f32[2,96,192]{2,1,0:T(8,128)}, u32[]{:S(2)}) copy-start(f32[2,96,192]{2,1,0:T(8,128)} %param.42) | copy-start | bytes 442372
  505.6 19.7 %copy-start.59 = (f32[2,96,192]{2,1,0:T(8,128)S(1)}, f32[2,96,192]{2,1,0:T(8,128)}, u32[]{:S(2)}) copy-start(f32[2,96,192]{2,1,0:T(8,128)} %param.43) | copy-start | bytes 442372
  506.5 19.7 %copy-start.8 = (bf16[2,1,2,64,768]{4,3,2,1,0:T(8,128)(2,1)S(1)}, bf16[2,1,2,64,768]{4,3,2,1,0:T(8,128)(2,1)}, u32[]{:S(2)}) copy-start(bf16[2,1,2,64,768]{4,3,2,1,0:T(8,128)(2,1)} %param.32) | copy-start | bytes 1179652
  506.5 19.7 %copy-start.69 = (f32[768]{0:T(1024)S(1)}, f32[768]{0:T(1024)}, u32[]{:S(2)}) copy-start(f32[768]{0:T(1024)} %copy-done.68) | copy-start | bytes 9220
  506.6 19.7 %copy-start.74 = (f32[256]{0:T(256)S(1)}, f32[256]{0:T(256)}, u32[]{:S(2)}) copy-start(f32[256]{0:T(256)} %copy-done.73) | copy-start | bytes 3076
  508.8 55.9 %copy-start.76 = (f32[256]{0:T(256)S(1)}, f32[256]{0:T(256)}, u32[]{:S(2)}) copy-start(f32[256]{0:T(256)} %copy-done.75) | copy-start | bytes 3076
  508.8 55.9 %copy-start.77 = (f32[2,24]{1,0:T(2,128)S(1)}, f32[2,24]{1,0:T(2,128)}, u32[]{:S(2)}) copy-start(f32[2,24]{1,0:T(2,128)} %param.57) | copy-start | bytes 580
  508.8 55.9 %copy-start.78 = (f32[2,24]{1,0:T(2,128)S(1)}, f32[2,24]{1,0:T(2,128)}, u32[]{:S(2)}) copy-start(f32[2,24]{1,0:T(2,128)} %param.58) | copy-start | bytes 580
  508.8 55.9 %copy-start.79 = (f32[2,24]{1,0:T(2,128)S(1)}, f32[2,24]{1,0:T(2,128)}, u32[]{:S(2)}) copy-start(f32[2,24]{1,0:T(2,128)} %param.59) | copy-start | bytes 580
  508.8 56.6 %copy-start.21 = (f32[256,768]{1,0:T(8,128)S(1)}, f32[256,768]{1,0:T(8,128)}, u32[]{:S(2)}) copy-start(f32[256,768]{1,0:T(8,128)} %get-tuple-element.606) | copy-start | bytes 2359300
  508.9 58.6 %copy-start.53 = (f32[192,96]{1,0:T(8,128)}, f32[192,96]{1,0:T(8,128)S(1)}, u32[]{:S(2)}) copy-start(f32[192,96]{1,0:T(8,128)S(1)} %convert_reduce_fusion.3) | copy-start | bytes 221188
  525.3 42.1 %copy-start.45 = (f32[2,96,192]{2,1,0:T(8,128)}, f32[2,96,192]{2,1,0:T(8,128)S(1)}, u32[]{:S(2)}) copy-start(f32[2,96,192]{2,1,0:T(8,128)S(1)} %convert_reduce_fusion.2) | copy-start | bytes 442372
  (60 other events, 251.8 us)
Sparse Core Ops, SparseCore 0:
  26.2 29.1 all-gather.9
  69.3 8.0 all-gather.11
  109.1 42.3 reduce-scatter.6
  307.7 30.9 all-gather.19
  396.8 9.0 reduce-scatter.12
  452.5 31.2 reduce-scatter.14
Sparse Core Ops, SparseCore 1:
  111.1 23.5 all-gather.13
  153.8 30.7 all-gather.17
  186.9 30.8 all-gather.15
  227.4 43.8 reduce-scatter.10
  274.2 30.8 reduce-scatter.8
where the time goes:
time: 583 us; the launch traced here: 575 us
  waiting for transfers between devices  242 us (42%)
  blocking collectives  112 us (19%)
  matrix products  70.4 us (12%)
  local copies, waits for them, and re-layouts  61.8 us (11%)
  other arithmetic  42.7 us (7%)
  starting transfers between devices  20.8 us (4%)
  between operations  17.2 us (3%)
  loops' own time  8.36 us (1%)
    all_to_all x5, waiting for transfers between devices, summed_on_arrival(): lax.all_to_all(blocks, axis, split_axis=0, concat_axis=0, tiled=True)  55.7 us
    reduce_scatter x1, waiting for transfers between devices, per_device(): lax.psum_scatter(matmul(mixed_heads, output_full), 'tensor', scatter_dime...  41.8 us
    reduce_scatter x1, waiting for transfers between devices, per_device(): lax.psum_scatter(times_transposed(grad_gating, gateup_full[0]) + times_tr...  40.4 us
    unnamed x1, blocking collectives  37 us
    reduce_scatter x1, waiting for transfers between devices, per_device(): lax.psum_scatter(matmul(active, down_full).astype(jnp.bfloat16), 'tensor'...  32.5 us
    all_gather x1, waiting for transfers between devices, per_device(): lax.all_gather(grad_middle.astype(jnp.bfloat16)[None], 'tensor', axis=0,...  30.5 us
    all_gather x1, waiting for transfers between devices, per_device(): lax.all_gather(grad_out.astype(jnp.bfloat16)[None], 'tensor', axis=0, til...  26.7 us
    all_to_all x5, starting transfers between devices, summed_on_arrival(): lax.all_to_all(blocks, axis, split_axis=0, concat_axis=0, tiled=True)  19.9 us
  transfers between devices with their start and end apart: 16, of which 11 were waited for; matrix products, arithmetic and copies ran while one was open for 12% of the time, Pallas kernels for 0%

commit v1 on v0

v1 whole, which is shorter than its diff:
```python
import functools

import jax
import jax.numpy as jnp
from jax import lax
from jax.experimental import pallas as pl
from jax.experimental.pallas import tpu as pltpu
from jax.sharding import PartitionSpec as P

H = 12
HD = 64
STEP = 10
PARTS = 4
HEADS = H // PARTS
TILE = 2 * HD
QKV = 5 * TILE

EPSILON = 1e-05
BETA_ONE = 0.9
BETA_TWO = 0.95
ADAM_EPSILON = 1e-08
WEIGHT_DECAY = 0.1
LEARNING_RATE = 0.01
OUTPUT_RATE = 0.08
GAIN_RATE = 0.4
ROTARY_BASE = 10000.0
NEGATIVE = -1e30

F32 = jnp.float32
BF16 = jnp.bfloat16
SMEM = pl.BlockSpec(memory_space=pltpu.SMEM)
VMEM = pl.BlockSpec(memory_space=pltpu.VMEM)


def call(name, body, outs, scalars, arrays, scratch=(), grown=None):
    extra = () if grown is None else (grown,)
    out_shape = [jax.ShapeDtypeStruct(shape, dtype) for shape, dtype in outs]
    out_shape += [jax.ShapeDtypeStruct(value.shape, value.dtype) for value in extra]
    anywhere = [pl.BlockSpec(memory_space=pl.ANY) for _ in extra]
    scratch_shapes = [pltpu.VMEM(shape, dtype) for shape, dtype in scratch]
    if extra:
        scratch_shapes.append(pltpu.SemaphoreType.DMA(()))
    position = len(scalars) + len(arrays)
    return pl.pallas_call(
        body,
        out_shape=out_shape,
        in_specs=[SMEM] * len(scalars) + [VMEM] * len(arrays) + anywhere,
        out_specs=[VMEM] * len(outs) + anywhere,
        scratch_shapes=scratch_shapes,
        input_output_aliases={position: len(outs)} if extra else {},
        compiler_params=pltpu.CompilerParams(vmem_limit_bytes=60 << 20),
        name=name,
    )(*scalars, *arrays, *extra)


def dot(left, right):
    return lax.dot_general(left, right, (((1,), (0,)), ((), ())), preferred_element_type=F32)


def dot_nt(left, right):
    return lax.dot_general(left, right, (((1,), (1,)), ((), ())), preferred_element_type=F32)


def dot_tn(left, right):
    return lax.dot_general(left, right, (((0,), (0,)), ((), ())), preferred_element_type=F32)


def rows_at(start, size, unit):
    return pl.ds(pl.multiple_of(start, unit), size)


def lanes_of(shape):
    return lax.broadcasted_iota(jnp.int32, shape, len(shape) - 1)


def swapped(tile):
    first = (lanes_of(tile.shape) % HD) < HD // 2
    return jnp.where(first, pltpu.roll(tile, TILE - HD // 2, 1), pltpu.roll(tile, HD // 2, 1))


def root_mean(values):
    return lax.rsqrt(jnp.mean(values * values, axis=-1, keepdims=True) + EPSILON)


def stack_body(meta, *refs):
    pieces, out = refs[:-1], refs[-1]
    count = len(pieces)
    for shift, piece in enumerate(pieces):
        out[lax.rem(meta[2] + count - shift, count)] = piece[...]


def assemble(meta, own, other, target, low, high):
    context = meta[1]
    count, rows, _ = own.shape
    for index in range(count):
        target[rows_at((2 * index + context) * rows, rows, 16), :] = own[index, :, low:high]
        target[rows_at((2 * index + 1 - context) * rows, rows, 16), :] = other[index, :, low:high]


def assemble_first_body(meta, own, other, weight, gains):
    assemble(meta, own, other, weight, 0, QKV)
    tile = weight[:, TILE : 2 * TILE].astype(F32)
    gains[...] = tile.T[HD : HD + 8, :]
    weight[:, TILE : 2 * TILE] = jnp.where(lanes_of(tile.shape) < HD, tile, 0.0).astype(BF16)


def project_body(
    meta, x0, x1, x2, x3, x4, gains, weight, cosine, sine, hidden, normed, query, keyval
):
    part = meta[0]
    blocks = x0.shape[0] // 64
    gain = gains[0:1, :]
    pieces = ((x0, 0, 0), (x1, 1, 0), (x2, 2, 0), (x3, 3, 0), (x4, 3, blocks // 2))
    for piece, offset, start in pieces:
        place = jnp.bitwise_xor(part, offset)

        def spread(block, carry, piece=piece, place=place, start=start):
            source = piece[rows_at(block * 64, 64, 64), :]
            values = source.astype(F32)
            target = rows_at((start + block) * 256 + place * 64, 64, 64)
            hidden[target, :] = source
            normed[target, :] = (values * root_mean(values) * gain).astype(BF16)
            return carry

        lax.fori_loop(0, piece.shape[0] // 64, spread, 0)

    def rotate(block, carry):
        rows = rows_at(block * 256, 256, 256)
        raw = dot(normed[rows, :], weight[...])
        cos, sin = cosine[rows, :], sine[rows, :]
        lower = lanes_of(cos.shape) < HD
        for index in range(5):
            tile = raw[:, index * TILE : (index + 1) * TILE]
            turned = tile * cos + swapped(tile) * sin
            lanes = slice((index - 2) * TILE, (index - 1) * TILE)
            if index < 2:
                query[rows, index * TILE : (index + 1) * TILE] = (turned * HD**-0.5).astype(BF16)
            else:
                keyval[rows, lanes] = jnp.where(lower, turned, tile).astype(BF16)
        return carry

    lax.fori_loop(0, blocks, rotate, 0)


def gather_keys(context, row, own, other, absolute):
    for side in range(2):
        rows = rows_at(row * 512 + side * 256, 256, 256)
        mine = context if side == 0 else 3 - context
        theirs = 1 - context if side == 0 else 2 + context
        absolute[mine] = own[rows, :]
        absolute[theirs] = other[rows, :]


def mask_bias(ends, row, query_quarter, key_quarter, documents):
    query_point = query_quarter * 256 + lax.broadcasted_iota(jnp.int32, (1, 256), 1)
    begin = jnp.zeros((1, 256), jnp.int32)
    for index in range(documents):
        end = ends[row, index]
        begin = jnp.where(query_point >= end, jnp.maximum(begin, end), begin)
    key_point = key_quarter * 256 + lax.broadcasted_iota(jnp.int32, (256, 256), 0)
    return jnp.where((key_point <= query_point) & (key_point >= begin), 0.0, NEGATIVE)


def query_pads(tiles):
    first, second = tiles[:, :TILE].astype(F32), tiles[:, TILE:].astype(F32)
    lower = lanes_of(first.shape) < HD
    return [
        jnp.where(lower, first, 0.0).astype(BF16),
        jnp.where(lower, pltpu.roll(first, HD, 1), 0.0).astype(BF16),
        jnp.where(lower, second, 0.0).astype(BF16),
    ]


def attend_body(meta, ends, query, own, other, mixed, logs, keys, keys_turned, bias, scores):
    context = meta[1]
    documents = ends.shape[1]

    def one(row, carry):
        gather_keys(context, row, own, other, keys)
        for quarter in range(4):
            for head in range(HEADS):
                lanes = slice(head * TILE, (head + 1) * TILE)
                keys_turned[quarter, lanes, :] = keys[quarter, :, lanes].astype(F32).T.astype(BF16)
        outs = []
        for side in range(2):
            quarter = context if side == 0 else 3 - context
            count = 2 + side
            base = 0 if side == 0 else 1 - context
            rows = rows_at(row * 512 + side * 256, 256, 256)
            for step in range(count):
                bias[step] = mask_bias(ends, meta[3] + row, quarter, base + step, documents)
            pads = query_pads(query[rows, :])
            turned = []
            for head in range(HEADS):
                lanes = slice(head * TILE, (head + 1) * TILE)
                highest = jnp.full((1, 256), NEGATIVE, F32)
                for step in range(count):
                    value = dot_nt(keys[base + step, :, lanes], pads[head]) + bias[step]
                    scores[step] = value
                    highest = jnp.maximum(highest, jnp.max(value, axis=0, keepdims=True))
                total = jnp.zeros((1, 256), F32)
                for step in range(count):
                    value = jnp.exp(scores[step] - highest)
                    scores[step] = value
                    total = total + jnp.sum(value, axis=0, keepdims=True)
                inverse = 1.0 / total
                result = jnp.zeros((TILE, 256), F32)
                for step in range(count):
                    weights = (scores[step] * inverse).astype(BF16)
                    result = result + dot(keys_turned[base + step, lanes, :], weights)
                turned.append(result[HD:, :])
                logs[2 * row + side, head : head + 1, :] = highest + jnp.log(total)
            pair = jnp.concatenate(turned[:2], axis=0)
            mixed[rows_at(row * 768 + side * 256, 256, 256), :] = pair.T.astype(BF16)
            outs.append(turned[2])
        packed = jnp.concatenate(outs, axis=0)
        mixed[rows_at(row * 768 + 512, 256, 256), :] = packed.T.astype(BF16)
        return carry

    lax.fori_loop(0, query.shape[0] // 512, one, 0)


def silu_parts(gating):
    gate = 1.0 / (1.0 + jnp.exp(-gating))
    return gate, gating * gate


def joined_heads(row, side, heads, target, lower):
    start = row * 768 + side * 256
    for index in range(PARTS):
        target[:, index * TILE : (index + 1) * TILE] = heads[index][start : start + 256, :]
    for index in range(2):
        tail = slice(row * 768 + 512, row * 768 + 768)
        left = heads[2 * index][tail, :].astype(F32)
        right = heads[2 * index + 1][tail, :].astype(F32)
        if side == 0:
            tile = jnp.where(lower, left, pltpu.roll(right, HD, 1))
        else:
            tile = jnp.where(lower, pltpu.roll(left, HD, 1), right)
        target[:, (PARTS + index) * TILE : (PARTS + index + 1) * TILE] = tile.astype(BF16)


def feed_body(
    meta, ends, hidden, h0, h1, h2, h3, c0, c1, c2, c3, gains, output, gateup, down,
    o0, o1, o2, o3, second, active, grads, spread, middle_own, heads_own,
    joined, block_grad, block_middle,
):
    part, context = meta[0], meta[1]
    width = down.shape[1]
    gain = gains[1:2, :]
    lower = lanes_of((256, TILE)) < HD
    for row in range(hidden.shape[0] // 512):
        for side in range(2):
            block = 2 * row + side
            rows = slice(block * 256, block * 256 + 256)
            joined_heads(row, side, (h0, h1, h2, h3), joined, lower)
            for offset, piece in enumerate((c0, c1, c2, c3)):
                place = jnp.bitwise_xor(part, offset)
                target = rows_at(block * 256 + place * 64, 64, 64)
                spread[target, :] = piece[block * 64 : block * 64 + 64, :]
            quarter = context if side == 0 else 3 - context
            point = quarter * 256 + lax.broadcasted_iota(jnp.int32, (256, 1), 0)
            keep = point < ends[meta[3] + row, ends.shape[1] - 1]
            out_grad = jnp.where(keep, spread[rows, :].astype(F32), 0.0).astype(BF16)
            spread[rows, :] = out_grad
            middle = hidden[rows, :].astype(F32) + dot_nt(joined[...], output[...])
            block_middle[...] = middle
            normed = (middle * root_mean(middle) * gain).astype(BF16)
            second[rows, :] = normed
            own = slice(block * 64, block * 64 + 64)
            mine = rows_at(part * 64, 64, 64)
            middle_own[own, :] = block_middle[mine, :]
            heads_own[own, :] = joined[mine, :]
            gate_up = dot(normed, gateup[...])
            gating, upward = gate_up[:, :width], gate_up[:, width:]
            grad_active = dot(out_grad, down[...])
            gate, passed = silu_parts(gating)
            active[rows, :] = (passed * upward).astype(BF16)
            grads[rows, :width] = (
                grad_active * upward * gate * (1.0 + gating * (1.0 - gate))
            ).astype(BF16)
            grads[rows, width:] = (grad_active * passed).astype(BF16)
            block_grad[...] = dot_nt(grads[rows, :], gateup[...]).astype(BF16)
            for offset, piece in enumerate((o0, o1, o2, o3)):
                place = jnp.bitwise_xor(part, offset)
                piece[own, :] = block_grad[rows_at(place * 64, 64, 64), :]


def fed_body(meta, active, down, out, block_out):
    for block in range(active.shape[0] // 256):
        rows = slice(block * 256, block * 256 + 256)
        block_out[...] = dot_nt(active[rows, :], down[...]).astype(BF16)
        for place in range(PARTS):
            out[place, block * 64 : block * 64 + 64, :] = block_out[place * 64 : place * 64 + 64, :]


def split_rows(context, source, keep, send, lanes):
    count, rows, _ = keep.shape
    for index in range(count):
        keep[index, :, lanes] = source[rows_at((2 * index + context) * rows, rows, 32), :]
        send[index, :, lanes] = source[
            rows_at((2 * index + 1 - context) * rows, rows, 32), :
        ].astype(BF16)


def feed_weights_body(meta, *refs):
    blocks = (len(refs) - 3) // 4
    second, grads, active, spread = (refs[i * blocks : (i + 1) * blocks] for i in range(4))
    out, left, right = refs[4 * blocks :]
    turned = 0
    for normed, grad in zip(second, spread):
        for block in range(normed.shape[0] // 256):
            rows = slice(block * 256, block * 256 + 256)
            lanes = slice(turned * 256, turned * 256 + 256)
            left[:, lanes] = normed[rows, :].T
            right[:, lanes] = grad[rows, :].T
            turned += 1
    width = active[0].shape[1]
    for start in range(0, 3 * width, 256):
        total = None
        offset = 0
        for index in range(blocks):
            size = second[index].shape[0]
            span = slice(offset, offset + size)
            if start < 2 * width:
                value = dot(left[:, span], grads[index][:, start : start + 256])
            else:
                first = start - 2 * width
                value = dot(right[:, span], active[index][:, first : first + 256])
            total = value if total is None else total + value
            offset += size
        out[:, start : start + 256] = total.astype(BF16)


def middle_body(
    meta, ends, g0, g1, g2, g3, middle_ref, out_grad_ref, gains, output,
    s0, s1, s2, s3, grad_ref, low_ref, gain_ref,
):
    part, context = meta[0], meta[1]
    total = g0[...].astype(F32) + g1[...].astype(F32) + g2[...].astype(F32) + g3[...].astype(F32)
    middle = middle_ref[...]
    scale = root_mean(middle)
    gain = gains[1:2, :]
    keeps = []
    for block in range(middle.shape[0] // 64):
        row, side = block // 2, block % 2
        quarter = context if side == 0 else 3 - context
        point = quarter * 256 + part * 64 + lax.broadcasted_iota(jnp.int32, (64, 1), 0)
        keeps.append(point < ends[meta[3] + row, ends.shape[1] - 1])
    keep = jnp.concatenate([value.astype(F32) for value in keeps], axis=0)
    out_grad = out_grad_ref[...].astype(F32) * keep
    scaled = gain * total
    inner = jnp.mean(scaled * middle, axis=-1, keepdims=True)
    grad = out_grad + scale * scaled - middle * (scale * scale * scale * inner)
    grad_ref[...] = grad
    low = grad.astype(BF16)
    low_ref[...] = low
    gain_ref[...] = jnp.broadcast_to(
        jnp.sum(total * middle * scale, axis=0, keepdims=True), gain_ref.shape
    )
    heads = dot(low, output[...])
    lower = lanes_of((64, TILE)) < HD
    for offset, piece in enumerate((s0, s1, s2, s3)):
        tail = PARTS + offset // 2
        for row in range(middle.shape[0] // 128):
            rows = slice(row * 128, row * 128 + 128)
            piece[row * 192 : row * 192 + 128, :] = heads[
                rows, offset * TILE : (offset + 1) * TILE
            ].astype(BF16)
            former = heads[row * 128 : row * 128 + 64, tail * TILE : (tail + 1) * TILE]
            latter = heads[row * 128 + 64 : row * 128 + 128, tail * TILE : (tail + 1) * TILE]
            if offset % 2 == 0:
                packed = jnp.where(lower, former, pltpu.roll(latter, HD, 1))
            else:
                packed = jnp.where(lower, pltpu.roll(former, HD, 1), latter)
            piece[row * 192 + 128 : row * 192 + 192, :] = packed.astype(BF16)


def output_weights_body(meta, low, heads, grown_in, grown, tile, arrived):
    turned = low[...].T
    width = tile.shape[1]
    for start in range(0, width, 256):
        tile[:, start : start + 256] = dot(turned, heads[:, start : start + 256]).astype(BF16)
    copy = pltpu.make_async_copy(tile, grown.at[:, pl.ds(grown.shape[1] - width, width)], arrived)
    copy.start()
    copy.wait()


def attend_back_body(
    meta, ends, query, own, other, g0, g1, g2, g3, logs, cosine, sine,
    grad_query, grad_own, grad_other, keys, keys_turned, bias, grad_heads, probs, grad_probs, sums,
):
    part, context = meta[0], meta[1]
    documents = ends.shape[1]

    def one(row, carry):
        gather_keys(context, row, own, other, keys)
        sums[...] = jnp.zeros_like(sums)
        for quarter in range(4):
            for head in range(HEADS):
                lanes = slice(head * TILE, (head + 1) * TILE)
                keys_turned[quarter, lanes, :] = keys[quarter, :, lanes].astype(F32).T.astype(BF16)
        for offset, piece in enumerate((g0, g1, g2, g3)):
            place = jnp.bitwise_xor(part, offset)
            for side in range(2):
                start = row * 192 + side * 64
                grad_heads[side, rows_at(place * 64, 64, 64), :TILE] = piece[rows_at(start, 64, 64), :]
            grad_heads[0, rows_at(place * 64, 64, 64), TILE:] = piece[
                rows_at(row * 192 + 128, 64, 64), :
            ]
        for side in range(2):
            quarter = context if side == 0 else 3 - context
            count = 2 + side
            base = 0 if side == 0 else 1 - context
            rows = rows_at(row * 512 + side * 256, 256, 256)
            for step in range(count):
                bias[step] = mask_bias(ends, meta[3] + row, quarter, base + step, documents)
            pads = query_pads(query[rows, :])
            first = grad_heads[side, :, :TILE].astype(F32)
            second = grad_heads[0, :, TILE:].astype(F32)
            upper = lanes_of(first.shape) >= HD
            tail = pltpu.roll(second, HD, 1) if side == 0 else second
            grads = [
                jnp.where(upper, pltpu.roll(first, HD, 1), 0.0).astype(BF16),
                jnp.where(upper, first, 0.0).astype(BF16),
                jnp.where(upper, tail, 0.0).astype(BF16),
            ]
            turned = []
            for head in range(HEADS):
                lanes = slice(head * TILE, (head + 1) * TILE)
                log = logs[2 * row + side, head : head + 1, :]
                inner = jnp.zeros((1, 256), F32)
                for step in range(count):
                    block = keys[base + step, :, lanes]
                    chance = jnp.exp(dot_nt(block, pads[head]) + bias[step] - log)
                    slope = dot_nt(block, grads[head])
                    probs[step] = chance
                    grad_probs[step] = slope
                    inner = inner + jnp.sum(chance * slope, axis=0, keepdims=True)
                sides = jnp.concatenate([pads[head], grads[head]], axis=0)
                result = jnp.zeros((TILE, 256), F32)
                for step in range(count):
                    chance = probs[step]
                    slope = (chance * (grad_probs[step] - inner)).astype(BF16)
                    both = jnp.concatenate([slope, chance.astype(BF16)], axis=1)
                    sums[base + step, :, lanes] += dot(both, sides)
                    result = result + dot(keys_turned[base + step, lanes, :], slope)
                turned.append(result[:HD, :])
            cos, sin = cosine[rows, :], sine[rows, :]
            turned.append(jnp.zeros((HD, 256), F32))
            for index in range(2):
                tile = jnp.concatenate(turned[2 * index : 2 * index + 2], axis=0).T * HD**-0.5
                grad_query[rows, index * TILE : (index + 1) * TILE] = (
                    tile * cos - swapped(tile) * sin
                ).astype(BF16)
        for side in range(2):
            rows = rows_at(row * 512 + side * 256, 256, 256)
            mine = context if side == 0 else 3 - context
            theirs = 1 - context if side == 0 else 2 + context
            grad_own[rows, :] = sums[mine]
            grad_other[rows, :] = sums[theirs].astype(BF16)
        return carry

    lax.fori_loop(0, query.shape[0] // 512, one, 0)


def first_body(meta, grad_query, grad_own, arrived, cosine, sine, grads):
    def one(block, carry):
        rows = rows_at(block * 256, 256, 256)
        cos, sin = cosine[rows, :], sine[rows, :]
        lower = lanes_of(cos.shape) < HD
        grads[rows, : 2 * TILE] = grad_query[rows, :]
        for index in range(HEADS):
            lanes = slice(index * TILE, (index + 1) * TILE)
            tile = grad_own[rows, lanes] + arrived[rows, lanes].astype(F32)
            turned = tile * cos - swapped(tile) * sin
            grads[rows, (2 + index) * TILE : (3 + index) * TILE] = jnp.where(
                lower, turned, tile
            ).astype(BF16)
        return carry

    lax.fori_loop(0, grad_query.shape[0] // 256, one, 0)


def spread_grad_body(meta, grads, weight, out, block_grad):
    def one(block, carry):
        rows = rows_at(block * 256, 256, 256)
        block_grad[...] = dot_nt(grads[rows, :], weight[...]).astype(BF16)
        for place in range(PARTS):
            target = rows_at(block * 64, 64, 64)
            out[place, target, :] = block_grad[place * 64 : place * 64 + 64, :]
        return carry

    lax.fori_loop(0, grads.shape[0] // 256, one, 0)


def first_weights_body(meta, normed, grads, weight, gains, gain_two, *refs):
    outs, total, turned = refs[:-2], refs[-2], refs[-1]
    turned[...] = normed[...].T
    width = total.shape[1]
    for start in range(0, width, TILE):
        lanes = slice(start, start + TILE)
        total[:, lanes] = dot(turned[...], grads[:, lanes])
    product = total[...] * weight[...].astype(F32)
    column = jnp.sum(product, axis=1, keepdims=True)
    lane = lanes_of((normed.shape[1], TILE))
    row = lax.broadcasted_iota(jnp.int32, (TILE, normed.shape[1]), 0)
    two = jnp.where(row == HD + 1, gain_two[0:1, :], 0.0)
    one = jnp.where(row == HD, 1.0 / gains[0:1, :], 0.0)
    total[:, TILE : 2 * TILE] += two.T + one.T * column
    if len(outs) == 2:
        split_rows(meta[1], total, *outs, slice(0, width))
    else:
        outs[0][...] = total[...].astype(BF16)


def input_body(meta, landed, tokens, grad_middle, gains, out):
    total = landed[0].astype(F32)
    for index in range(1, PARTS):
        total = total + landed[index].astype(F32)
    values = tokens[...].astype(F32)
    scale = root_mean(values)
    scaled = gains[0:1, :] * total
    inner = jnp.mean(scaled * values, axis=-1, keepdims=True)
    out[...] = grad_middle[...] + scale * scaled - values * (scale * scale * scale * inner)


def context_sum_body(meta, keep, arrived, *outs):
    count = len(outs)
    for shift, out in enumerate(outs):
        index = lax.rem(meta[2] + shift, count)
        out[...] = (keep[index] + arrived[index].astype(F32)).astype(out.dtype)


def document_ends(lengths, dealing):
    documents = dealing.shape[-1]
    picked = (dealing[..., :, None] == jnp.arange(documents, dtype=jnp.int32)).astype(jnp.int32)
    placed = jnp.sum(picked * lengths[..., None, :documents], axis=-1)
    return jnp.cumsum(placed, axis=-1)


def rotary_tables(ends, context):
    inverse = ROTARY_BASE ** (-(jnp.arange(HD // 2, dtype=F32) * 2.0 / HD))
    inverse = jnp.tile(inverse, 4)
    inner = jnp.arange(256, dtype=jnp.int32)
    points = jnp.stack([context * 256 + inner, (3 - context) * 256 + inner]).reshape(1, 512)
    after = points[..., None] >= ends[:, None, :]
    position = points - jnp.max(jnp.where(after, ends[:, None, :], 0), axis=-1)
    phase = position.astype(F32).reshape(-1, 1) * inverse
    sign = jnp.where((jnp.arange(TILE) % HD) < HD // 2, -1.0, 1.0).astype(F32)
    return jnp.cos(phase), jnp.sin(phase) * sign


def adam_step(gradient, master, moment, variance, decay, rate):
    moment_new = BETA_ONE * moment + (1.0 - BETA_ONE) * gradient
    variance_new = BETA_TWO * variance + (1.0 - BETA_TWO) * gradient * gradient
    first_fix = 1.0 - BETA_ONE**STEP
    second_fix = 1.0 - BETA_TWO**STEP
    stepped = (
        moment_new / first_fix / (jnp.sqrt(variance_new / second_fix) + ADAM_EPSILON)
        + decay * master
    )
    return (gradient, master - rate * stepped, moment_new, variance_new)


def swap_ctx(value):
    return lax.ppermute(value, "ctx", [(0, 1), (1, 0)])


def across(value, offset):
    return lax.ppermute(value, "tensor", [(i, i ^ offset) for i in range(PARTS)])


def shift_dp(value, shift):
    size = lax.axis_size("dp")
    return lax.ppermute(value, "dp", [(i, (i + shift) % size) for i in range(size)])


def spread_all(value):
    return [value] + [across(value, offset) for offset in range(1, PARTS)]


def spread_in_turn(value):
    half = value.shape[0] // 2
    first, second = across(value, 1), across(value, 2)
    return [value, first, second, across(second[:half], 1), across(first[half:], 2)]


def exchange(pieces):
    return [pieces[0]] + [across(pieces[offset], offset) for offset in range(1, PARTS)]


def after(value, *others):
    return lax.optimization_barrier((value, others))[0]


class Chain:
    def __init__(self, meta):
        self.meta = meta

    def call(self, name, body, outs, scalars, arrays, scratch=(), grown=None):
        results = call(name, body, outs, (self.meta, *scalars), arrays, scratch, grown)
        self.meta = after(self.meta, results[-1])
        return results


def gather_blocks(block):
    count = lax.axis_size("dp")
    return [block] + [shift_dp(block, shift) for shift in range(1, count)]


def stack_blocks(chain, pieces):
    shape = (len(pieces), *pieces[0].shape)
    return chain.call("stack", stack_body, [(shape, BF16)], (), pieces)[0]


def context_sums(chain, keep, arrived):
    count = lax.axis_size("dp")
    _, rows, width = keep.shape
    outs = [((rows, width), F32)] + [((rows, width), BF16)] * (count - 1)
    return chain.call("context_sum", context_sum_body, outs, (), (keep, arrived))


def landed_blocks(sums):
    total = sums[0]
    for shift in range(1, len(sums)):
        total = total + shift_dp(sums[shift], shift).astype(F32)
    return total


def per_device(
    tokens,
    cotangent,
    document_lengths,
    dealing,
    query_weight,
    query_master,
    query_moment,
    query_variance,
    keyvalue_weight,
    keyvalue_master,
    keyvalue_moment,
    keyvalue_variance,
    output_weight,
    output_master,
    output_moment,
    output_variance,
    gateup_weight,
    gateup_master,
    gateup_moment,
    gateup_variance,
    down_weight,
    down_master,
    down_moment,
    down_variance,
    norm_gain,
    gain_master,
    gain_moment,
    gain_variance,
):
    features = tokens.shape[-1]
    row_count = tokens.shape[0]
    block_rows = query_weight.shape[0]
    hidden_width = down_weight.shape[0]
    block_count = lax.axis_size("dp")
    part = lax.axis_index("tensor").astype(jnp.int32)
    context = lax.axis_index("ctx").astype(jnp.int32)
    own_dp = lax.axis_index("dp").astype(jnp.int32)
    meta = jnp.stack([part, context, own_dp, jnp.int32(0)])
    ends = document_ends(document_lengths, dealing)

    chain = Chain(meta)
    own_rows = row_count * 128
    count = row_count * 512
    own_tokens = tokens.reshape(own_rows, features)
    own_grad = cotangent.reshape(own_rows, features)
    token_pieces = spread_in_turn(own_tokens)

    keys = [keyvalue_weight[i, :, h * HD : (h + 1) * HD] for h in range(HEADS) for i in range(2)]
    filler = jnp.zeros((block_rows, HD - 2), BF16)
    first_block = jnp.concatenate([query_weight, norm_gain.T, filler] + keys, axis=1)
    by_hand = block_rows % 32 == 0 and block_count <= 8
    first_pieces = gather_blocks(first_block) if by_hand else []
    output_pieces = spread_all(after(output_weight.T, token_pieces[1:3], first_pieces))
    second_block = jnp.concatenate(
        [piece[:, :TILE] for piece in output_pieces]
        + [piece[:, TILE:] for piece in output_pieces]
        + [gateup_weight[0], gateup_weight[1], down_weight.T],
        axis=1,
    )
    cosine, sine = rotary_tables(ends, context)
    second_full = lax.all_gather(second_block, ("dp", "ctx"), axis=0, tiled=True)
    if by_hand:
        first_own = stack_blocks(chain, first_pieces)
        weight, gains = chain.call(
            "assemble_first",
            assemble_first_body,
            [((features, QKV), BF16), ((8, features), F32)],
            (),
            (first_own, swap_ctx(first_own)),
        )
    else:
        first_full = lax.all_gather(first_block, ("dp", "ctx"), axis=0, tiled=True)
        gains = jnp.pad(first_full[:, 3 * HD : 3 * HD + 2].T.astype(F32), ((0, 6), (0, 0)))
        lane = jnp.arange(QKV)
        weight = jnp.where((lane >= 3 * HD) & (lane < 4 * HD), 0, first_full).astype(BF16)
    hidden, normed, query, keyval = chain.call(
        "project",
        project_body,
        [((count, features), BF16)] * 2 + [((count, 2 * TILE), BF16), ((count, 3 * TILE), BF16)],
        (),
        (*token_pieces, gains, weight, cosine, sine),
    )
    grad_pieces = spread_all(after(own_grad, token_pieces))
    keyval_other = swap_ctx(keyval)
    key_scratch = [((4, 256, 3 * TILE), BF16), ((4, 3 * TILE, 256), BF16), ((3, 256, 256), F32)]
    mixed, logs = chain.call(
        "attend",
        attend_body,
        [((row_count * 768, TILE), BF16), ((row_count * 2, 8, 256), F32)],
        (ends,),
        (query, keyval, keyval_other),
        key_scratch + [((3, 256, 256), F32)],
    )
    head_pieces = spread_all(mixed)
    output = second_full[:, :features]
    gateup = second_full[:, features : features + 2 * hidden_width]
    down = second_full[:, features + 2 * hidden_width :]
    piece_shape = ((own_rows, features), BF16)
    feed = chain.call(
        "feed",
        feed_body,
        [piece_shape] * 4
        + [
            ((count, features), BF16),
            ((count, hidden_width), BF16),
            ((count, 2 * hidden_width), BF16),
            ((count, features), BF16),
            ((own_rows, features), F32),
            ((own_rows, features), BF16),
        ],
        (ends,),
        (hidden, *head_pieces, *grad_pieces, gains, output, gateup, down),
        [((256, features), BF16), ((256, features), BF16), ((256, features), F32)],
    )
    second_grads = exchange(feed[:4])
    second, active, feed_grads, spread, middle_own, heads_own = feed[4:]
    feed_sum = chain.call(
        "feed_weights",
        feed_weights_body,
        [((features, 3 * hidden_width + features), BF16)],
        (),
        (second, feed_grads, active, spread),
        [((features, count), BF16), ((features, count), BF16)],
    )[0]
    fed = chain.call(
        "fed",
        fed_body,
        [((PARTS, own_rows, features), BF16)],
        (),
        (active, down),
        [((256, features), BF16)],
    )[0]
    sends = chain.call(
        "middle",
        middle_body,
        [((row_count * 192, TILE), BF16)] * 4
        + [((own_rows, features), F32), ((own_rows, features), BF16), ((8, features), F32)],
        (ends,),
        (*second_grads, middle_own, own_grad, gains, output),
    )
    grad_heads = exchange(sends[:4])
    grad_middle, grad_low, gain_two = sends[4:]
    grad_heads = exchange(sends[:4])
    grad_middle, grad_low, gain_two = sends[4:]
    feed_total = lax.psum_scatter(
        after(feed_sum, grad_low), ("dp", "ctx"), scatter_dimension=0, tiled=True
    ).astype(F32)
    wide_sum = chain.call(
        "output_weights",
        output_weights_body,
        [],
        (),
        (grad_low, heads_own),
        [((features, features), BF16)],
        grown=feed_sum,
    )[0]
    fed_landed = lax.all_to_all(after(fed, grad_heads), "tensor", 0, 0)
    block_output = middle_own + fed_landed.astype(F32).sum(axis=0)
    block_output = block_output.astype(BF16).reshape(tokens.shape)
    grad_query, grad_own, grad_other = chain.call(
        "attend_back",
        attend_back_body,
        [((count, 2 * TILE), BF16), ((count, 3 * TILE), F32), ((count, 3 * TILE), BF16)],
        (ends,),
        (query, keyval, keyval_other, *grad_heads, logs, cosine, sine),
        key_scratch
        + [
            ((2, 256, 2 * TILE), BF16),
            ((3, 256, 256), F32),
            ((3, 256, 256), F32),
            ((4, 256, 3 * TILE), F32),
        ],
    )
    arrived = swap_ctx(grad_other)
    wide_total = lax.psum_scatter(
        after(wide_sum, grad_other), ("dp", "ctx"), scatter_dimension=0, tiled=True
    ).astype(F32)
    feed_total = wide_total[:, : 3 * hidden_width]
    output_total = wide_total[:, 3 * hidden_width :]
    grads = chain.call(
        "first",
        first_body,
        [((count, QKV), BF16)],
        (),
        (grad_query, grad_own, arrived, cosine, sine),
    )[0]
    block_shape = (block_count, block_rows, QKV)
    first_sums = chain.call(
        "first_weights",
        first_weights_body,
        [(block_shape, F32), (block_shape, BF16)] if by_hand else [((features, QKV), BF16)],
        (),
        (normed, grads, weight, gains, gain_two),
        [((features, QKV), F32), ((features, count), BF16)],
    )
    if by_hand:
        arrived_one = swap_ctx(first_sums[1])
    spread_grads = chain.call(
        "spread_grad",
        spread_grad_body,
        [((PARTS, own_rows, features), BF16)],
        (),
        (grads, after(weight, fed_landed)),
        [((256, features), BF16)],
    )[0]
    first_grads = lax.all_to_all(spread_grads, "tensor", 0, 0)
    if by_hand:
        first_total = landed_blocks(context_sums(chain, first_sums[0], arrived_one))
    else:
        first_total = lax.psum_scatter(
            first_sums[0], ("dp", "ctx"), scatter_dimension=0, tiled=True
        ).astype(F32)
    input_grad = chain.call(
        "input",
        input_body,
        [((own_rows, features), F32)],
        (),
        (first_grads, own_tokens, grad_middle, gains),
    )[0].reshape(tokens.shape)

    output_sends = []
    for offset in range(PARTS):
        head_lanes = output_total[:, offset * TILE : (offset + 1) * TILE]
        start = PARTS * TILE + offset * HD
        output_sends.append(
            jnp.concatenate([head_lanes, output_total[:, start : start + HD]], axis=1)
        )
    output_grad = output_sends[0]
    for offset in range(1, PARTS):
        output_grad = output_grad + across(output_sends[offset].astype(BF16), offset).astype(F32)
    output_grad = output_grad.T

    gain_total = first_total[:, 3 * HD : 3 * HD + 2].T
    gain_size = block_rows // PARTS
    gain_grad = lax.dynamic_slice_in_dim(gain_total, part * gain_size, gain_size, 1)
    for offset in range(1, PARTS):
        target = jnp.bitwise_xor(part, offset)
        piece = lax.dynamic_slice_in_dim(gain_total, target * gain_size, gain_size, 1)
        gain_grad = gain_grad + across(piece, offset)

    query_grad = first_total[:, : HEADS * HD]
    key_tiles = [first_total[:, (2 + h) * TILE : (3 + h) * TILE] for h in range(HEADS)]
    keyvalue_grad = jnp.stack(
        [
            jnp.concatenate([tile[:, :HD] for tile in key_tiles], axis=1),
            jnp.concatenate([tile[:, HD:] for tile in key_tiles], axis=1),
        ]
    )
    gateup_grad = jnp.stack(
        [feed_total[:, :hidden_width], feed_total[:, hidden_width : 2 * hidden_width]]
    )
    down_grad = feed_total[:, 2 * hidden_width :].T
    return (
        block_output,
        input_grad,
        *adam_step(
            query_grad, query_master, query_moment, query_variance, WEIGHT_DECAY, LEARNING_RATE
        ),
        *adam_step(
            keyvalue_grad,
            keyvalue_master,
            keyvalue_moment,
            keyvalue_variance,
            WEIGHT_DECAY,
            LEARNING_RATE,
        ),
        *adam_step(
            output_grad, output_master, output_moment, output_variance, WEIGHT_DECAY, OUTPUT_RATE
        ),
        *adam_step(
            gateup_grad, gateup_master, gateup_moment, gateup_variance, WEIGHT_DECAY, LEARNING_RATE
        ),
        *adam_step(
            down_grad, down_master, down_moment, down_variance, WEIGHT_DECAY, LEARNING_RATE
        ),
        *adam_step(gain_grad, gain_master, gain_moment, gain_variance, 0.0, GAIN_RATE),
    )


def solution(mesh):
    hidden = P("dp", "ctx", None, "tensor", None)
    rows = P(("dp", "ctx"), "tensor")
    stacked = P(None, ("dp", "ctx"), "tensor")
    columns = P("tensor", ("dp", "ctx"))
    gain = P(None, ("dp", "ctx", "tensor"))
    return jax.shard_map(
        per_device,
        mesh=mesh,
        in_specs=(
            (hidden, hidden, P("dp", None), P("dp", None))
            + (rows,) * 4
            + (stacked,) * 4
            + (columns,) * 4
            + (stacked,) * 4
            + (columns,) * 4
            + (P(None, ("dp", "ctx")),)
            + (gain,) * 3
        ),
        out_specs=(
            (hidden, hidden)
            + (rows,) * 4
            + (stacked,) * 4
            + (columns,) * 4
            + (stacked,) * 4
            + (columns,) * 4
            + (gain,) * 4
        ),
        check_vma=False,
    )
```

time: 583 us -> 238 us (0.41); the launches traced: 575 us -> 237 us
  waiting for transfers between devices: 242 us -> 45.6 us
  blocking collectives: 112 us -> 0 us
  Pallas kernels: 0 us -> 85 us
  matrix products: 70.4 us -> 0 us
  local copies, waits for them, and re-layouts: 61.8 us -> 27.7 us
  starting transfers between devices: 20.8 us -> 51.3 us
  other arithmetic: 42.7 us -> 12.8 us
  loops' own time: 8.36 us -> 0 us
    reduce_scatter x5 -> x1, waiting for transfers between devices: 115 us -> 0.02 us  [per_device(): lax.psum_scatter(after(wide_sum, grad_other), ('dp', 'ctx'), scatter_dime...]
    pallas_call x0 -> x15, Pallas kernels: none -> 85 us  [call(): pl.pallas_call(body, out_shape=out_shape, in_specs=[SMEM] * len(scalars)...]
    all_gather x5 -> x0, blocking collectives: 74.9 us -> none  [the longest x1 16.2 us: per_device(): lax.all_gather(keyvalue_weight, ('dp', 'ctx'), axis=1, tiled=True)]
    dot_general x35 -> x0, matrix products: 70.4 us -> none  [the longest x7 16.3 us: matmul(): return jnp.dot(left, right, preferred_element_type=jnp.float32)]
    all_gather x6 -> x1, waiting for transfers between devices: 71.2 us -> 4.91 us  [per_device(): lax.all_gather(second_block, ('dp', 'ctx'), axis=0, tiled=True)]
    all_to_all x5 -> x2, waiting for transfers between devices: 55.7 us -> 7.9 us  [the longest x1 7.89 us: per_device(): fed_landed = lax.all_to_all(after(fed, grad_heads), 'tensor', 0, 0)]
    ppermute x0 -> x35, starting transfers between devices: none -> 44.1 us  [the longest x25 32.7 us: across(): lax.ppermute(value, 'tensor', [(i, i ^ offset) for i in range(PARTS)])]
    unnamed x1 -> x0, blocking collectives: 37 us -> none
  transfers between devices with their start and end apart: 16 -> 39, of which waited for: 11 -> 14; matrix products, arithmetic and copies ran while one was open for 12% -> 11% of each run, Pallas kernels for 0% -> 23%
where the time goes in v1:
time: 238 us; the launch traced here: 237 us
  Pallas kernels  85 us (36%)
  starting transfers between devices  51.3 us (22%)
  waiting for transfers between devices  45.6 us (19%)
  local copies, waits for them, and re-layouts  27.7 us (12%)
  between operations  14.8 us (6%)
  other arithmetic  12.8 us (5%)
    pallas_call x15, Pallas kernels, call(): pl.pallas_call(body, out_shape=out_shape, in_specs=[SMEM] * len(scalars)...  85 us
    ppermute x25, starting transfers between devices, across(): lax.ppermute(value, 'tensor', [(i, i ^ offset) for i in range(PARTS)])  32.7 us
    ppermute x25, waiting for transfers between devices, across(): lax.ppermute(value, 'tensor', [(i, i ^ offset) for i in range(PARTS)])  20.1 us
    unnamed x119, local copies, waits for them, and re-layouts  15.8 us
    ppermute x6, waiting for transfers between devices, shift_dp(): lax.ppermute(value, 'dp', [(i, (i + shift) % size) for i in range(size)])  12.6 us
    ppermute x6, starting transfers between devices, shift_dp(): lax.ppermute(value, 'dp', [(i, (i + shift) % size) for i in range(size)])  10.9 us
    all_to_all x1, waiting for transfers between devices, per_device(): fed_landed = lax.all_to_all(after(fed, grad_heads), 'tensor', 0, 0)  7.89 us
    all_gather x1, waiting for transfers between devices, per_device(): lax.all_gather(second_block, ('dp', 'ctx'), axis=0, tiled=True)  4.91 us
  transfers between devices with their start and end apart: 39, of which 14 were waited for; matrix products, arithmetic and copies ran while one was open for 11% of the time, Pallas kernels for 23%

profile of v1, /device:TPU:0, one launch (start us, length us, event | category | flops | bytes accessed | tf_op | source)
XLA Modules:
  0.0 237.2 jit_solution(895636690346376006)
XLA Ops:
  7.3 3.0 %collective-permute-start.4 = (bf16[256,768]{1,0:T(8,128)(2,1)}, bf16[256,768]{1,0:T(8,128)(2,1)S(1)}, u32[]{:S(2)}, u32[]{:S(2)}) collective-permute-start(bf16[256,768]{1,0:T(8,128)(2,1)} %bitcast.69), channel_id=1, source_target_pairs={{0,1},{1,0},{2,3},{3,2},{4,5},{5,4},{6,7},{7,6},{8,9},{9,8},{10,11... | collective-permute-start | bytes 1179656 | tf_op jit(solution)/shard_map/ppermute | solution.py:571
  10.3 1.5 collective-permute-start.5
  14.5 1.6 collective-permute-start
  16.1 2.6 %collective-permute-start.1 = (bf16[96,640]{1,0:T(8,128)(2,1)S(1)}, bf16[96,640]{1,0:T(8,128)(2,1)S(1)}, u32[]{:S(2)}, u32[]{:S(2)}) collective-permute-start(bf16[96,640]{1,0:T(8,128)(2,1)S(1)} %concatenate.27.refs_0_), channel_id=1, source_target_pairs={{0,16},{8,24},{16,0},{24,8},{1,17},{9,25},{17,1},{25,9},{2,18},{10... | collective-permute-start | bytes 368648 | tf_op jit(solution)/shard_map/ppermute | solution.py:576
  20.9 1.7 collective-permute-done.refs_1_
  22.6 3.6 %collective-permute-done.1.refs_2_ = bf16[96,640]{1,0:T(8,128)(2,1)S(1)} collective-permute-done((bf16[96,640]{1,0:T(8,128)(2,1)S(1)}, bf16[96,640]{1,0:T(8,128)(2,1)S(1)}, u32[]{:S(2)}, u32[]{:S(2)}) %collective-permute-start.1) | collective-permute-done | bytes 122912 | tf_op jit(solution)/shard_map/ppermute | solution.py:576
  27.5 2.6 %collective-permute-start.17 = (bf16[96,192]{1,0:T(8,128)(2,1)S(1)}, bf16[96,192]{1,0:T(8,128)(2,1)S(1)}, u32[]{:S(2)}, u32[]{:S(2)}) collective-permute-start(bf16[96,192]{1,0:T(8,128)(2,1)S(1)} %bitcast.77), channel_id=1, source_target_pairs={{0,3},{1,2},{2,1},{3,0},{4,7},{5,6},{6,5},{7,4},{8,11},{9,10},{10,... | collective-permute-start | bytes 110600 | tf_op jit(solution)/shard_map/ppermute | solution.py:571
  35.1 1.9 stack.47.own
  37.1 1.7 collective-permute-start.6
  38.8 1.6 collective-permute-start.7
  40.4 3.1 %fusion = (f32[1024,128]{1,0:T(8,128)}, f32[1024,128]{1,0:T(8,128)}) fusion(f32[128]{0:T(128)S(1)} %compare_select_fusion.2, f32[128]{0:T(128)S(1)} %mul.261, f32[1024]{0:T(1024)S(1)} %bitcast.84), kind=kLoop, calls=%fused_computation.5 | loop fusion | flops 262144 | bytes 1053696 | tf_op jit(solution)/shard_map/mul | solution.py:551
  44.3 2.3 assemble_first.1
  47.3 8.1 %project.1 = (bf16[1024,768]{1,0:T(8,128)(2,1)}, bf16[1024,768]{1,0:T(8,128)(2,1)}, bf16[1024,256]{1,0:T(8,128)(2,1)}, bf16[1024,384]{1,0:T(8,128)(2,1)}) custom-call(s32[4]{0:T(128)} %pad_add_fusion.meta, bf16[256,768]{1,0:T(8,128)(2,1)} %bitcast.71, bf16[256,768]{1,0:T(8,128)(2,1)} %copy-done.5, bf16[256,768]{1,0:T(8,128)(2,1)} %copy-done.6, ...), custom_call_target="tpu_custom_call" | custom-call | tf_op jit(solution)/shard_map/project/pallas_call | solution.py:44
  56.8 2.2 collective-permute-start.14
  59.9 8.5 %attend.1 = (bf16[1536,128]{1,0:T(8,128)(2,1)}, f32[4,8,256]{2,1,0:T(8,128)}) custom-call(s32[4]{0:T(128)} %pad_add_fusion.meta, s32[2,7]{1,0:T(2,128)} %copy-done.44, bf16[1024,256]{1,0:T(8,128)(2,1)} %get-tuple-element.85.query, bf16[1024,384]{1,0:T(8,128)(2,1)} %get-tuple-element.83.own, bf16[1024,384]{1,0:T(8,128)(2,1)} %copy-done.1), custom_call_target="tpu_custom_call" | custom-call | tf_op jit(solution)/shard_map/attend/pallas_call | solution.py:44
  69.2 1.4 collective-permute-start.11
  71.9 4.9 %all-gather.2.cloned.1.call-done = bf16[768,2304]{1,0:T(8,128)(2,1)} async-done(((bf16[96,2304]{1,0:T(8,128)(2,1)}), bf16[768,2304]{1,0:T(8,128)(2,1)}) %all-gather.2.cloned.1.call-update) | async-done | bytes 3538960 | tf_op jit(solution)/shard_map/all_gather | solution.py:692
  76.8 2.7 %slice.201.gateup = bf16[768,1024]{1,0:T(8,128)(2,1)} slice(bf16[768,2304]{1,0:T(8,128)(2,1)} %all-gather.2.cloned.1.call-done), slice={[0:768], [768:1792]} | slice | bytes 3145728 | tf_op jit(solution)/shard_map/slice | solution.py:727
  79.5 2.4 %slice.200.output = bf16[768,768]{1,0:T(8,128)(2,1)} slice(bf16[768,2304]{1,0:T(8,128)(2,1)} %all-gather.2.cloned.1.call-done), slice={[0:768], [0:768]} | slice | bytes 2359296 | tf_op jit(solution)/shard_map/slice | solution.py:726
  81.9 2.1 slice.202.down
  84.3 8.5 %collective-permute-done.10.h2 = bf16[1536,128]{1,0:T(8,128)(2,1)S(1)} collective-permute-done((bf16[1536,128]{1,0:T(8,128)(2,1)}, bf16[1536,128]{1,0:T(8,128)(2,1)S(1)}, u32[]{:S(2)}, u32[]{:S(2)}) %collective-permute-start.10) | collective-permute-done | bytes 393248 | tf_op jit(solution)/shard_map/ppermute | solution.py:571
  93.7 13.5 %feed.1 = (bf16[256,768]{1,0:T(8,128)(2,1)}, bf16[256,768]{1,0:T(8,128)(2,1)}, bf16[256,768]{1,0:T(8,128)(2,1)}, bf16[256,768]{1,0:T(8,128)(2,1)}, bf16[1024,768...) custom-call(s32[4]{0:T(128)} %pad_add_fusion.meta, ...), custom_call_target="tpu_custom_call" | custom-call | tf_op jit(solution)/shard_map/feed/pallas_call | solution.py:44
  109.3 1.4 collective-permute-start.20
  110.8 7.3 %feed_weights.1.grown_in = bf16[768,2304]{1,0:T(8,128)(2,1)} custom-call(s32[4]{0:T(128)} %pad_add_fusion.meta, bf16[1024,768]{1,0:T(8,128)(2,1)} %get-tuple-element.95.refs_0_, bf16[1024,1024]{1,0:T(8,128)(2,1)} %get-tuple-element.96.refs_1_, bf16[1024,512]{1,0:T(8,128)(2,1)} %get-tuple-element.97.refs_2_.active, bf16[1024,768]{1,0:T(8,128)(2,1)} %get-tuple-element.98.refs_3_), custom_call_target="tpu_custom_call" | custom-call | tf_op jit(solution)/shard_map/feed_weights/pallas_call | solution.py:44
  118.1 3.7 %fed.1 = bf16[4,256,768]{2,1,0:T(8,128)(2,1)} custom-call(s32[4]{0:T(128)} %pad_add_fusion.meta, bf16[1024,512]{1,0:T(8,128)(2,1)} %get-tuple-element.97.refs_2_.active, bf16[768,512]{1,0:T(8,128)(2,1)} %slice.202.down), custom_call_target="tpu_custom_call" | custom-call | tf_op jit(solution)/shard_map/fed/pallas_call | solution.py:44
  121.8 5.6 %collective-permute-done.20.g3 = bf16[256,768]{1,0:T(8,128)(2,1)S(1)} collective-permute-done((bf16[256,768]{1,0:T(8,128)(2,1)}, bf16[256,768]{1,0:T(8,128)(2,1)S(1)}, u32[]{:S(2)}, u32[]{:S(2)}) %collective-permute-start.20) | collective-permute-done | bytes 393248 | tf_op jit(solution)/shard_map/ppermute | solution.py:571
  128.1 4.1 %middle.1 = (bf16[384,128]{1,0:T(8,128)(2,1)}, bf16[384,128]{1,0:T(8,128)(2,1)}, bf16[384,128]{1,0:T(8,128)(2,1)}, bf16[384,128]{1,0:T(8,128)(2,1)}, f32[256,768...) custom-call(s32[4]{0:T(128)} %pad_add_fusion.meta, s32[2,7]{1,0:T(2,128)} %copy-done.44, ...), custom_call_target="tpu_custom_call" | custom-call | tf_op jit(solution)/shard_map/middle/pallas_call | solution.py:44
  132.3 1.5 collective-permute-start.21
  135.8 2.8 %output_weights.1 = bf16[768,2304]{1,0:T(8,128)(2,1)} custom-call(s32[4]{0:T(128)} %pad_add_fusion.meta, bf16[256,768]{1,0:T(8,128)(2,1)} %get-tuple-element.112.low, bf16[256,768]{1,0:T(8,128)(2,1)} %get-tuple-element.93.heads, bf16[768,2304]{1,0:T(8,128)(2,1)} %feed_weights.1.grown_in), custom_call_target="tpu_custom_call", output_to_operand_aliasing={{}: (3, {})} | custom-call | tf_op jit(solution)/shard_map/output_weights/pallas_call | solution.py:44
  138.6 1.8 collective-permute-done.23.g3
  141.1 12.4 %attend_back.1 = (bf16[1024,256]{1,0:T(8,128)(2,1)}, f32[1024,384]{1,0:T(8,128)}, bf16[1024,384]{1,0:T(8,128)(2,1)}) custom-call(s32[4]{0:T(128)} %pad_add_fusion.meta, s32[2,7]{1,0:T(2,128)} %copy-done.44, bf16[1024,256]{1,0:T(8,128)(2,1)} %get-tuple-element.85.query, bf16[1024,384]{1,0:T(8,128)(2,1)} %get-tuple-element.83.own, ...), custom_call_target="tpu_custom_call" | custom-call | tf_op jit(solution)/shard_map/attend_back/pallas_call | solution.py:44
  154.6 3.6 %all-to-all-start = ((bf16[4,256,768]{2,1,0:T(8,128)(2,1)}), bf16[4,256,768]{2,1,0:T(8,128)(2,1)S(1)}, u32[]{:S(2)}, u32[]{:S(2)}) async-start(bf16[4,256,768]{2,1,0:T(8,128)(2,1)} %fed.1), calls=%async_computation | async-start | bytes 3145728 | tf_op jit(solution)/shard_map/all_to_all | solution.py:788
  159.1 4.5 %first.1.grads = bf16[1024,640]{1,0:T(8,128)(2,1)} custom-call(s32[4]{0:T(128)} %pad_add_fusion.meta, bf16[1024,256]{1,0:T(8,128)(2,1)} %get-tuple-element.116.grad_query, f32[1024,384]{1,0:T(8,128)} %get-tuple-element.117.grad_own, bf16[1024,384]{1,0:T(8,128)(2,1)} %copy-done.7, f32[1024,128]{1,0:T(8,128)} %get-tuple-element.261.cosine, ...), custom_call_target="tpu_custom_call" | custom-call | tf_op jit(solution)/shard_map/first/pallas_call | solution.py:44
  163.7 5.7 %first_weights.1 = (f32[4,96,640]{2,1,0:T(8,128)}, bf16[4,96,640]{2,1,0:T(8,128)(2,1)}) custom-call(s32[4]{0:T(128)} %pad_add_fusion.meta, bf16[1024,768]{1,0:T(8,128)(2,1)} %get-tuple-element.119.normed, bf16[1024,640]{1,0:T(8,128)(2,1)} %first.1.grads, bf16[768,640]{1,0:T(8,128)(2,1)} %get-tuple-element.122.weight, f32[8,768]{1,0:T(8,128)} %get-tuple-element.80.gains, ...), custom_call_target="tpu_custom_call" | custom-call | tf_op jit(solution)/shard_map/first_weights/pallas_call | solution.py:44
  170.5 7.9 %all-to-all-done = bf16[4,256,768]{2,1,0:T(8,128)(2,1)S(1)} async-done(((bf16[4,256,768]{2,1,0:T(8,128)(2,1)}), bf16[4,256,768]{2,1,0:T(8,128)(2,1)S(1)}, u32[]{:S(2)}, u32[]{:S(2)}) %all-to-all-start) | async-done | bytes 1572896 | tf_op jit(solution)/shard_map/all_to_all | solution.py:788
  178.4 4.8 %spread_grad.1 = bf16[4,256,768]{2,1,0:T(8,128)(2,1)} custom-call(s32[4]{0:T(128)} %pad_add_fusion.meta, bf16[1024,640]{1,0:T(8,128)(2,1)} %first.1.grads, bf16[768,640]{1,0:T(8,128)(2,1)} %get-tuple-element.122.weight), custom_call_target="tpu_custom_call" | custom-call | tf_op jit(solution)/shard_map/spread_grad/pallas_call | solution.py:44
  183.2 3.6 %all-to-all-start.1 = ((bf16[4,256,768]{2,1,0:T(8,128)(2,1)}), bf16[4,256,768]{2,1,0:T(8,128)(2,1)S(1)}, u32[]{:S(2)}, u32[]{:S(2)}) async-start(bf16[4,256,768]{2,1,0:T(8,128)(2,1)} %spread_grad.1), calls=%async_computation.1 | async-start | bytes 3145728 | tf_op jit(solution)/shard_map/all_to_all | solution.py:837
  187.9 2.3 context_sum.1
  190.2 2.9 %collective-permute-start.26 = (bf16[96,640]{1,0:T(8,128)(2,1)}, bf16[96,640]{1,0:T(8,128)(2,1)S(1)}, u32[]{:S(2)}, u32[]{:S(2)}) collective-permute-start(bf16[96,640]{1,0:T(8,128)(2,1)} %get-tuple-element.129), channel_id=1, source_target_pairs={{0,8},{8,16},{16,24},{24,0},{1,9},{9,17},{17,25},{25,1},{2,10},{10... | collective-permute-start | bytes 368648 | tf_op jit(solution)/shard_map/ppermute | solution.py:576
  193.1 1.7 collective-permute-start.27
  195.5 2.0 add_convert_fusion
  197.5 2.3 collective-permute-done.26
  199.8 4.8 %collective-permute-done.27 = bf16[96,640]{1,0:T(8,128)(2,1)S(1)} collective-permute-done((bf16[96,640]{1,0:T(8,128)(2,1)}, bf16[96,640]{1,0:T(8,128)(2,1)S(1)}, u32[]{:S(2)}, u32[]{:S(2)}) %collective-permute-start.27) | collective-permute-done | bytes 122912 | tf_op jit(solution)/shard_map/ppermute | solution.py:576
  204.7 1.9 collective-permute-start.32
  206.6 1.5 collective-permute-start.33
  210.3 2.4 collective-permute-done.34
  216.7 3.1 %input.1 = f32[256,768]{1,0:T(8,128)} custom-call(s32[4]{0:T(128)} %pad_add_fusion.meta, bf16[4,256,768]{2,1,0:T(8,128)(2,1)} %copy-done, bf16[256,768]{1,0:T(8,128)(2,1)} %bitcast.72, f32[256,768]{1,0:T(8,128)} %get-tuple-element.127.grad_middle, f32[8,768]{1,0:T(8,128)} %get-tuple-element.80.gains), custom_call_target="tpu_custom_call" | custom-call | tf_op jit(solution)/shard_map/input/pallas_call | solution.py:44
  222.3 2.7 %collective-permute-start.31 = (bf16[96,192]{1,0:T(8,128)(2,1)S(1)}, bf16[96,192]{1,0:T(8,128)(2,1)S(1)}, u32[]{:S(2)}, u32[]{:S(2)}) collective-permute-start(bf16[96,192]{1,0:T(8,128)(2,1)S(1)} %pad_maximum_fusion.4), channel_id=1, source_target_pairs={{0,3},{1,2},{2,1},{3,0},{4,7},{5,6},{6,5},{7,4},{8,11},{9,10},{10,... | collective-permute-start | bytes 110600 | tf_op jit(solution)/shard_map/ppermute | solution.py:571
  (231 shorter events, 42.9 us)
Async XLA Ops:
  7.2 25.3 %copy-start.37 = (bf16[512,96]{0,1:T(8,128)(2,1)S(1)}, bf16[512,96]{0,1:T(8,128)(2,1)}, u32[]{:S(2)}) copy-start(bf16[512,96]{0,1:T(8,128)(2,1)} %param.48) | copy-start | bytes 294916
  7.2 26.3 %copy-start.46 = (s32[2,7]{1,0:T(2,128)S(1)}, s32[2,7]{1,0:T(2,128)}, u32[]{:S(2)}) copy-start(s32[2,7]{1,0:T(2,128)} %param.31) | copy-start | bytes 172
  7.2 26.4 %copy-start.47 = (s32[2,8]{1,0:T(2,128)S(1)}, s32[2,8]{1,0:T(2,128)}, u32[]{:S(2)}) copy-start(s32[2,8]{1,0:T(2,128)} %param.30) | copy-start | bytes 196
  7.2 69.6 %all-gather.2.cloned.1.call-start = ((), (), s32[]{:S(2)}) async-start(), calls=%async_computation.3 | async-start | bytes 3981312 | tf_op jit(solution)/shard_map/all_gather | solution.py:692
  7.3 19.2 %collective-permute-start.4 = (bf16[256,768]{1,0:T(8,128)(2,1)}, bf16[256,768]{1,0:T(8,128)(2,1)S(1)}, u32[]{:S(2)}, u32[]{:S(2)}) collective-permute-start(bf16[256,768]{1,0:T(8,128)(2,1)} %bitcast.69), channel_id=1, source_target_pairs={{0,1},{1,0},{2,3},{3,2},{4,5},{5,4},{6,7},{7,6},{8,9},{9,8},{10,11... | collective-permute-start | bytes 1179656 | tf_op jit(solution)/shard_map/ppermute | solution.py:571
  10.3 16.2 %collective-permute-start.5 = (bf16[256,768]{1,0:T(8,128)(2,1)}, bf16[256,768]{1,0:T(8,128)(2,1)S(1)}, u32[]{:S(2)}, u32[]{:S(2)}) collective-permute-start(bf16[256,768]{1,0:T(8,128)(2,1)} %bitcast.70), channel_id=1, source_target_pairs={{0,2},{1,3},{2,0},{3,1},{4,6},{5,7},{6,4},{7,5},{8,10},{9,11},{10,... | collective-permute-start | bytes 1179656 | tf_op jit(solution)/shard_map/ppermute | solution.py:571
  14.5 20.6 %copy-start.9 = (bf16[96,640]{1,0:T(8,128)(2,1)}, bf16[96,640]{1,0:T(8,128)(2,1)S(1)}, u32[]{:S(2)}) copy-start(bf16[96,640]{1,0:T(8,128)(2,1)S(1)} %concatenate.27.refs_0_) | copy-start | bytes 368644
  14.5 8.2 %collective-permute-start = (bf16[96,640]{1,0:T(8,128)(2,1)S(1)}, bf16[96,640]{1,0:T(8,128)(2,1)S(1)}, u32[]{:S(2)}, u32[]{:S(2)}) collective-permute-start(bf16[96,640]{1,0:T(8,128)(2,1)S(1)} %concatenate.27.refs_0_), channel_id=1, source_target_pairs={{0,8},{8,16},{16,24},{24,0},{1,9},{9,17},{17,25},{25,1},{2,10},{10... | collective-permute-start | bytes 368648 | tf_op jit(solution)/shard_map/ppermute | solution.py:576
  16.1 10.1 %collective-permute-start.1 = (bf16[96,640]{1,0:T(8,128)(2,1)S(1)}, bf16[96,640]{1,0:T(8,128)(2,1)S(1)}, u32[]{:S(2)}, u32[]{:S(2)}) collective-permute-start(bf16[96,640]{1,0:T(8,128)(2,1)S(1)} %concatenate.27.refs_0_), channel_id=1, source_target_pairs={{0,16},{8,24},{16,0},{24,8},{1,17},{9,25},{17,1},{25,9},{2,18},{10... | collective-permute-start | bytes 368648 | tf_op jit(solution)/shard_map/ppermute | solution.py:576
  18.7 7.8 %collective-permute-start.2 = (bf16[96,640]{1,0:T(8,128)(2,1)S(1)}, bf16[96,640]{1,0:T(8,128)(2,1)S(1)}, u32[]{:S(2)}, u32[]{:S(2)}) collective-permute-start(bf16[96,640]{1,0:T(8,128)(2,1)S(1)} %concatenate.27.refs_0_), channel_id=1, source_target_pairs={{0,24},{8,0},{16,8},{24,16},{1,25},{9,1},{17,9},{25,17},{2,26},{10... | collective-permute-start | bytes 368648 | tf_op jit(solution)/shard_map/ppermute | solution.py:576
  22.6 12.4 %copy-start.31 = (bf16[96,640]{1,0:T(8,128)(2,1)}, bf16[96,640]{1,0:T(8,128)(2,1)S(1)}, u32[]{:S(2)}) copy-start(bf16[96,640]{1,0:T(8,128)(2,1)S(1)} %collective-permute-done.refs_1_) | copy-start | bytes 368644
  26.5 4.5 %collective-permute-start.15 = (bf16[96,192]{1,0:T(8,128)(2,1)S(1)}, bf16[96,192]{1,0:T(8,128)(2,1)S(1)}, u32[]{:S(2)}, u32[]{:S(2)}) collective-permute-start(bf16[96,192]{1,0:T(8,128)(2,1)S(1)} %bitcast.75), channel_id=1, source_target_pairs={{0,1},{1,0},{2,3},{3,2},{4,5},{5,4},{6,7},{7,6},{8,9},{9,8},{10,11... | collective-permute-start | bytes 110600 | tf_op jit(solution)/shard_map/ppermute | solution.py:571
  27.1 4.4 %collective-permute-start.16 = (bf16[96,192]{1,0:T(8,128)(2,1)S(1)}, bf16[96,192]{1,0:T(8,128)(2,1)S(1)}, u32[]{:S(2)}, u32[]{:S(2)}) collective-permute-start(bf16[96,192]{1,0:T(8,128)(2,1)S(1)} %bitcast.76), channel_id=1, source_target_pairs={{0,2},{1,3},{2,0},{3,1},{4,6},{5,7},{6,4},{7,5},{8,10},{9,11},{10,... | collective-permute-start | bytes 110600 | tf_op jit(solution)/shard_map/ppermute | solution.py:571
  27.5 5.0 %collective-permute-start.17 = (bf16[96,192]{1,0:T(8,128)(2,1)S(1)}, bf16[96,192]{1,0:T(8,128)(2,1)S(1)}, u32[]{:S(2)}, u32[]{:S(2)}) collective-permute-start(bf16[96,192]{1,0:T(8,128)(2,1)S(1)} %bitcast.77), channel_id=1, source_target_pairs={{0,3},{1,2},{2,1},{3,0},{4,7},{5,6},{6,5},{7,4},{8,11},{9,10},{10,... | collective-permute-start | bytes 110600 | tf_op jit(solution)/shard_map/ppermute | solution.py:571
  33.4 186.4 %reduce-scatter.2.cloned.1.call-start = ((), (), s32[]{:S(2)}) async-start(), calls=%async_computation.4 | async-start | bytes 3981312 | tf_op jit(solution)/shard_map/reduce_scatter | solution.py:806
  37.0 6.5 %collective-permute-start.3 = (bf16[4,96,640]{2,1,0:T(8,128)(2,1)}, bf16[4,96,640]{2,1,0:T(8,128)(2,1)S(1)}, u32[]{:S(2)}, u32[]{:S(2)}) collective-permute-start(bf16[4,96,640]{2,1,0:T(8,128)(2,1)} %stack.47.own), channel_id=1, source_target_pairs={{0,4},{4,0},{1,5},{5,1},{2,6},{6,2},{3,7},{7,3},{8,12},{12,8},{9,1... | collective-permute-start | bytes 1474568 | tf_op jit(solution)/shard_map/ppermute | solution.py:567
  37.1 9.4 %collective-permute-start.6 = (bf16[128,768]{1,0:T(8,128)(2,1)S(1)}, bf16[128,768]{1,0:T(8,128)(2,1)S(1)}, u32[]{:S(2)}, u32[]{:S(2)}) collective-permute-start(bf16[128,768]{1,0:T(8,128)(2,1)S(1)} %slice.192), channel_id=1, source_target_pairs={{0,1},{1,0},{2,3},{3,2},{4,5},{5,4},{6,7},{7,6},{8,9},{9,8},{10,11... | collective-permute-start | bytes 589832 | tf_op jit(solution)/shard_map/ppermute | solution.py:571
  38.8 7.7 %collective-permute-start.7 = (bf16[128,768]{1,0:T(8,128)(2,1)S(1)}, bf16[128,768]{1,0:T(8,128)(2,1)S(1)}, u32[]{:S(2)}, u32[]{:S(2)}) collective-permute-start(bf16[128,768]{1,0:T(8,128)(2,1)S(1)} %slice.193), channel_id=1, source_target_pairs={{0,2},{1,3},{2,0},{3,1},{4,6},{5,7},{6,4},{7,5},{8,10},{9,11},{10,... | collective-permute-start | bytes 589832 | tf_op jit(solution)/shard_map/ppermute | solution.py:571
  55.4 3.6 %collective-permute-start.8 = (bf16[1024,384]{1,0:T(8,128)(2,1)}, bf16[1024,384]{1,0:T(8,128)(2,1)S(1)}, u32[]{:S(2)}, u32[]{:S(2)}) collective-permute-start(bf16[1024,384]{1,0:T(8,128)(2,1)} %get-tuple-element.83.own), channel_id=1, source_target_pairs={{0,4},{4,0},{1,5},{5,1},{2,6},{6,2},{3,7},{7,3},{8,12},{12,8},{9,1... | collective-permute-start | bytes 2359304 | tf_op jit(solution)/shard_map/ppermute | solution.py:567
  55.4 15.2 %collective-permute-start.12 = (bf16[256,768]{1,0:T(8,128)(2,1)S(1)}, bf16[256,768]{1,0:T(8,128)(2,1)S(1)}, u32[]{:S(2)}, u32[]{:S(2)}) collective-permute-start(bf16[256,768]{1,0:T(8,128)(2,1)S(1)} %bitcast.66), channel_id=1, source_target_pairs={{0,1},{1,0},{2,3},{3,2},{4,5},{5,4},{6,7},{7,6},{8,9},{9,8},{10,11... | collective-permute-start | bytes 1179656 | tf_op jit(solution)/shard_map/ppermute | solution.py:571
  56.3 28.0 %collective-permute-start.13 = (bf16[256,768]{1,0:T(8,128)(2,1)S(1)}, bf16[256,768]{1,0:T(8,128)(2,1)S(1)}, u32[]{:S(2)}, u32[]{:S(2)}) collective-permute-start(bf16[256,768]{1,0:T(8,128)(2,1)S(1)} %bitcast.67), channel_id=1, source_target_pairs={{0,2},{1,3},{2,0},{3,1},{4,6},{5,7},{6,4},{7,5},{8,10},{9,11},{10,... | collective-permute-start | bytes 1179656 | tf_op jit(solution)/shard_map/ppermute | solution.py:571
  56.8 27.4 %collective-permute-start.14 = (bf16[256,768]{1,0:T(8,128)(2,1)S(1)}, bf16[256,768]{1,0:T(8,128)(2,1)S(1)}, u32[]{:S(2)}, u32[]{:S(2)}) collective-permute-start(bf16[256,768]{1,0:T(8,128)(2,1)S(1)} %bitcast.68), channel_id=1, source_target_pairs={{0,3},{1,2},{2,1},{3,0},{4,7},{5,6},{6,5},{7,4},{8,11},{9,10},{10,... | collective-permute-start | bytes 1179656 | tf_op jit(solution)/shard_map/ppermute | solution.py:571
  68.4 24.3 %collective-permute-start.10 = (bf16[1536,128]{1,0:T(8,128)(2,1)}, bf16[1536,128]{1,0:T(8,128)(2,1)S(1)}, u32[]{:S(2)}, u32[]{:S(2)}) collective-permute-start(bf16[1536,128]{1,0:T(8,128)(2,1)} %get-tuple-element.89.h0), channel_id=1, source_target_pairs={{0,2},{1,3},{2,0},{3,1},{4,6},{5,7},{6,4},{7,5},{8,10},{9,11},{10,... | collective-permute-start | bytes 1179656 | tf_op jit(solution)/shard_map/ppermute | solution.py:571
  69.2 23.5 %collective-permute-start.11 = (bf16[1536,128]{1,0:T(8,128)(2,1)}, bf16[1536,128]{1,0:T(8,128)(2,1)S(1)}, u32[]{:S(2)}, u32[]{:S(2)}) collective-permute-start(bf16[1536,128]{1,0:T(8,128)(2,1)} %get-tuple-element.89.h0), channel_id=1, source_target_pairs={{0,3},{1,2},{2,1},{3,0},{4,7},{5,6},{6,5},{7,4},{8,11},{9,10},{10,... | collective-permute-start | bytes 1179656 | tf_op jit(solution)/shard_map/ppermute | solution.py:571
  70.6 22.1 %collective-permute-start.9 = (bf16[1536,128]{1,0:T(8,128)(2,1)}, bf16[1536,128]{1,0:T(8,128)(2,1)S(1)}, u32[]{:S(2)}, u32[]{:S(2)}) collective-permute-start(bf16[1536,128]{1,0:T(8,128)(2,1)} %get-tuple-element.89.h0), channel_id=1, source_target_pairs={{0,1},{1,0},{2,3},{3,2},{4,5},{5,4},{6,7},{7,6},{8,9},{9,8},{10,11... | collective-permute-start | bytes 1179656 | tf_op jit(solution)/shard_map/ppermute | solution.py:571
  107.2 14.5 %collective-permute-start.18 = (bf16[256,768]{1,0:T(8,128)(2,1)}, bf16[256,768]{1,0:T(8,128)(2,1)S(1)}, u32[]{:S(2)}, u32[]{:S(2)}) collective-permute-start(bf16[256,768]{1,0:T(8,128)(2,1)} %get-tuple-element.102), channel_id=1, source_target_pairs={{0,1},{1,0},{2,3},{3,2},{4,5},{5,4},{6,7},{7,6},{8,9},{9,8},{10,11... | collective-permute-start | bytes 1179656 | tf_op jit(solution)/shard_map/ppermute | solution.py:571
  108.6 13.2 %collective-permute-start.19 = (bf16[256,768]{1,0:T(8,128)(2,1)}, bf16[256,768]{1,0:T(8,128)(2,1)S(1)}, u32[]{:S(2)}, u32[]{:S(2)}) collective-permute-start(bf16[256,768]{1,0:T(8,128)(2,1)} %get-tuple-element.103), channel_id=1, source_target_pairs={{0,2},{1,3},{2,0},{3,1},{4,6},{5,7},{6,4},{7,5},{8,10},{9,11},{10,... | collective-permute-start | bytes 1179656 | tf_op jit(solution)/shard_map/ppermute | solution.py:571
  109.3 18.0 %collective-permute-start.20 = (bf16[256,768]{1,0:T(8,128)(2,1)}, bf16[256,768]{1,0:T(8,128)(2,1)S(1)}, u32[]{:S(2)}, u32[]{:S(2)}) collective-permute-start(bf16[256,768]{1,0:T(8,128)(2,1)} %get-tuple-element.104), channel_id=1, source_target_pairs={{0,3},{1,2},{2,1},{3,0},{4,7},{5,6},{6,5},{7,4},{8,11},{9,10},{10,... | collective-permute-start | bytes 1179656 | tf_op jit(solution)/shard_map/ppermute | solution.py:571
  132.3 6.4 %collective-permute-start.21 = (bf16[384,128]{1,0:T(8,128)(2,1)}, bf16[384,128]{1,0:T(8,128)(2,1)S(1)}, u32[]{:S(2)}, u32[]{:S(2)}) collective-permute-start(bf16[384,128]{1,0:T(8,128)(2,1)} %get-tuple-element.106), channel_id=1, source_target_pairs={{0,1},{1,0},{2,3},{3,2},{4,5},{5,4},{6,7},{7,6},{8,9},{9,8},{10,11... | collective-permute-start | bytes 294920 | tf_op jit(solution)/shard_map/ppermute | solution.py:571
  133.8 4.9 %collective-permute-start.22 = (bf16[384,128]{1,0:T(8,128)(2,1)}, bf16[384,128]{1,0:T(8,128)(2,1)S(1)}, u32[]{:S(2)}, u32[]{:S(2)}) collective-permute-start(bf16[384,128]{1,0:T(8,128)(2,1)} %get-tuple-element.107), channel_id=1, source_target_pairs={{0,2},{1,3},{2,0},{3,1},{4,6},{5,7},{6,4},{7,5},{8,10},{9,11},{10,... | collective-permute-start | bytes 294920 | tf_op jit(solution)/shard_map/ppermute | solution.py:571
  134.7 5.7 %collective-permute-start.23 = (bf16[384,128]{1,0:T(8,128)(2,1)}, bf16[384,128]{1,0:T(8,128)(2,1)S(1)}, u32[]{:S(2)}, u32[]{:S(2)}) collective-permute-start(bf16[384,128]{1,0:T(8,128)(2,1)} %get-tuple-element.108), channel_id=1, source_target_pairs={{0,3},{1,2},{2,1},{3,0},{4,7},{5,6},{6,5},{7,4},{8,11},{9,10},{10,... | collective-permute-start | bytes 294920 | tf_op jit(solution)/shard_map/ppermute | solution.py:571
  154.6 3.6 %collective-permute-start.24 = (bf16[1024,384]{1,0:T(8,128)(2,1)S(1)}, bf16[1024,384]{1,0:T(8,128)(2,1)S(1)}, u32[]{:S(2)}, u32[]{:S(2)}) collective-permute-start(bf16[1024,384]{1,0:T(8,128)(2,1)S(1)} %copy-done.50), channel_id=1, source_target_pairs={{0,4},{4,0},{1,5},{5,1},{2,6},{6,2},{3,7},{7,3},{8,12},{12,8},{9,1... | collective-permute-start | bytes 2359304 | tf_op jit(solution)/shard_map/ppermute | solution.py:567
  154.6 23.7 %all-to-all-start = ((bf16[4,256,768]{2,1,0:T(8,128)(2,1)}), bf16[4,256,768]{2,1,0:T(8,128)(2,1)S(1)}, u32[]{:S(2)}, u32[]{:S(2)}) async-start(bf16[4,256,768]{2,1,0:T(8,128)(2,1)} %fed.1), calls=%async_computation | async-start | bytes 3145728 | tf_op jit(solution)/shard_map/all_to_all | solution.py:788
  169.4 18.5 %collective-permute-start.25 = (bf16[4,96,640]{2,1,0:T(8,128)(2,1)}, bf16[4,96,640]{2,1,0:T(8,128)(2,1)}, u32[]{:S(2)}, u32[]{:S(2)}) collective-permute-start(bf16[4,96,640]{2,1,0:T(8,128)(2,1)} %get-tuple-element.120), channel_id=1, source_target_pairs={{0,4},{4,0},{1,5},{5,1},{2,6},{6,2},{3,7},{7,3},{8,12},{12,8},{9,1... | collective-permute-start | bytes 1474568 | tf_op jit(solution)/shard_map/ppermute | solution.py:567
  183.2 32.3 %all-to-all-start.1 = ((bf16[4,256,768]{2,1,0:T(8,128)(2,1)}), bf16[4,256,768]{2,1,0:T(8,128)(2,1)S(1)}, u32[]{:S(2)}, u32[]{:S(2)}) async-start(bf16[4,256,768]{2,1,0:T(8,128)(2,1)} %spread_grad.1), calls=%async_computation.1 | async-start | bytes 3145728 | tf_op jit(solution)/shard_map/all_to_all | solution.py:837
  190.2 14.4 %copy-start.22 = (f32[96,640]{1,0:T(8,128)S(1)}, f32[96,640]{1,0:T(8,128)}, u32[]{:S(2)}) copy-start(f32[96,640]{1,0:T(8,128)} %get-tuple-element.128) | copy-start | bytes 737284
  190.2 9.6 %collective-permute-start.26 = (bf16[96,640]{1,0:T(8,128)(2,1)}, bf16[96,640]{1,0:T(8,128)(2,1)S(1)}, u32[]{:S(2)}, u32[]{:S(2)}) collective-permute-start(bf16[96,640]{1,0:T(8,128)(2,1)} %get-tuple-element.129), channel_id=1, source_target_pairs={{0,8},{8,16},{16,24},{24,0},{1,9},{9,17},{17,25},{25,1},{2,10},{10... | collective-permute-start | bytes 368648 | tf_op jit(solution)/shard_map/ppermute | solution.py:576
  193.1 11.5 %collective-permute-start.27 = (bf16[96,640]{1,0:T(8,128)(2,1)}, bf16[96,640]{1,0:T(8,128)(2,1)S(1)}, u32[]{:S(2)}, u32[]{:S(2)}) collective-permute-start(bf16[96,640]{1,0:T(8,128)(2,1)} %get-tuple-element.130), channel_id=1, source_target_pairs={{0,16},{8,24},{16,0},{24,8},{1,17},{9,25},{17,1},{25,9},{2,18},{10... | collective-permute-start | bytes 368648 | tf_op jit(solution)/shard_map/ppermute | solution.py:576
  194.7 13.8 %copy-start.23 = (f32[2,96,192]{2,1,0:T(8,128)S(1)}, f32[2,96,192]{2,1,0:T(8,128)}, u32[]{:S(2)}) copy-start(f32[2,96,192]{2,1,0:T(8,128)} %param.37) | copy-start | bytes 442372
  194.7 13.8 %copy-start.24 = (f32[2,96,192]{2,1,0:T(8,128)S(1)}, f32[2,96,192]{2,1,0:T(8,128)}, u32[]{:S(2)}) copy-start(f32[2,96,192]{2,1,0:T(8,128)} %param.38) | copy-start | bytes 442372
  194.7 13.8 %copy-start.25 = (f32[2,96,192]{2,1,0:T(8,128)S(1)}, f32[2,96,192]{2,1,0:T(8,128)}, u32[]{:S(2)}) copy-start(f32[2,96,192]{2,1,0:T(8,128)} %param.39) | copy-start | bytes 442372
  194.7 9.8 %collective-permute-start.28 = (bf16[96,640]{1,0:T(8,128)(2,1)}, bf16[96,640]{1,0:T(8,128)(2,1)S(1)}, u32[]{:S(2)}, u32[]{:S(2)}) collective-permute-start(bf16[96,640]{1,0:T(8,128)(2,1)} %get-tuple-element.125), channel_id=1, source_target_pairs={{0,24},{8,0},{16,8},{24,16},{1,25},{9,1},{17,9},{25,17},{2,26},{10... | collective-permute-start | bytes 368648 | tf_op jit(solution)/shard_map/ppermute | solution.py:576
  204.7 5.5 %collective-permute-start.32 = (f32[2,24]{0,1:T(8,128)S(1)}, f32[2,24]{0,1:T(8,128)S(1)}, u32[]{:S(2)}, u32[]{:S(2)}) collective-permute-start(f32[2,24]{0,1:T(8,128)S(1)} %get-tuple-element.257), channel_id=1, source_target_pairs={{0,1},{1,0},{2,3},{3,2},{4,5},{5,4},{6,7},{7,6},{8,9},{9,8},{10,11... | collective-permute-start | bytes 584 | tf_op jit(solution)/shard_map/ppermute | solution.py:571
  206.6 3.7 %collective-permute-start.33 = (f32[2,24]{0,1:T(8,128)S(1)}, f32[2,24]{0,1:T(8,128)S(1)}, u32[]{:S(2)}, u32[]{:S(2)}) collective-permute-start(f32[2,24]{0,1:T(8,128)S(1)} %get-tuple-element.259), channel_id=1, source_target_pairs={{0,2},{1,3},{2,0},{3,1},{4,6},{5,7},{6,4},{7,5},{8,10},{9,11},{10,... | collective-permute-start | bytes 584 | tf_op jit(solution)/shard_map/ppermute | solution.py:571
  208.1 4.6 %collective-permute-start.34 = (f32[2,24]{0,1:T(8,128)S(1)}, f32[2,24]{0,1:T(8,128)S(1)}, u32[]{:S(2)}, u32[]{:S(2)}) collective-permute-start(f32[2,24]{0,1:T(8,128)S(1)} %get-tuple-element.258), channel_id=1, source_target_pairs={{0,3},{1,2},{2,1},{3,0},{4,7},{5,6},{6,5},{7,4},{8,11},{9,10},{10,... | collective-permute-start | bytes 584 | tf_op jit(solution)/shard_map/ppermute | solution.py:571
  221.2 6.0 %collective-permute-start.29 = (bf16[96,192]{1,0:T(8,128)(2,1)S(1)}, bf16[96,192]{1,0:T(8,128)(2,1)S(1)}, u32[]{:S(2)}, u32[]{:S(2)}) collective-permute-start(bf16[96,192]{1,0:T(8,128)(2,1)S(1)} %pad_maximum_fusion.2), channel_id=1, source_target_pairs={{0,1},{1,0},{2,3},{3,2},{4,5},{5,4},{6,7},{7,6},{8,9},{9,8},{10,11... | collective-permute-start | bytes 110600 | tf_op jit(solution)/shard_map/ppermute | solution.py:571
  221.9 5.4 %collective-permute-start.30 = (bf16[96,192]{1,0:T(8,128)(2,1)S(1)}, bf16[96,192]{1,0:T(8,128)(2,1)S(1)}, u32[]{:S(2)}, u32[]{:S(2)}) collective-permute-start(bf16[96,192]{1,0:T(8,128)(2,1)S(1)} %pad_maximum_fusion.3), channel_id=1, source_target_pairs={{0,2},{1,3},{2,0},{3,1},{4,6},{5,7},{6,4},{7,5},{8,10},{9,11},{10,... | collective-permute-start | bytes 110600 | tf_op jit(solution)/shard_map/ppermute | solution.py:571
  222.3 5.1 %collective-permute-start.31 = (bf16[96,192]{1,0:T(8,128)(2,1)S(1)}, bf16[96,192]{1,0:T(8,128)(2,1)S(1)}, u32[]{:S(2)}, u32[]{:S(2)}) collective-permute-start(bf16[96,192]{1,0:T(8,128)(2,1)S(1)} %pad_maximum_fusion.4), channel_id=1, source_target_pairs={{0,3},{1,2},{2,1},{3,0},{4,7},{5,6},{6,5},{7,4},{8,11},{9,10},{10,... | collective-permute-start | bytes 110600 | tf_op jit(solution)/shard_map/ppermute | solution.py:571
  (42 other events, 193.8 us)
Sparse Core Ops, SparseCore 0:
  33.5 43.2 all-gather.1
  153.7 45.3 reduce-scatter.1

commit v2 on v1

--- a/solution.py
+++ b/solution.py
@@ -2,6 +2,7 @@
 
 import jax
 import jax.numpy as jnp
+import numpy as np
 from jax import lax
 from jax.experimental import pallas as pl
 from jax.experimental.pallas import tpu as pltpu
@@ -28,6 +29,8 @@
 
 F32 = jnp.float32
 BF16 = jnp.bfloat16
+VMEM_LIMIT = {}
+FROM_HBM = ('prepare', 'prepare_rest')
 SMEM = pl.BlockSpec(memory_space=pltpu.SMEM)
 VMEM = pl.BlockSpec(memory_space=pltpu.VMEM)
 
@@ -40,6 +43,8 @@
     scratch_shapes = [pltpu.VMEM(shape, dtype) for shape, dtype in scratch]
     if extra:
         scratch_shapes.append(pltpu.SemaphoreType.DMA(()))
+    if name in FROM_HBM:
+        arrays = [pltpu.with_memory_space_constraint(value, pltpu.HBM) for value in arrays]
     position = len(scalars) + len(arrays)
     return pl.pallas_call(
         body,
@@ -48,7 +53,7 @@
         out_specs=[VMEM] * len(outs) + anywhere,
         scratch_shapes=scratch_shapes,
         input_output_aliases={position: len(outs)} if extra else {},
-        compiler_params=pltpu.CompilerParams(vmem_limit_bytes=60 << 20),
+        compiler_params=pltpu.CompilerParams(vmem_limit_bytes=VMEM_LIMIT.get(name, 8) << 20),
         name=name,
     )(*scalars, *arrays, *extra)
 
@@ -80,6 +85,37 @@
 
 def root_mean(values):
     return lax.rsqrt(jnp.mean(values * values, axis=-1, keepdims=True) + EPSILON)
+
+
+def prepare_body(meta, query, keyvalue, gain, first):
+    rows, width = query.shape
+    first[:, :width] = query[...]
+    gains = jnp.concatenate([gain[...].astype(F32), jnp.zeros((HD - 2, rows), F32)], axis=0)
+    first[:, width : width + HD] = gains.T.astype(BF16)
+    for head in range(HEADS):
+        start = (2 + head) * TILE
+        lanes = slice(head * HD, (head + 1) * HD)
+        first[:, start : start + TILE] = jnp.concatenate(
+            [keyvalue[0, :, lanes], keyvalue[1, :, lanes]], axis=1
+        )
+
+
+def prepare_rest_body(meta, output, gateup, down, turned, rest):
+    turned[...] = output[...].astype(F32).T.astype(BF16)
+    hidden = down.shape[1]
+    rest[:, :hidden] = gateup[0]
+    rest[:, hidden : 2 * hidden] = gateup[1]
+    rest[:, 2 * hidden :] = down[...]
+
+
+def join_body(meta, p0, p1, p2, p3, out):
+    for index, piece in enumerate((p0, p1, p2, p3)):
+        out[:, index * TILE : (index + 1) * TILE] = piece[:, :TILE]
+    for index, pair in enumerate(((p0, p1), (p2, p3))):
+        start = (PARTS + index) * TILE
+        out[:, start : start + TILE] = jnp.concatenate(
+            [pair[0][:, TILE:], pair[1][:, TILE:]], axis=1
+        )
 
 
 def stack_body(meta, *refs):
@@ -95,6 +131,21 @@
     for index in range(count):
         target[rows_at((2 * index + context) * rows, rows, 16), :] = own[index, :, low:high]
         target[rows_at((2 * index + 1 - context) * rows, rows, 16), :] = other[index, :, low:high]
+
+
+def assemble_second_body(meta, wide_own, wide_other, rest_own, rest_other, out):
+    split = wide_own.shape[2]
+    context = meta[1]
+    count, rows, _ = wide_own.shape
+    for pair, lanes in (
+        ((wide_own, wide_other), slice(0, split)),
+        ((rest_own, rest_other), slice(split, out.shape[1])),
+    ):
+        for index in range(count):
+            first = rows_at((2 * index + context) * rows, rows, 16)
+            second = rows_at((2 * index + 1 - context) * rows, rows, 16)
+            out[first, lanes] = pair[0][index]
+            out[second, lanes] = pair[1][index]
 
 
 def assemble_first_body(meta, own, other, weight, gains):
@@ -226,11 +277,11 @@
 
 
 def joined_heads(row, side, heads, target, lower):
-    start = row * 768 + side * 256
+    start = side * 256
     for index in range(PARTS):
         target[:, index * TILE : (index + 1) * TILE] = heads[index][start : start + 256, :]
     for index in range(2):
-        tail = slice(row * 768 + 512, row * 768 + 768)
+        tail = slice(512, 768)
         left = heads[2 * index][tail, :].astype(F32)
         right = heads[2 * index + 1][tail, :].astype(F32)
         if side == 0:
@@ -241,23 +292,34 @@
 
 
 def feed_body(
-    meta, ends, hidden, h0, h1, h2, h3, c0, c1, c2, c3, gains, output, gateup, down,
+    meta, ends, hidden, h0, h1, h2, h3, h4, c0, c1, c2, c3, c4, gains, wide,
     o0, o1, o2, o3, second, active, grads, spread, middle_own, heads_own,
     joined, block_grad, block_middle,
 ):
     part, context = meta[0], meta[1]
-    width = down.shape[1]
+    features = hidden.shape[1]
+    width = active.shape[1]
+    output = wide.at[:, :features]
+    gateup = wide.at[:, features : features + 2 * width]
+    down = wide.at[:, features + 2 * width :]
     gain = gains[1:2, :]
     lower = lanes_of((256, TILE)) < HD
-    for row in range(hidden.shape[0] // 512):
+    row_count = hidden.shape[0] // 512
+    for row in range(row_count):
+        far = row >= row_count // 2
+        shift = row_count // 2 if far else 0
+        heads = [piece.at[row * 768 : row * 768 + 768, :] for piece in (h0, h1, h2)]
+        start = (row - shift) * 768
+        heads.append((h4 if far else h3).at[start : start + 768, :])
         for side in range(2):
             block = 2 * row + side
             rows = slice(block * 256, block * 256 + 256)
-            joined_heads(row, side, (h0, h1, h2, h3), joined, lower)
-            for offset, piece in enumerate((c0, c1, c2, c3)):
+            joined_heads(row, side, heads, joined, lower)
+            for offset, piece in enumerate((c0, c1, c2, c4 if far else c3)):
                 place = jnp.bitwise_xor(part, offset)
                 target = rows_at(block * 256 + place * 64, 64, 64)
-                spread[target, :] = piece[block * 64 : block * 64 + 64, :]
+                source = (block - 2 * shift if offset == 3 else block) * 64
+                spread[target, :] = piece[source : source + 64, :]
             quarter = context if side == 0 else 3 - context
             point = quarter * 256 + lax.broadcasted_iota(jnp.int32, (256, 1), 0)
             keep = point < ends[meta[3] + row, ends.shape[1] - 1]
@@ -286,12 +348,23 @@
                 piece[own, :] = block_grad[rows_at(place * 64, 64, 64), :]
 
 
-def fed_body(meta, active, down, out, block_out):
+def fed_body(meta, active, wide, o0, o1, o2, o3, block_out):
+    part = meta[0]
+    down = wide.at[:, wide.shape[1] - active.shape[1] :]
     for block in range(active.shape[0] // 256):
         rows = slice(block * 256, block * 256 + 256)
         block_out[...] = dot_nt(active[rows, :], down[...]).astype(BF16)
-        for place in range(PARTS):
-            out[place, block * 64 : block * 64 + 64, :] = block_out[place * 64 : place * 64 + 64, :]
+        for offset, piece in enumerate((o0, o1, o2, o3)):
+            place = jnp.bitwise_xor(part, offset)
+            piece[block * 64 : block * 64 + 64, :] = block_out[rows_at(place * 64, 64, 64), :]
+
+
+def give_rows(context, total, tile, outs, lanes):
+    if len(outs) == 2:
+        tile[...] = total
+        split_rows(context, tile, *outs, lanes)
+    else:
+        outs[0][:, lanes] = total.astype(BF16)
 
 
 def split_rows(context, source, keep, send, lanes):
@@ -303,37 +376,23 @@
         ].astype(BF16)
 
 
-def feed_weights_body(meta, *refs):
-    blocks = (len(refs) - 3) // 4
-    second, grads, active, spread = (refs[i * blocks : (i + 1) * blocks] for i in range(4))
-    out, left, right = refs[4 * blocks :]
-    turned = 0
-    for normed, grad in zip(second, spread):
-        for block in range(normed.shape[0] // 256):
-            rows = slice(block * 256, block * 256 + 256)
-            lanes = slice(turned * 256, turned * 256 + 256)
-            left[:, lanes] = normed[rows, :].T
-            right[:, lanes] = grad[rows, :].T
-            turned += 1
-    width = active[0].shape[1]
+def feed_weights_body(meta, second, grads, active, spread, *refs):
+    outs, (left, right, tile) = refs[:-3], refs[-3:]
+    for block in range(second.shape[0] // 256):
+        rows = slice(block * 256, block * 256 + 256)
+        left[:, rows] = second[rows, :].T
+        right[:, rows] = spread[rows, :].T
+    width = active.shape[1]
     for start in range(0, 3 * width, 256):
-        total = None
-        offset = 0
-        for index in range(blocks):
-            size = second[index].shape[0]
-            span = slice(offset, offset + size)
-            if start < 2 * width:
-                value = dot(left[:, span], grads[index][:, start : start + 256])
-            else:
-                first = start - 2 * width
-                value = dot(right[:, span], active[index][:, first : first + 256])
-            total = value if total is None else total + value
-            offset += size
-        out[:, start : start + 256] = total.astype(BF16)
+        if start < 2 * width:
+            total = dot(left[...], grads[:, start : start + 256])
+        else:
+            total = dot(right[...], active[:, start - 2 * width : start - 2 * width + 256])
+        give_rows(meta[1], total, tile, outs, slice(start, start + 256))
 
 
 def middle_body(
-    meta, ends, g0, g1, g2, g3, middle_ref, out_grad_ref, gains, output,
+    meta, ends, g0, g1, g2, g3, middle_ref, out_grad_ref, gains, wide,
     s0, s1, s2, s3, grad_ref, low_ref, gain_ref,
 ):
     part, context = meta[0], meta[1]
@@ -358,7 +417,7 @@
     gain_ref[...] = jnp.broadcast_to(
         jnp.sum(total * middle * scale, axis=0, keepdims=True), gain_ref.shape
     )
-    heads = dot(low, output[...])
+    heads = dot(low, wide[:, : low.shape[1]])
     lower = lanes_of((64, TILE)) < HD
     for offset, piece in enumerate((s0, s1, s2, s3)):
         tail = PARTS + offset // 2
@@ -376,14 +435,12 @@
             piece[row * 192 + 128 : row * 192 + 192, :] = packed.astype(BF16)
 
 
-def output_weights_body(meta, low, heads, grown_in, grown, tile, arrived):
+def output_weights_body(meta, low, heads, *refs):
+    outs, tile = refs[:-1], refs[-1]
     turned = low[...].T
-    width = tile.shape[1]
-    for start in range(0, width, 256):
-        tile[:, start : start + 256] = dot(turned, heads[:, start : start + 256]).astype(BF16)
-    copy = pltpu.make_async_copy(tile, grown.at[:, pl.ds(grown.shape[1] - width, width)], arrived)
-    copy.start()
-    copy.wait()
+    for start in range(0, heads.shape[1], 256):
+        total = dot(turned, heads[:, start : start + 256])
+        give_rows(meta[1], total, tile, outs, slice(start, start + 256))
 
 
 def attend_back_body(
@@ -525,30 +582,107 @@
     out[...] = grad_middle[...] + scale * scaled - values * (scale * scale * scale * inner)
 
 
-def context_sum_body(meta, keep, arrived, *outs):
-    count = len(outs)
+def collect_body(meta, *refs):
+    pieces, first, packed = refs[: -1 - PARTS], refs[-1 - PARTS], refs[-PARTS:]
+    count = len(pieces) // 2
+    total, wide = pieces[0][...].astype(F32), pieces[count][...].astype(F32)
+    for index in range(1, count):
+        total = total + pieces[index][...].astype(F32)
+        wide = wide + pieces[count + index][...].astype(F32)
+    first[...] = total
+    rows, width = total.shape[0], packed[0].shape[1]
+    turned = total[:, TILE : 2 * TILE].T
+    gains = jnp.concatenate([turned[HD : HD + 1, :], turned[HD + 1 : HD + 2, :]], axis=1)
+    high = gains.astype(BF16)
+    low = (gains - high.astype(F32)).astype(BF16)
+    tail = jnp.concatenate([high, low, jnp.zeros((14, 2 * rows), BF16)], axis=0)
+    for offset in range(PARTS):
+        start = offset * TILE
+        rest = PARTS * TILE + offset * HD
+        packed[offset][:rows, :TILE] = wide[:, start : start + TILE].astype(BF16)
+        packed[offset][:rows, TILE:] = wide[:, rest : rest + HD].astype(BF16)
+        packed[offset][rows:, :] = jnp.pad(tail, ((0, 0), (0, width - 2 * rows)))
+
+
+def finish_body(meta, p0, p1, p2, p3, *refs):
+    output_states, gain_states = refs[:3], refs[3:6]
+    output_outs, gain_outs = refs[6:10], refs[10:]
+    total = p0[...].astype(F32) + p1[...].astype(F32) + p2[...].astype(F32) + p3[...].astype(F32)
+    width, rows = output_outs[0].shape
+    values = adam_step(
+        total[:rows, :].T, *[ref[...] for ref in output_states], WEIGHT_DECAY, OUTPUT_RATE
+    )
+    for out, value in zip(output_outs, values):
+        out[...] = value
+    gains = total[rows : rows + 1, :] + total[rows + 1 : rows + 2, :]
+    size = gain_outs[0].shape[1]
+    picked = []
+    for index in range(2):
+        kept = jnp.zeros((1, size), F32)
+        for place in range(PARTS):
+            start = index * rows + place * size
+            kept = jnp.where(meta[0] == place, gains[:, start : start + size], kept)
+        picked.append(kept)
+    values = adam_step(
+        jnp.concatenate(picked, axis=0), *[ref[...] for ref in gain_states], 0.0, GAIN_RATE
+    )
+    for out, value in zip(gain_outs, values):
+        out[...] = value
+
+
+def context_sum_body(meta, *refs):
+    count = refs[0].shape[0]
+    pairs, outs = refs[:-count], refs[-count:]
     for shift, out in enumerate(outs):
         index = lax.rem(meta[2] + shift, count)
-        out[...] = (keep[index] + arrived[index].astype(F32)).astype(out.dtype)
-
-
-def document_ends(lengths, dealing):
-    documents = dealing.shape[-1]
-    picked = (dealing[..., :, None] == jnp.arange(documents, dtype=jnp.int32)).astype(jnp.int32)
-    placed = jnp.sum(picked * lengths[..., None, :documents], axis=-1)
-    return jnp.cumsum(placed, axis=-1)
-
-
-def rotary_tables(ends, context):
-    inverse = ROTARY_BASE ** (-(jnp.arange(HD // 2, dtype=F32) * 2.0 / HD))
-    inverse = jnp.tile(inverse, 4)
-    inner = jnp.arange(256, dtype=jnp.int32)
-    points = jnp.stack([context * 256 + inner, (3 - context) * 256 + inner]).reshape(1, 512)
-    after = points[..., None] >= ends[:, None, :]
-    position = points - jnp.max(jnp.where(after, ends[:, None, :], 0), axis=-1)
-    phase = position.astype(F32).reshape(-1, 1) * inverse
-    sign = jnp.where((jnp.arange(TILE) % HD) < HD // 2, -1.0, 1.0).astype(F32)
-    return jnp.cos(phase), jnp.sin(phase) * sign
+        start = 0
+        for keep, arrived in zip(pairs[::2], pairs[1::2]):
+            width = keep.shape[2]
+            total = keep[index] + arrived[index].astype(F32)
+            out[:, start : start + width] = total.astype(out.dtype)
+            start += width
+
+
+def tables_body(meta, lengths, dealing, inverse, ends, cosine, sine):
+    rows, documents = dealing.shape
+    quarters = (meta[1], 3 - meta[1])
+    for row in range(rows):
+        total = jnp.int32(0)
+        for index in range(documents):
+            total = total + lengths[row, dealing[row, index]]
+            ends[row, index] = total
+    sign = jnp.where((lanes_of((1, TILE)) % HD) < HD // 2, -1.0, 1.0)
+
+    def one(block, carry):
+        row = block // 2
+        quarter = jnp.where(block % 2 == 0, quarters[0], quarters[1])
+        point = quarter * 256 + lax.broadcasted_iota(jnp.int32, (256, 1), 0)
+        begin = jnp.zeros((256, 1), jnp.int32)
+        for index in range(documents):
+            end = ends[row, index]
+            begin = jnp.where(point >= end, end, begin)
+        phase = (point - begin).astype(F32) * inverse[...]
+        target = rows_at(block * 256, 256, 256)
+        cosine[target, :] = jnp.cos(phase)
+        sine[target, :] = jnp.sin(phase) * sign
+        return carry
+
+    lax.fori_loop(0, 2 * rows, one, 0)
+
+
+def rotary_tables(meta, lengths, dealing):
+    inverse = ROTARY_BASE ** (-(np.arange(HD // 2, dtype=np.float64) * 2.0 / HD))
+    inverse = np.tile(inverse, 4).astype(np.float32)[None]
+    rows, documents = dealing.shape
+    table = jax.ShapeDtypeStruct((rows * 512, TILE), F32)
+    return pl.pallas_call(
+        tables_body,
+        out_shape=[jax.ShapeDtypeStruct((rows, documents), jnp.int32), table, table],
+        in_specs=[SMEM, SMEM, SMEM, VMEM],
+        out_specs=[SMEM, VMEM, VMEM],
+        compiler_params=pltpu.CompilerParams(vmem_limit_bytes=4 << 20),
+        name="tables",
+    )(meta, lengths, dealing, jnp.asarray(inverse))
 
 
 def adam_step(gradient, master, moment, variance, decay, rate):
@@ -614,18 +748,15 @@
     return chain.call("stack", stack_body, [(shape, BF16)], (), pieces)[0]
 
 
-def context_sums(chain, keep, arrived):
-    count = lax.axis_size("dp")
-    _, rows, width = keep.shape
+def context_sums(chain, *pairs):
+    count, rows, _ = pairs[0].shape
+    width = sum(value.shape[2] for value in pairs[::2])
     outs = [((rows, width), F32)] + [((rows, width), BF16)] * (count - 1)
-    return chain.call("context_sum", context_sum_body, outs, (), (keep, arrived))
+    return chain.call("context_sum", context_sum_body, outs, (), pairs)
 
 
 def landed_blocks(sums):
-    total = sums[0]
-    for shift in range(1, len(sums)):
-        total = total + shift_dp(sums[shift], shift).astype(F32)
-    return total
+    return [sums[0]] + [shift_dp(sums[shift], shift) for shift in range(1, len(sums))]
 
 
 def per_device(
@@ -667,31 +798,45 @@
     context = lax.axis_index("ctx").astype(jnp.int32)
     own_dp = lax.axis_index("dp").astype(jnp.int32)
     meta = jnp.stack([part, context, own_dp, jnp.int32(0)])
-    ends = document_ends(document_lengths, dealing)
 
     chain = Chain(meta)
     own_rows = row_count * 128
     count = row_count * 512
     own_tokens = tokens.reshape(own_rows, features)
     own_grad = cotangent.reshape(own_rows, features)
-    token_pieces = spread_in_turn(own_tokens)
-
-    keys = [keyvalue_weight[i, :, h * HD : (h + 1) * HD] for h in range(HEADS) for i in range(2)]
-    filler = jnp.zeros((block_rows, HD - 2), BF16)
-    first_block = jnp.concatenate([query_weight, norm_gain.T, filler] + keys, axis=1)
-    by_hand = block_rows % 32 == 0 and block_count <= 8
-    first_pieces = gather_blocks(first_block) if by_hand else []
-    output_pieces = spread_all(after(output_weight.T, token_pieces[1:3], first_pieces))
-    second_block = jnp.concatenate(
-        [piece[:, :TILE] for piece in output_pieces]
-        + [piece[:, TILE:] for piece in output_pieces]
-        + [gateup_weight[0], gateup_weight[1], down_weight.T],
-        axis=1,
-    )
-    cosine, sine = rotary_tables(ends, context)
-    second_full = lax.all_gather(second_block, ("dp", "ctx"), axis=0, tiled=True)
+    by_hand = block_rows % 32 == 0 and block_count == 4
+    half = own_rows // 2
+    first_block = chain.call(
+        "prepare",
+        prepare_body,
+        [((block_rows, QKV), BF16)],
+        (),
+        (query_weight, keyvalue_weight, norm_gain),
+    )[0]
+    turned_output, rest_block = chain.call(
+        "prepare_rest",
+        prepare_rest_body,
+        [(output_weight.shape[::-1], BF16), ((block_rows, 3 * hidden_width), BF16)],
+        (),
+        (output_weight, gateup_weight, down_weight.T),
+    )
+    ends, cosine, sine = rotary_tables(chain.meta, document_lengths, dealing)
+
+    tokens_x, tokens_y = across(own_tokens, 1), across(own_tokens, 2)
     if by_hand:
-        first_own = stack_blocks(chain, first_pieces)
+        first_pieces = [first_block] + [shift_dp(first_block, shift) for shift in (1, 2, 3)]
+    else:
+        first_pieces = [lax.all_gather(first_block, ("dp", "ctx"), axis=0, tiled=True)]
+    done = (tokens_x, tokens_y, first_pieces[1:], cosine)
+
+    tokens_d = [
+        across(after(tokens_y, done)[:half], 1),
+        across(after(tokens_x, done)[half:], 2),
+    ]
+    rest_pieces = [rest_block]
+    if by_hand:
+        rest_pieces.append(shift_dp(after(rest_block, done), 1))
+        first_own = stack_blocks(chain, after(first_pieces, done))
         weight, gains = chain.call(
             "assemble_first",
             assemble_first_body,
@@ -700,32 +845,90 @@
             (first_own, swap_ctx(first_own)),
         )
     else:
-        first_full = lax.all_gather(first_block, ("dp", "ctx"), axis=0, tiled=True)
+        first_full = first_pieces[0]
         gains = jnp.pad(first_full[:, 3 * HD : 3 * HD + 2].T.astype(F32), ((0, 6), (0, 0)))
         lane = jnp.arange(QKV)
         weight = jnp.where((lane >= 3 * HD) & (lane < 4 * HD), 0, first_full).astype(BF16)
+    done = (tokens_d, rest_pieces[1:], weight)
+
+    grads_x = across(after(own_grad, done), 1)
+    grads_y = across(after(own_grad, done), 2)
+    wide_y = across(after(turned_output, done), 2)
+    if by_hand:
+        rest_pieces.append(shift_dp(after(rest_block, done), 2))
     hidden, normed, query, keyval = chain.call(
         "project",
         project_body,
         [((count, features), BF16)] * 2 + [((count, 2 * TILE), BF16), ((count, 3 * TILE), BF16)],
         (),
-        (*token_pieces, gains, weight, cosine, sine),
-    )
-    grad_pieces = spread_all(after(own_grad, token_pieces))
-    keyval_other = swap_ctx(keyval)
+        (
+            own_tokens,
+            tokens_x,
+            tokens_y,
+            *tokens_d,
+            gains,
+            after(weight, done),
+            cosine,
+            sine,
+        ),
+    )
+    done = (grads_x, grads_y, wide_y, rest_pieces[1:])
+    keyval_other = swap_ctx(after(keyval, done))
+    wide_x = across(after(turned_output, keyval, done), 1)
+    wide_d = across(after(turned_output, keyval, done), 3)
+    done = (keyval_other, wide_x, wide_d)
+
+    grads_d = [
+        across(after(grads_y, done)[:half], 1),
+        across(after(grads_x, done)[half:], 2),
+    ]
+    if by_hand:
+        rest_pieces.append(shift_dp(after(rest_block, done), 3))
     key_scratch = [((4, 256, 3 * TILE), BF16), ((4, 3 * TILE, 256), BF16), ((3, 256, 256), F32)]
     mixed, logs = chain.call(
         "attend",
         attend_body,
         [((row_count * 768, TILE), BF16), ((row_count * 2, 8, 256), F32)],
         (ends,),
-        (query, keyval, keyval_other),
+        (after(query, done), keyval, keyval_other),
         key_scratch + [((3, 256, 256), F32)],
     )
-    head_pieces = spread_all(mixed)
-    output = second_full[:, :features]
-    gateup = second_full[:, features : features + 2 * hidden_width]
-    down = second_full[:, features + 2 * hidden_width :]
+    done = (grads_d, rest_pieces[1:])
+
+    heads_x = across(after(mixed, done), 1)
+    heads_y = across(after(mixed, done), 2)
+    wide_block = chain.call(
+        "join",
+        join_body,
+        [((block_rows, features), BF16)],
+        (),
+        (turned_output, wide_x, wide_y, wide_d),
+    )[0]
+    if by_hand:
+        wide_pieces = [wide_block] + [
+            shift_dp(after(wide_block, done), shift) for shift in (1, 2, 3)
+        ]
+        rest_own = stack_blocks(chain, after(rest_pieces, done))
+        done = (heads_x, heads_y, wide_pieces[1:], rest_own)
+        rest_other = swap_ctx(after(rest_own, done))
+        wide_own = stack_blocks(chain, after(wide_pieces, done))
+        second_full = chain.call(
+            "assemble_second",
+            assemble_second_body,
+            [((features, features + 3 * hidden_width), BF16)],
+            (),
+            (wide_own, swap_ctx(wide_own), rest_own, rest_other),
+        )[0]
+    else:
+        done = (heads_x, heads_y)
+        second_full = lax.all_gather(
+            jnp.concatenate([wide_block, rest_block], axis=1), ("dp", "ctx"), axis=0, tiled=True
+        )
+    half_heads = mixed.shape[0] // 2
+    heads_d = [
+        across(after(heads_y, done)[:half_heads], 1),
+        across(after(heads_x, done)[half_heads:], 2),
+    ]
     piece_shape = ((own_rows, features), BF16)
     feed = chain.call(
         "feed",
@@ -740,54 +943,79 @@
             ((own_rows, features), BF16),
         ],
         (ends,),
-        (hidden, *head_pieces, *grad_pieces, gains, output, gateup, down),
+        (
+            hidden,
+            mixed,
+            heads_x,
+            heads_y,
+            *heads_d,
+            own_grad,
+            grads_x,
+            grads_y,
+            *grads_d,
+            gains,
+            second_full,
+        ),
         [((256, features), BF16), ((256, features), BF16), ((256, features), F32)],
     )
+    second, active, feed_grads, spread, middle_own, heads_own = feed[4:]
+
+    def block_outs(width):
+        if by_hand:
+            shape = (block_count, block_rows, width)
+            return [(shape, F32), (shape, BF16)]
+        return [((features, width), BF16)]
+
     second_grads = exchange(feed[:4])
-    second, active, feed_grads, spread, middle_own, heads_own = feed[4:]
-    feed_sum = chain.call(
+    feed_sums = chain.call(
         "feed_weights",
         feed_weights_body,
-        [((features, 3 * hidden_width + features), BF16)],
+        block_outs(3 * hidden_width),
         (),
         (second, feed_grads, active, spread),
-        [((features, count), BF16), ((features, count), BF16)],
-    )[0]
+        [((features, count), BF16), ((features, count), BF16), ((features, 256), F32)],
+    )
+    if by_hand:
+        feed_parts = context_sums(chain, feed_sums[0], swap_ctx(feed_sums[1]))
     fed = chain.call(
         "fed",
         fed_body,
-        [((PARTS, own_rows, features), BF16)],
-        (),
-        (active, down),
+        [piece_shape] * 4,
+        (),
+        (active, second_full),
         [((256, features), BF16)],
-    )[0]
+    )
+    feed_landed = []
+    if by_hand:
+        feed_landed = [feed_parts[0]]
+        feed_landed += [shift_dp(after(feed_parts[k], fed[0]), k) for k in (1, 3)]
+        middle_own = after(middle_own, feed_landed[1:])
     sends = chain.call(
         "middle",
         middle_body,
         [((row_count * 192, TILE), BF16)] * 4
         + [((own_rows, features), F32), ((own_rows, features), BF16), ((8, features), F32)],
         (ends,),
-        (*second_grads, middle_own, own_grad, gains, output),
-    )
-    grad_heads = exchange(sends[:4])
+        (*second_grads, middle_own, own_grad, gains, second_full),
+    )
     grad_middle, grad_low, gain_two = sends[4:]
     grad_heads = exchange(sends[:4])
-    grad_middle, grad_low, gain_two = sends[4:]
-    feed_total = lax.psum_scatter(
-        after(feed_sum, grad_low), ("dp", "ctx"), scatter_dimension=0, tiled=True
-    ).astype(F32)
-    wide_sum = chain.call(
+    output_sums = chain.call(
         "output_weights",
         output_weights_body,
-        [],
+        block_outs(features),
         (),
         (grad_low, heads_own),
-        [((features, features), BF16)],
-        grown=feed_sum,
-    )[0]
-    fed_landed = lax.all_to_all(after(fed, grad_heads), "tensor", 0, 0)
-    block_output = middle_own + fed_landed.astype(F32).sum(axis=0)
-    block_output = block_output.astype(BF16).reshape(tokens.shape)
+        [((features, 256), F32)],
+    )
+    done = (grad_heads,)
+
+    fed_near = [across(after(fed[offset], done), offset) for offset in (1, 2)]
+    if by_hand:
+        feed_landed.append(shift_dp(after(feed_parts[2], done), 2))
+        arrived_output = swap_ctx(after(output_sums[1], done))
+    else:
+        arrived_output = grad_low
     grad_query, grad_own, grad_other = chain.call(
         "attend_back",
         attend_back_body,
@@ -802,12 +1030,18 @@
             ((4, 256, 3 * TILE), F32),
         ],
     )
-    arrived = swap_ctx(grad_other)
-    wide_total = lax.psum_scatter(
-        after(wide_sum, grad_other), ("dp", "ctx"), scatter_dimension=0, tiled=True
-    ).astype(F32)
-    feed_total = wide_total[:, : 3 * hidden_width]
-    output_total = wide_total[:, 3 * hidden_width :]
+    done = (fed_near, arrived_output, feed_landed[3:])
+    arrived = swap_ctx(after(grad_other, done))
+
+    fed_far = across(after(fed[3], arrived), 3)
+    output_landed = []
+    if by_hand:
+        output_parts = context_sums(chain, output_sums[0], after(arrived_output, arrived))
+        output_landed = [output_parts[0]] + [shift_dp(output_parts[k], k) for k in (1, 2, 3)]
+    block_output = middle_own
+    for piece in (fed[0], *fed_near, fed_far):
+        block_output = block_output + piece.astype(F32)
+    block_output = block_output.astype(BF16).reshape(tokens.shape)
     grads = chain.call(
         "first",
         first_body,
@@ -815,32 +1049,47 @@
         (),
         (grad_query, grad_own, arrived, cosine, sine),
     )[0]
-    block_shape = (block_count, block_rows, QKV)
     first_sums = chain.call(
         "first_weights",
         first_weights_body,
-        [(block_shape, F32), (block_shape, BF16)] if by_hand else [((features, QKV), BF16)],
+        block_outs(QKV),
         (),
         (normed, grads, weight, gains, gain_two),
         [((features, QKV), F32), ((features, count), BF16)],
     )
-    if by_hand:
-        arrived_one = swap_ctx(first_sums[1])
     spread_grads = chain.call(
         "spread_grad",
         spread_grad_body,
         [((PARTS, own_rows, features), BF16)],
         (),
-        (grads, after(weight, fed_landed)),
+        (grads, weight),
         [((256, features), BF16)],
     )[0]
-    first_grads = lax.all_to_all(spread_grads, "tensor", 0, 0)
+    done = (fed_far, output_landed[1:])
+    arrived_first = swap_ctx(after(first_sums[1], spread_grads, done)) if by_hand else grads
+    first_grads = lax.all_to_all(after(spread_grads, done), "tensor", 0, 0)
     if by_hand:
-        first_total = landed_blocks(context_sums(chain, first_sums[0], arrived_one))
+        feed_total = feed_landed[0]
+        for piece in feed_landed[1:]:
+            feed_total = feed_total + piece.astype(F32)
+        last_parts = context_sums(chain, first_sums[0], arrived_first)
+        last_landed = [last_parts[0]] + [shift_dp(last_parts[k], k) for k in (1, 2, 3)]
     else:
-        first_total = lax.psum_scatter(
-            first_sums[0], ("dp", "ctx"), scatter_dimension=0, tiled=True
-        ).astype(F32)
+        scatter = functools.partial(
+            lax.psum_scatter, axis_name=("dp", "ctx"), scatter_dimension=0, tiled=True
+        )
+        last_landed = [scatter(first_sums[0])]
+        output_landed = [scatter(output_sums[0])]
+        feed_total = scatter(feed_sums[0]).astype(F32)
+    packed_shape = (block_rows + 16, HEADS * HD)
+    first_total, *packed = chain.call(
+        "collect",
+        collect_body,
+        [((block_rows, QKV), F32)] + [(packed_shape, BF16)] * PARTS,
+        (),
+        (*last_landed, *output_landed),
+    )
+    packed = exchange(packed)
     input_grad = chain.call(
         "input",
         input_body,
@@ -848,26 +1097,21 @@
         (),
         (first_grads, own_tokens, grad_middle, gains),
     )[0].reshape(tokens.shape)
-
-    output_sends = []
-    for offset in range(PARTS):
-        head_lanes = output_total[:, offset * TILE : (offset + 1) * TILE]
-        start = PARTS * TILE + offset * HD
-        output_sends.append(
-            jnp.concatenate([head_lanes, output_total[:, start : start + HD]], axis=1)
-        )
-    output_grad = output_sends[0]
-    for offset in range(1, PARTS):
-        output_grad = output_grad + across(output_sends[offset].astype(BF16), offset).astype(F32)
-    output_grad = output_grad.T
-
-    gain_total = first_total[:, 3 * HD : 3 * HD + 2].T
-    gain_size = block_rows // PARTS
-    gain_grad = lax.dynamic_slice_in_dim(gain_total, part * gain_size, gain_size, 1)
-    for offset in range(1, PARTS):
-        target = jnp.bitwise_xor(part, offset)
-        piece = lax.dynamic_slice_in_dim(gain_total, target * gain_size, gain_size, 1)
-        gain_grad = gain_grad + across(piece, offset)
+    output_results = chain.call(
+        "finish",
+        finish_body,
+        [(output_weight.shape, F32)] * 4 + [(gain_master.shape, F32)] * 4,
+        (),
+        (
+            *packed,
+            output_master,
+            output_moment,
+            output_variance,
+            gain_master,
+            gain_moment,
+            gain_variance,
+        ),
+    )
 
     query_grad = first_total[:, : HEADS * HD]
     key_tiles = [first_total[:, (2 + h) * TILE : (3 + h) * TILE] for h in range(HEADS)]
@@ -895,16 +1139,14 @@
             WEIGHT_DECAY,
             LEARNING_RATE,
         ),
-        *adam_step(
-            output_grad, output_master, output_moment, output_variance, WEIGHT_DECAY, OUTPUT_RATE
-        ),
+        *output_results[:4],
         *adam_step(
             gateup_grad, gateup_master, gateup_moment, gateup_variance, WEIGHT_DECAY, LEARNING_RATE
         ),
         *adam_step(
             down_grad, down_master, down_moment, down_variance, WEIGHT_DECAY, LEARNING_RATE
         ),
-        *adam_step(gain_grad, gain_master, gain_moment, gain_variance, 0.0, GAIN_RATE),
+        *output_results[4:],
     )
 
 

time: 238 us -> 201 us (0.84)
  local copies, waits for them, and re-layouts: 27.7 us -> 3.17 us
  Pallas kernels: 85 us -> 62.1 us
  waiting for transfers between devices: 45.6 us -> 67 us
  between operations: 14.8 us -> 1.4 us
  starting transfers between devices: 51.3 us -> 60.6 us
  other arithmetic: 12.8 us -> 6.53 us
    ppermute x6 -> x18, waiting for transfers between devices: 12.6 us -> 44 us  [shift_dp(): lax.ppermute(value, 'dp', [(i, (i + shift) % size) for i in range(size)])]
    pallas_call x15 -> x25, Pallas kernels: 85 us -> 59.2 us  [call(): pl.pallas_call(body, out_shape=out_shape, in_specs=[SMEM] * len(scalars)...]
    ppermute x6 -> x18, starting transfers between devices: 10.9 us -> 25.3 us  [shift_dp(): lax.ppermute(value, 'dp', [(i, (i + shift) % size) for i in range(size)])]
    unnamed x119 -> x82, local copies, waits for them, and re-layouts: 15.8 us -> 2.96 us
    all_to_all x2 -> x1, waiting for transfers between devices: 7.9 us -> 0.01 us  [per_device(): first_grads = lax.all_to_all(after(spread_grads, done), 'tensor', 0, 0)]
    slice x18 -> x6, local copies, waits for them, and re-layouts: 7.42 us -> 0.09 us  [the longest x1 0.01 us: per_device(): after(tokens_x, done)[half:]]
    all_gather x1 -> x0, waiting for transfers between devices: 4.91 us -> none  [per_device(): lax.all_gather(second_block, ('dp', 'ctx'), axis=0, tiled=True)]
    all_to_all x2 -> x1, starting transfers between devices: 7.13 us -> 3.57 us  [per_device(): first_grads = lax.all_to_all(after(spread_grads, done), 'tensor', 0, 0)]
  transfers between devices with their start and end apart: 39 -> 54, of which waited for: 14 -> 24; matrix products, arithmetic and copies ran while one was open for 11% -> 3% of each run, Pallas kernels for 23% -> 23%
where the time goes in v2:
time: 201 us
  waiting for transfers between devices  67 us (33%)
  Pallas kernels  62.1 us (31%)
  starting transfers between devices  60.6 us (30%)
  other arithmetic  6.53 us (3%)
  local copies, waits for them, and re-layouts  3.17 us (2%)
    pallas_call x25, Pallas kernels, call(): pl.pallas_call(body, out_shape=out_shape, in_specs=[SMEM] * len(scalars)...  59.2 us
    ppermute x18, waiting for transfers between devices, shift_dp(): lax.ppermute(value, 'dp', [(i, (i + shift) % size) for i in range(size)])  44 us
    ppermute x27, starting transfers between devices, across(): lax.ppermute(value, 'tensor', [(i, i ^ offset) for i in range(PARTS)])  30.8 us
    ppermute x18, starting transfers between devices, shift_dp(): lax.ppermute(value, 'dp', [(i, (i + shift) % size) for i in range(size)])  25.3 us
    ppermute x27, waiting for transfers between devices, across(): lax.ppermute(value, 'tensor', [(i, i ^ offset) for i in range(PARTS)])  20.1 us
    sub x4, other arithmetic, adam_step(): return (gradient, master - rate * stepped, moment_new, variance_new)  5.23 us
  transfers between devices with their start and end apart: 54, of which 24 were waited for; matrix products, arithmetic and copies ran while one was open for 3% of the time, Pallas kernels for 23%

profile of v2, /device:TPU:0, one launch (start us, length us, event | category | flops | bytes accessed | tf_op | source)
XLA Modules:
  0.0 200.8 jit_solution(4860216302709716549)
XLA Ops:
  0.7 3.0 %collective-permute-start.4 = (bf16[256,768]{1,0:T(8,128)(2,1)}, bf16[256,768]{1,0:T(8,128)(2,1)S(1)}, u32[]{:S(2)}, u32[]{:S(2)}) collective-permute-start(bf16[256,768]{1,0:T(8,128)(2,1)} %bitcast.23), channel_id=1, source_target_pairs={{0,2},{1,3},{2,0},{3,1},{4,6},{5,7},{6,4},{7,5},{8,10},{9,11},{10,... | collective-permute-start | bytes 1179656 | tf_op jit(solution)/shard_map/ppermute | solution.py:705
  3.7 1.5 collective-permute-start.3
  6.4 3.7 %collective-permute-start.2 = (bf16[96,640]{1,0:T(8,128)(2,1)S(1)}, bf16[96,640]{1,0:T(8,128)(2,1)S(1)}, u32[]{:S(2)}, u32[]{:S(2)}) collective-permute-start(bf16[96,640]{1,0:T(8,128)(2,1)S(1)} %prepare.1.refs_0_), channel_id=1, source_target_pairs={{0,24},{8,0},{16,8},{24,16},{1,25},{9,1},{17,9},{25,17},{2,26},{10... | collective-permute-start | bytes 368648 | tf_op jit(solution)/shard_map/ppermute | solution.py:710
  14.2 2.9 %tables.1 = (s32[2,7]{1,0:T(2,128)S(1)}, f32[1024,128]{1,0:T(8,128)S(1)}, f32[1024,128]{1,0:T(8,128)S(1)}) custom-call(s32[4]{0:T(128)S(1)} %pad_add_fusion.meta, s32[2,8]{1,0:T(2,128)S(1)} %copy-done.22, s32[2,7]{1,0:T(2,128)S(1)} %copy-done.23, f32[1,128]{1,0:T(1,128)S(1)} %copy-done.24), custom_call_target="tpu_custom_call" | custom-call | tf_op jit(solution)/shard_map/tables/pallas_call | solution.py:678
  17.1 3.1 %collective-permute-done.1.refs_2_ = bf16[96,640]{1,0:T(8,128)(2,1)S(1)} collective-permute-done((bf16[96,640]{1,0:T(8,128)(2,1)S(1)}, bf16[96,640]{1,0:T(8,128)(2,1)S(1)}, u32[]{:S(2)}, u32[]{:S(2)}) %collective-permute-start.1) | collective-permute-done | bytes 122912 | tf_op jit(solution)/shard_map/ppermute | solution.py:710
  23.5 5.0 %collective-permute-done.7.x4 = bf16[128,768]{1,0:T(8,128)(2,1)S(1)} collective-permute-done((bf16[128,768]{1,0:T(8,128)(2,1)S(1)}, bf16[128,768]{1,0:T(8,128)(2,1)S(1)}, u32[]{:S(2)}, u32[]{:S(2)}) %collective-permute-start.7) | collective-permute-done | bytes 196640 | tf_op jit(solution)/shard_map/ppermute | solution.py:705
  28.7 3.4 %collective-permute-done.8.refs_1_ = bf16[96,1536]{1,0:T(8,128)(2,1)S(1)} collective-permute-done((bf16[96,1536]{1,0:T(8,128)(2,1)S(1)}, bf16[96,1536]{1,0:T(8,128)(2,1)S(1)}, u32[]{:S(2)}, u32[]{:S(2)}) %collective-permute-start.8) | collective-permute-done | bytes 294944 | tf_op jit(solution)/shard_map/ppermute | solution.py:710
  33.7 1.5 collective-permute-start.11
  35.2 5.1 %project.1 = (bf16[1024,768]{1,0:T(8,128)(2,1)S(1)}, bf16[1024,768]{1,0:T(8,128)(2,1)S(1)}, bf16[1024,256]{1,0:T(8,128)(2,1)S(1)}, bf16[1024,384]{1,0:T(8,128)(2,1)S(1)}) custom-call(s32[4]{0:T(128)S(1)} %pad_add_fusion.meta, bf16[256,768]{1,0:T(8,128)(2,1)S(1)} %bitcast.25, bf16[256,768]{1,0:T(8,128)(2,1)S(1)} %collective-permute-done.3.x1, ...), custom_call_target="tpu_custom_call" | custom-call | tf_op jit(solution)/shard_map/project/pallas_call | solution.py:49
  40.4 3.5 %collective-permute-done.11.p2 = bf16[96,192]{1,0:T(8,128)(2,1)S(1)} collective-permute-done((bf16[96,192]{1,0:T(8,128)(2,1)S(1)}, bf16[96,192]{1,0:T(8,128)(2,1)S(1)}, u32[]{:S(2)}, u32[]{:S(2)}) %collective-permute-start.11) | collective-permute-done | bytes 36896 | tf_op jit(solution)/shard_map/ppermute | solution.py:705
  43.8 3.4 %collective-permute-done.12.refs_2_ = bf16[96,1536]{1,0:T(8,128)(2,1)S(1)} collective-permute-done((bf16[96,1536]{1,0:T(8,128)(2,1)S(1)}, bf16[96,1536]{1,0:T(8,128)(2,1)S(1)}, u32[]{:S(2)}, u32[]{:S(2)}) %collective-permute-start.12) | collective-permute-done | bytes 294944 | tf_op jit(solution)/shard_map/ppermute | solution.py:710
  47.3 1.7 collective-permute-start.15
  49.5 2.8 %collective-permute-done.15.p3 = bf16[96,192]{1,0:T(8,128)(2,1)S(1)} collective-permute-done((bf16[96,192]{1,0:T(8,128)(2,1)S(1)}, bf16[96,192]{1,0:T(8,128)(2,1)S(1)}, u32[]{:S(2)}, u32[]{:S(2)}) %collective-permute-start.15) | collective-permute-done | bytes 36896 | tf_op jit(solution)/shard_map/ppermute | solution.py:705
  53.1 2.4 %collective-permute-start.16 = (bf16[96,1536]{1,0:T(8,128)(2,1)S(1)}, bf16[96,1536]{1,0:T(8,128)(2,1)S(1)}, u32[]{:S(2)}, u32[]{:S(2)}) collective-permute-start(bf16[96,1536]{1,0:T(8,128)(2,1)S(1)} %get-tuple-element.194.refs_0_), channel_id=1, source_target_pairs={{0,24},{8,0},{16,8},{24,16},{1,25},{9,1},{17,9},{25,17},{2,26},{10... | collective-permute-start | bytes 884744 | tf_op jit(solution)/shard_map/ppermute | solution.py:710
  56.1 1.4 collective-permute-start.17
  57.5 6.6 %attend.1 = (bf16[1536,128]{1,0:T(8,128)(2,1)S(1)}, f32[4,8,256]{2,1,0:T(8,128)S(1)}) custom-call(s32[4]{0:T(128)S(1)} %pad_add_fusion.meta, s32[2,7]{1,0:T(2,128)S(1)} %get-tuple-element.179.ends, bf16[1024,256]{1,0:T(8,128)(2,1)S(1)} %get-tuple-element.187.query, bf16[1024,384]{1,0:T(8,128)(2,1)S(1)} %get-tuple-element.185.own, ...), custom_call_target="tpu_custom_call" | custom-call | tf_op jit(solution)/shard_map/attend/pallas_call | solution.py:49
  69.7 3.8 %collective-permute-done.21.refs_3_ = bf16[96,768]{1,0:T(8,128)(2,1)S(1)} collective-permute-done((bf16[96,768]{1,0:T(8,128)(2,1)S(1)}, bf16[96,768]{1,0:T(8,128)(2,1)S(1)}, u32[]{:S(2)}, u32[]{:S(2)}) %collective-permute-start.21) | collective-permute-done | bytes 147488 | tf_op jit(solution)/shard_map/ppermute | solution.py:710
  73.5 6.9 %collective-permute-done.20.refs_2_ = bf16[96,768]{1,0:T(8,128)(2,1)S(1)} collective-permute-done((bf16[96,768]{1,0:T(8,128)(2,1)S(1)}, bf16[96,768]{1,0:T(8,128)(2,1)S(1)}, u32[]{:S(2)}, u32[]{:S(2)}) %collective-permute-start.20) | collective-permute-done | bytes 147488 | tf_op jit(solution)/shard_map/ppermute | solution.py:710
  84.9 3.6 %collective-permute-done.27.h4 = bf16[768,128]{1,0:T(8,128)(2,1)S(1)} collective-permute-done((bf16[768,128]{1,0:T(8,128)(2,1)S(1)}, bf16[768,128]{1,0:T(8,128)(2,1)S(1)}, u32[]{:S(2)}, u32[]{:S(2)}) %collective-permute-start.27) | collective-permute-done | bytes 196640 | tf_op jit(solution)/shard_map/ppermute | solution.py:705
  89.2 8.0 %feed.1 = (bf16[256,768]{1,0:T(8,128)(2,1)S(1)}, bf16[256,768]{1,0:T(8,128)(2,1)S(1)}, bf16[256,768]{1,0:T(8,128)(2,1)S(1)}, bf16[256,768]{1,0:T(8,128)(2,1)S(1)...) custom-call(s32[4]{0:T(128)S(1)} %pad_add_fusion.meta, ...), custom_call_target="tpu_custom_call" | custom-call | tf_op jit(solution)/shard_map/feed/pallas_call | solution.py:49
  97.2 3.6 %feed_weights.1 = (f32[4,96,1536]{2,1,0:T(8,128)S(1)}, bf16[4,96,1536]{2,1,0:T(8,128)(2,1)S(1)}) custom-call(s32[4]{0:T(128)S(1)} %pad_add_fusion.meta, bf16[1024,768]{1,0:T(8,128)(2,1)S(1)} %get-tuple-element.215.second, bf16[1024,1024]{1,0:T(8,128)(2,1)S(1)} %get-tuple-element.216.grads, bf16[1024,512]{1,0:T(8,128)(2,1)S(1)} %get-tuple-element.217.active, ...), custom_call_target="tpu_custom_call" | custom-call | tf_op jit(solution)/shard_map/feed_weights/pallas_call | solution.py:49
  102.6 1.8 collective-permute-start.33
  105.2 1.6 fed.1
  106.9 3.8 %collective-permute-start.30 = (bf16[96,1536]{1,0:T(8,128)(2,1)S(1)}, bf16[96,1536]{1,0:T(8,128)(2,1)S(1)}, u32[]{:S(2)}, u32[]{:S(2)}) collective-permute-start(bf16[96,1536]{1,0:T(8,128)(2,1)S(1)} %get-tuple-element.227), channel_id=1, source_target_pairs={{0,24},{8,0},{16,8},{24,16},{1,25},{9,1},{17,9},{25,17},{2,26},{10... | collective-permute-start | bytes 884744 | tf_op jit(solution)/shard_map/ppermute | solution.py:710
  110.7 7.9 %collective-permute-done.29 = bf16[96,1536]{1,0:T(8,128)(2,1)S(1)} collective-permute-done((bf16[96,1536]{1,0:T(8,128)(2,1)S(1)}, bf16[96,1536]{1,0:T(8,128)(2,1)S(1)}, u32[]{:S(2)}, u32[]{:S(2)}) %collective-permute-start.29) | collective-permute-done | bytes 294944 | tf_op jit(solution)/shard_map/ppermute | solution.py:710
  118.6 3.4 %collective-permute-done.30 = bf16[96,1536]{1,0:T(8,128)(2,1)S(1)} collective-permute-done((bf16[96,1536]{1,0:T(8,128)(2,1)S(1)}, bf16[96,1536]{1,0:T(8,128)(2,1)S(1)}, u32[]{:S(2)}, u32[]{:S(2)}) %collective-permute-start.30) | collective-permute-done | bytes 294944 | tf_op jit(solution)/shard_map/ppermute | solution.py:710
  122.1 1.6 middle.1
  125.4 1.8 collective-permute-start.36
  129.1 2.1 %collective-permute-done.35.g2 = bf16[384,128]{1,0:T(8,128)(2,1)S(1)} collective-permute-done((bf16[384,128]{1,0:T(8,128)(2,1)S(1)}, bf16[384,128]{1,0:T(8,128)(2,1)S(1)}, u32[]{:S(2)}, u32[]{:S(2)}) %collective-permute-start.35) | collective-permute-done | bytes 98336 | tf_op jit(solution)/shard_map/ppermute | solution.py:705
  133.3 2.1 %collective-permute-start.40 = (bf16[96,1536]{1,0:T(8,128)(2,1)S(1)}, bf16[96,1536]{1,0:T(8,128)(2,1)S(1)}, u32[]{:S(2)}, u32[]{:S(2)}) collective-permute-start(bf16[96,1536]{1,0:T(8,128)(2,1)S(1)} %get-tuple-element.251), channel_id=1, source_target_pairs={{0,16},{8,24},{16,0},{24,8},{1,17},{9,25},{17,1},{25,9},{2,18},{10... | collective-permute-start | bytes 884744 | tf_op jit(solution)/shard_map/ppermute | solution.py:710
  135.4 9.4 %attend_back.1 = (bf16[1024,256]{1,0:T(8,128)(2,1)S(1)}, f32[1024,384]{1,0:T(8,128)S(1)}, bf16[1024,384]{1,0:T(8,128)(2,1)S(1)}) custom-call(s32[4]{0:T(128)S(1)} %pad_add_fusion.meta, s32[2,7]{1,0:T(2,128)S(1)} %get-tuple-element.179.ends, bf16[1024,256]{1,0:T(8,128)(2,1)S(1)} %get-tuple-element.187.query, bf16[1024,384]{1,0:T(8,128)(2,1)S(1)} %get-tuple-element.185.own, ...), custom_call_target="tpu_custom_call" | custom-call | tf_op jit(solution)/shard_map/attend_back/pallas_call | solution.py:49
  144.8 4.6 %collective-permute-done.40 = bf16[96,1536]{1,0:T(8,128)(2,1)S(1)} collective-permute-done((bf16[96,1536]{1,0:T(8,128)(2,1)S(1)}, bf16[96,1536]{1,0:T(8,128)(2,1)S(1)}, u32[]{:S(2)}, u32[]{:S(2)}) %collective-permute-start.40) | collective-permute-done | bytes 294944 | tf_op jit(solution)/shard_map/ppermute | solution.py:710
  149.5 2.3 %collective-permute-done.41.arrived = bf16[1024,384]{1,0:T(8,128)(2,1)S(1)} collective-permute-done((bf16[1024,384]{1,0:T(8,128)(2,1)S(1)}, bf16[1024,384]{1,0:T(8,128)(2,1)S(1)}, u32[]{:S(2)}, u32[]{:S(2)}) %collective-permute-start.41) | collective-permute-done | bytes 786464 | tf_op jit(solution)/shard_map/ppermute | solution.py:701
  154.0 2.2 %collective-permute-start.44 = (bf16[96,768]{1,0:T(8,128)(2,1)S(1)}, bf16[96,768]{1,0:T(8,128)(2,1)S(1)}, u32[]{:S(2)}, u32[]{:S(2)}) collective-permute-start(bf16[96,768]{1,0:T(8,128)(2,1)S(1)} %get-tuple-element.268), channel_id=1, source_target_pairs={{0,16},{8,24},{16,0},{24,8},{1,17},{9,25},{17,1},{25,9},{2,18},{10... | collective-permute-start | bytes 442376 | tf_op jit(solution)/shard_map/ppermute | solution.py:710
  156.2 1.6 collective-permute-start.45
  157.8 1.6 first.1.grads
  159.5 3.8 %first_weights.1 = (f32[4,96,640]{2,1,0:T(8,128)S(1)}, bf16[4,96,640]{2,1,0:T(8,128)(2,1)}) custom-call(s32[4]{0:T(128)S(1)} %pad_add_fusion.meta, bf16[1024,768]{1,0:T(8,128)(2,1)S(1)} %get-tuple-element.262.normed, bf16[1024,640]{1,0:T(8,128)(2,1)S(1)} %first.1.grads, bf16[768,640]{1,0:T(8,128)(2,1)S(1)} %get-tuple-element.175.weight, ...), custom_call_target="tpu_custom_call" | custom-call | tf_op jit(solution)/shard_map/first_weights/pallas_call | solution.py:49
  163.3 3.7 %spread_grad.1 = bf16[4,256,768]{2,1,0:T(8,128)(2,1)} custom-call(s32[4]{0:T(128)S(1)} %pad_add_fusion.meta, bf16[1024,640]{1,0:T(8,128)(2,1)S(1)} %first.1.grads, bf16[768,640]{1,0:T(8,128)(2,1)S(1)} %get-tuple-element.175.weight), custom_call_target="tpu_custom_call" | custom-call | tf_op jit(solution)/shard_map/spread_grad/pallas_call | solution.py:49
  169.9 3.6 %all-to-all-start = ((bf16[4,256,768]{2,1,0:T(8,128)(2,1)}), bf16[4,256,768]{2,1,0:T(8,128)(2,1)S(1)}, u32[]{:S(2)}, u32[]{:S(2)}) async-start(bf16[4,256,768]{2,1,0:T(8,128)(2,1)} %spread_grad.1), calls=%async_computation | async-start | bytes 3145728 | tf_op jit(solution)/shard_map/all_to_all | solution.py:1070
  173.6 2.3 %multiply_subtract_fusion.1 = (f32[512,96]{0,1:T(8,128)}, f32[512,96]{0,1:T(8,128)}, f32[512,96]{0,1:T(8,128)}, f32[512,96]{0,1:T(8,128)}) fusion(f32[512,96]{0,1:T(8,128)} %param.50, f32[512,96]{0,1:T(8,128)} %param.51, f32[512,96]{0,1:T(8,128)} %param.52, f32[96,1536]{1,0:T(8,128)} %copy-done.25), kind=kLoop, calls=%fused_computation.15 | loop fusion | flops 737280 | bytes 1572864 | tf_op jit(solution)/shard_map/sub | solution.py:697
  177.1 2.8 %collective-permute-start.47 = (bf16[96,640]{1,0:T(8,128)(2,1)S(1)}, bf16[96,640]{1,0:T(8,128)(2,1)S(1)}, u32[]{:S(2)}, u32[]{:S(2)}) collective-permute-start(bf16[96,640]{1,0:T(8,128)(2,1)S(1)} %get-tuple-element.273), channel_id=1, source_target_pairs={{0,8},{8,16},{16,24},{24,0},{1,9},{9,17},{17,25},{25,1},{2,10},{10... | collective-permute-start | bytes 368648 | tf_op jit(solution)/shard_map/ppermute | solution.py:710
  180.2 2.2 %collective-permute-start.49 = (bf16[96,640]{1,0:T(8,128)(2,1)S(1)}, bf16[96,640]{1,0:T(8,128)(2,1)S(1)}, u32[]{:S(2)}, u32[]{:S(2)}) collective-permute-start(bf16[96,640]{1,0:T(8,128)(2,1)S(1)} %get-tuple-element.270), channel_id=1, source_target_pairs={{0,24},{8,0},{16,8},{24,16},{1,25},{9,1},{17,9},{25,17},{2,26},{10... | collective-permute-start | bytes 368648 | tf_op jit(solution)/shard_map/ppermute | solution.py:710
  183.3 1.8 collective-permute-done.47.refs_1_
  185.1 4.8 %collective-permute-done.48.refs_2_ = bf16[96,640]{1,0:T(8,128)(2,1)S(1)} collective-permute-done((bf16[96,640]{1,0:T(8,128)(2,1)S(1)}, bf16[96,640]{1,0:T(8,128)(2,1)S(1)}, u32[]{:S(2)}, u32[]{:S(2)}) %collective-permute-start.48) | collective-permute-done | bytes 122912 | tf_op jit(solution)/shard_map/ppermute | solution.py:710
  190.8 1.8 collective-permute-start.50
  192.6 1.5 collective-permute-start.51
  196.4 1.9 input.1
  199.1 1.7 finish.1
  (184 shorter events, 42.8 us)
Async XLA Ops:
  0.7 19.5 %collective-permute-start.4 = (bf16[256,768]{1,0:T(8,128)(2,1)}, bf16[256,768]{1,0:T(8,128)(2,1)S(1)}, u32[]{:S(2)}, u32[]{:S(2)}) collective-permute-start(bf16[256,768]{1,0:T(8,128)(2,1)} %bitcast.23), channel_id=1, source_target_pairs={{0,2},{1,3},{2,0},{3,1},{4,6},{5,7},{6,4},{7,5},{8,10},{9,11},{10,... | collective-permute-start | bytes 1179656 | tf_op jit(solution)/shard_map/ppermute | solution.py:705
  3.7 16.5 %collective-permute-start.3 = (bf16[256,768]{1,0:T(8,128)(2,1)}, bf16[256,768]{1,0:T(8,128)(2,1)S(1)}, u32[]{:S(2)}, u32[]{:S(2)}) collective-permute-start(bf16[256,768]{1,0:T(8,128)(2,1)} %bitcast.24), channel_id=1, source_target_pairs={{0,1},{1,0},{2,3},{3,2},{4,5},{5,4},{6,7},{7,6},{8,9},{9,8},{10,11... | collective-permute-start | bytes 1179656 | tf_op jit(solution)/shard_map/ppermute | solution.py:705
  6.4 10.7 %collective-permute-start.2 = (bf16[96,640]{1,0:T(8,128)(2,1)S(1)}, bf16[96,640]{1,0:T(8,128)(2,1)S(1)}, u32[]{:S(2)}, u32[]{:S(2)}) collective-permute-start(bf16[96,640]{1,0:T(8,128)(2,1)S(1)} %prepare.1.refs_0_), channel_id=1, source_target_pairs={{0,24},{8,0},{16,8},{24,16},{1,25},{9,1},{17,9},{25,17},{2,26},{10... | collective-permute-start | bytes 368648 | tf_op jit(solution)/shard_map/ppermute | solution.py:710
  10.0 10.2 %collective-permute-start.1 = (bf16[96,640]{1,0:T(8,128)(2,1)S(1)}, bf16[96,640]{1,0:T(8,128)(2,1)S(1)}, u32[]{:S(2)}, u32[]{:S(2)}) collective-permute-start(bf16[96,640]{1,0:T(8,128)(2,1)S(1)} %prepare.1.refs_0_), channel_id=1, source_target_pairs={{0,16},{8,24},{16,0},{24,8},{1,17},{9,25},{17,1},{25,9},{2,18},{10... | collective-permute-start | bytes 368648 | tf_op jit(solution)/shard_map/ppermute | solution.py:710
  10.0 10.2 %collective-permute-start = (bf16[96,640]{1,0:T(8,128)(2,1)S(1)}, bf16[96,640]{1,0:T(8,128)(2,1)S(1)}, u32[]{:S(2)}, u32[]{:S(2)}) collective-permute-start(bf16[96,640]{1,0:T(8,128)(2,1)S(1)} %prepare.1.refs_0_), channel_id=1, source_target_pairs={{0,8},{8,16},{16,24},{24,0},{1,9},{9,17},{17,25},{25,1},{2,10},{10... | collective-permute-start | bytes 368648 | tf_op jit(solution)/shard_map/ppermute | solution.py:710
  20.9 11.2 %collective-permute-start.8 = (bf16[96,1536]{1,0:T(8,128)(2,1)S(1)}, bf16[96,1536]{1,0:T(8,128)(2,1)S(1)}, u32[]{:S(2)}, u32[]{:S(2)}) collective-permute-start(bf16[96,1536]{1,0:T(8,128)(2,1)S(1)} %get-tuple-element.194.refs_0_), channel_id=1, source_target_pairs={{0,8},{8,16},{16,24},{24,0},{1,9},{9,17},{17,25},{25,1},{2,10},{10... | collective-permute-start | bytes 884744 | tf_op jit(solution)/shard_map/ppermute | solution.py:710
  21.4 7.0 %collective-permute-start.7 = (bf16[128,768]{1,0:T(8,128)(2,1)S(1)}, bf16[128,768]{1,0:T(8,128)(2,1)S(1)}, u32[]{:S(2)}, u32[]{:S(2)}) collective-permute-start(bf16[128,768]{1,0:T(8,128)(2,1)S(1)} %slice.58), channel_id=1, source_target_pairs={{0,2},{1,3},{2,0},{3,1},{4,6},{5,7},{6,4},{7,5},{8,10},{9,11},{10,... | collective-permute-start | bytes 589832 | tf_op jit(solution)/shard_map/ppermute | solution.py:705
  22.0 6.7 %collective-permute-start.6 = (bf16[128,768]{1,0:T(8,128)(2,1)S(1)}, bf16[128,768]{1,0:T(8,128)(2,1)S(1)}, u32[]{:S(2)}, u32[]{:S(2)}) collective-permute-start(bf16[128,768]{1,0:T(8,128)(2,1)S(1)} %slice.57), channel_id=1, source_target_pairs={{0,1},{1,0},{2,3},{3,2},{4,5},{5,4},{6,7},{7,6},{8,9},{9,8},{10,11... | collective-permute-start | bytes 589832 | tf_op jit(solution)/shard_map/ppermute | solution.py:705
  32.1 15.2 %collective-permute-start.10 = (bf16[256,768]{1,0:T(8,128)(2,1)S(1)}, bf16[256,768]{1,0:T(8,128)(2,1)S(1)}, u32[]{:S(2)}, u32[]{:S(2)}) collective-permute-start(bf16[256,768]{1,0:T(8,128)(2,1)S(1)} %bitcast.27), channel_id=1, source_target_pairs={{0,2},{1,3},{2,0},{3,1},{4,6},{5,7},{6,4},{7,5},{8,10},{9,11},{10,... | collective-permute-start | bytes 1179656 | tf_op jit(solution)/shard_map/ppermute | solution.py:705
  32.6 14.7 %collective-permute-start.9 = (bf16[256,768]{1,0:T(8,128)(2,1)S(1)}, bf16[256,768]{1,0:T(8,128)(2,1)S(1)}, u32[]{:S(2)}, u32[]{:S(2)}) collective-permute-start(bf16[256,768]{1,0:T(8,128)(2,1)S(1)} %bitcast.28), channel_id=1, source_target_pairs={{0,1},{1,0},{2,3},{3,2},{4,5},{5,4},{6,7},{7,6},{8,9},{9,8},{10,11... | collective-permute-start | bytes 1179656 | tf_op jit(solution)/shard_map/ppermute | solution.py:705
  33.1 14.1 %collective-permute-start.12 = (bf16[96,1536]{1,0:T(8,128)(2,1)S(1)}, bf16[96,1536]{1,0:T(8,128)(2,1)S(1)}, u32[]{:S(2)}, u32[]{:S(2)}) collective-permute-start(bf16[96,1536]{1,0:T(8,128)(2,1)S(1)} %get-tuple-element.194.refs_0_), channel_id=1, source_target_pairs={{0,16},{8,24},{16,0},{24,8},{1,17},{9,25},{17,1},{25,9},{2,18},{10... | collective-permute-start | bytes 884744 | tf_op jit(solution)/shard_map/ppermute | solution.py:710
  33.7 10.1 %collective-permute-start.11 = (bf16[96,192]{1,0:T(8,128)(2,1)S(1)}, bf16[96,192]{1,0:T(8,128)(2,1)S(1)}, u32[]{:S(2)}, u32[]{:S(2)}) collective-permute-start(bf16[96,192]{1,0:T(8,128)(2,1)S(1)} %get-tuple-element.186.p0), channel_id=1, source_target_pairs={{0,2},{1,3},{2,0},{3,1},{4,6},{5,7},{6,4},{7,5},{8,10},{9,11},{10,... | collective-permute-start | bytes 110600 | tf_op jit(solution)/shard_map/ppermute | solution.py:705
  47.3 5.8 %collective-permute-start.13 = (bf16[1024,384]{1,0:T(8,128)(2,1)S(1)}, bf16[1024,384]{1,0:T(8,128)(2,1)S(1)}, u32[]{:S(2)}, u32[]{:S(2)}) collective-permute-start(bf16[1024,384]{1,0:T(8,128)(2,1)S(1)} %get-tuple-element.185.own), channel_id=1, source_target_pairs={{0,4},{4,0},{1,5},{5,1},{2,6},{6,2},{3,7},{7,3},{8,12},{12,8},{9,1... | collective-permute-start | bytes 2359304 | tf_op jit(solution)/shard_map/ppermute | solution.py:701
  47.3 5.0 %collective-permute-start.15 = (bf16[96,192]{1,0:T(8,128)(2,1)S(1)}, bf16[96,192]{1,0:T(8,128)(2,1)S(1)}, u32[]{:S(2)}, u32[]{:S(2)}) collective-permute-start(bf16[96,192]{1,0:T(8,128)(2,1)S(1)} %get-tuple-element.186.p0), channel_id=1, source_target_pairs={{0,3},{1,2},{2,1},{3,0},{4,7},{5,6},{6,5},{7,4},{8,11},{9,10},{10,... | collective-permute-start | bytes 110600 | tf_op jit(solution)/shard_map/ppermute | solution.py:705
  53.1 11.0 %collective-permute-start.16 = (bf16[96,1536]{1,0:T(8,128)(2,1)S(1)}, bf16[96,1536]{1,0:T(8,128)(2,1)S(1)}, u32[]{:S(2)}, u32[]{:S(2)}) collective-permute-start(bf16[96,1536]{1,0:T(8,128)(2,1)S(1)} %get-tuple-element.194.refs_0_), channel_id=1, source_target_pairs={{0,24},{8,0},{16,8},{24,16},{1,25},{9,1},{17,9},{25,17},{2,26},{10... | collective-permute-start | bytes 884744 | tf_op jit(solution)/shard_map/ppermute | solution.py:710
  55.5 8.6 %collective-permute-start.18 = (bf16[128,768]{1,0:T(8,128)(2,1)S(1)}, bf16[128,768]{1,0:T(8,128)(2,1)S(1)}, u32[]{:S(2)}, u32[]{:S(2)}) collective-permute-start(bf16[128,768]{1,0:T(8,128)(2,1)S(1)} %slice.60), channel_id=1, source_target_pairs={{0,2},{1,3},{2,0},{3,1},{4,6},{5,7},{6,4},{7,5},{8,10},{9,11},{10,... | collective-permute-start | bytes 589832 | tf_op jit(solution)/shard_map/ppermute | solution.py:705
  56.1 8.0 %collective-permute-start.17 = (bf16[128,768]{1,0:T(8,128)(2,1)S(1)}, bf16[128,768]{1,0:T(8,128)(2,1)S(1)}, u32[]{:S(2)}, u32[]{:S(2)}) collective-permute-start(bf16[128,768]{1,0:T(8,128)(2,1)S(1)} %slice.59), channel_id=1, source_target_pairs={{0,1},{1,0},{2,3},{3,2},{4,5},{5,4},{6,7},{7,6},{8,9},{9,8},{10,11... | collective-permute-start | bytes 589832 | tf_op jit(solution)/shard_map/ppermute | solution.py:705
  64.1 16.2 %collective-permute-start.23 = (bf16[1536,128]{1,0:T(8,128)(2,1)S(1)}, bf16[1536,128]{1,0:T(8,128)(2,1)S(1)}, u32[]{:S(2)}, u32[]{:S(2)}) collective-permute-start(bf16[1536,128]{1,0:T(8,128)(2,1)S(1)} %get-tuple-element.201.h0), channel_id=1, source_target_pairs={{0,2},{1,3},{2,0},{3,1},{4,6},{5,7},{6,4},{7,5},{8,10},{9,11},{10,... | collective-permute-start | bytes 1179656 | tf_op jit(solution)/shard_map/ppermute | solution.py:705
  65.3 15.0 %collective-permute-start.22 = (bf16[1536,128]{1,0:T(8,128)(2,1)S(1)}, bf16[1536,128]{1,0:T(8,128)(2,1)S(1)}, u32[]{:S(2)}, u32[]{:S(2)}) collective-permute-start(bf16[1536,128]{1,0:T(8,128)(2,1)S(1)} %get-tuple-element.201.h0), channel_id=1, source_target_pairs={{0,1},{1,0},{2,3},{3,2},{4,5},{5,4},{6,7},{7,6},{8,9},{9,8},{10,11... | collective-permute-start | bytes 1179656 | tf_op jit(solution)/shard_map/ppermute | solution.py:705
  66.9 6.5 %collective-permute-start.21 = (bf16[96,768]{1,0:T(8,128)(2,1)S(1)}, bf16[96,768]{1,0:T(8,128)(2,1)S(1)}, u32[]{:S(2)}, u32[]{:S(2)}) collective-permute-start(bf16[96,768]{1,0:T(8,128)(2,1)S(1)} %join.1.refs_0_), channel_id=1, source_target_pairs={{0,24},{8,0},{16,8},{24,16},{1,25},{9,1},{17,9},{25,17},{2,26},{10... | collective-permute-start | bytes 442376 | tf_op jit(solution)/shard_map/ppermute | solution.py:710
  68.1 12.2 %collective-permute-start.20 = (bf16[96,768]{1,0:T(8,128)(2,1)S(1)}, bf16[96,768]{1,0:T(8,128)(2,1)S(1)}, u32[]{:S(2)}, u32[]{:S(2)}) collective-permute-start(bf16[96,768]{1,0:T(8,128)(2,1)S(1)} %join.1.refs_0_), channel_id=1, source_target_pairs={{0,16},{8,24},{16,0},{24,8},{1,17},{9,25},{17,1},{25,9},{2,18},{10... | collective-permute-start | bytes 442376 | tf_op jit(solution)/shard_map/ppermute | solution.py:710
  68.1 12.2 %collective-permute-start.19 = (bf16[96,768]{1,0:T(8,128)(2,1)S(1)}, bf16[96,768]{1,0:T(8,128)(2,1)S(1)}, u32[]{:S(2)}, u32[]{:S(2)}) collective-permute-start(bf16[96,768]{1,0:T(8,128)(2,1)S(1)} %join.1.refs_0_), channel_id=1, source_target_pairs={{0,8},{8,16},{16,24},{24,0},{1,9},{9,17},{17,25},{25,1},{2,10},{10... | collective-permute-start | bytes 442376 | tf_op jit(solution)/shard_map/ppermute | solution.py:710
  81.6 6.9 %collective-permute-start.27 = (bf16[768,128]{1,0:T(8,128)(2,1)S(1)}, bf16[768,128]{1,0:T(8,128)(2,1)S(1)}, u32[]{:S(2)}, u32[]{:S(2)}) collective-permute-start(bf16[768,128]{1,0:T(8,128)(2,1)S(1)} %slice.62), channel_id=1, source_target_pairs={{0,2},{1,3},{2,0},{3,1},{4,6},{5,7},{6,4},{7,5},{8,10},{9,11},{10,... | collective-permute-start | bytes 589832 | tf_op jit(solution)/shard_map/ppermute | solution.py:705
  82.6 6.5 %collective-permute-start.26 = (bf16[768,128]{1,0:T(8,128)(2,1)S(1)}, bf16[768,128]{1,0:T(8,128)(2,1)S(1)}, u32[]{:S(2)}, u32[]{:S(2)}) collective-permute-start(bf16[768,128]{1,0:T(8,128)(2,1)S(1)} %slice.61), channel_id=1, source_target_pairs={{0,1},{1,0},{2,3},{3,2},{4,5},{5,4},{6,7},{7,6},{8,9},{9,8},{10,11... | collective-permute-start | bytes 589832 | tf_op jit(solution)/shard_map/ppermute | solution.py:705
  100.9 21.2 %collective-permute-start.31 = (bf16[256,768]{1,0:T(8,128)(2,1)S(1)}, bf16[256,768]{1,0:T(8,128)(2,1)S(1)}, u32[]{:S(2)}, u32[]{:S(2)}) collective-permute-start(bf16[256,768]{1,0:T(8,128)(2,1)S(1)} %get-tuple-element.233), channel_id=1, source_target_pairs={{0,1},{1,0},{2,3},{3,2},{4,5},{5,4},{6,7},{7,6},{8,9},{9,8},{10,11... | collective-permute-start | bytes 1179656 | tf_op jit(solution)/shard_map/ppermute | solution.py:705
  102.0 20.0 %collective-permute-start.32 = (bf16[256,768]{1,0:T(8,128)(2,1)S(1)}, bf16[256,768]{1,0:T(8,128)(2,1)S(1)}, u32[]{:S(2)}, u32[]{:S(2)}) collective-permute-start(bf16[256,768]{1,0:T(8,128)(2,1)S(1)} %get-tuple-element.234), channel_id=1, source_target_pairs={{0,2},{1,3},{2,0},{3,1},{4,6},{5,7},{6,4},{7,5},{8,10},{9,11},{10,... | collective-permute-start | bytes 1179656 | tf_op jit(solution)/shard_map/ppermute | solution.py:705
  102.6 19.4 %collective-permute-start.33 = (bf16[256,768]{1,0:T(8,128)(2,1)S(1)}, bf16[256,768]{1,0:T(8,128)(2,1)S(1)}, u32[]{:S(2)}, u32[]{:S(2)}) collective-permute-start(bf16[256,768]{1,0:T(8,128)(2,1)S(1)} %get-tuple-element.235), channel_id=1, source_target_pairs={{0,3},{1,2},{2,1},{3,0},{4,7},{5,6},{6,5},{7,4},{8,11},{9,10},{10,... | collective-permute-start | bytes 1179656 | tf_op jit(solution)/shard_map/ppermute | solution.py:705
  106.8 11.8 %collective-permute-start.29 = (bf16[96,1536]{1,0:T(8,128)(2,1)S(1)}, bf16[96,1536]{1,0:T(8,128)(2,1)S(1)}, u32[]{:S(2)}, u32[]{:S(2)}) collective-permute-start(bf16[96,1536]{1,0:T(8,128)(2,1)S(1)} %get-tuple-element.226), channel_id=1, source_target_pairs={{0,8},{8,16},{16,24},{24,0},{1,9},{9,17},{17,25},{25,1},{2,10},{10... | collective-permute-start | bytes 884744 | tf_op jit(solution)/shard_map/ppermute | solution.py:710
  106.9 15.2 %collective-permute-start.30 = (bf16[96,1536]{1,0:T(8,128)(2,1)S(1)}, bf16[96,1536]{1,0:T(8,128)(2,1)S(1)}, u32[]{:S(2)}, u32[]{:S(2)}) collective-permute-start(bf16[96,1536]{1,0:T(8,128)(2,1)S(1)} %get-tuple-element.227), channel_id=1, source_target_pairs={{0,24},{8,0},{16,8},{24,16},{1,25},{9,1},{17,9},{25,17},{2,26},{10... | collective-permute-start | bytes 884744 | tf_op jit(solution)/shard_map/ppermute | solution.py:710
  123.7 5.4 %collective-permute-start.34 = (bf16[384,128]{1,0:T(8,128)(2,1)S(1)}, bf16[384,128]{1,0:T(8,128)(2,1)S(1)}, u32[]{:S(2)}, u32[]{:S(2)}) collective-permute-start(bf16[384,128]{1,0:T(8,128)(2,1)S(1)} %get-tuple-element.237), channel_id=1, source_target_pairs={{0,1},{1,0},{2,3},{3,2},{4,5},{5,4},{6,7},{7,6},{8,9},{9,8},{10,11... | collective-permute-start | bytes 294920 | tf_op jit(solution)/shard_map/ppermute | solution.py:705
  124.8 6.4 %collective-permute-start.35 = (bf16[384,128]{1,0:T(8,128)(2,1)S(1)}, bf16[384,128]{1,0:T(8,128)(2,1)S(1)}, u32[]{:S(2)}, u32[]{:S(2)}) collective-permute-start(bf16[384,128]{1,0:T(8,128)(2,1)S(1)} %get-tuple-element.238), channel_id=1, source_target_pairs={{0,2},{1,3},{2,0},{3,1},{4,6},{5,7},{6,4},{7,5},{8,10},{9,11},{10,... | collective-permute-start | bytes 294920 | tf_op jit(solution)/shard_map/ppermute | solution.py:705
  125.4 5.7 %collective-permute-start.36 = (bf16[384,128]{1,0:T(8,128)(2,1)S(1)}, bf16[384,128]{1,0:T(8,128)(2,1)S(1)}, u32[]{:S(2)}, u32[]{:S(2)}) collective-permute-start(bf16[384,128]{1,0:T(8,128)(2,1)S(1)} %get-tuple-element.239), channel_id=1, source_target_pairs={{0,3},{1,2},{2,1},{3,0},{4,7},{5,6},{6,5},{7,4},{8,11},{9,10},{10,... | collective-permute-start | bytes 294920 | tf_op jit(solution)/shard_map/ppermute | solution.py:705
  131.1 18.3 %collective-permute-start.39 = (bf16[4,96,768]{2,1,0:T(8,128)(2,1)S(1)}, bf16[4,96,768]{2,1,0:T(8,128)(2,1)S(1)}, u32[]{:S(2)}, u32[]{:S(2)}) collective-permute-start(bf16[4,96,768]{2,1,0:T(8,128)(2,1)S(1)} %get-tuple-element.249), channel_id=1, source_target_pairs={{0,4},{4,0},{1,5},{5,1},{2,6},{6,2},{3,7},{7,3},{8,12},{12,8},{9,1... | collective-permute-start | bytes 1769480 | tf_op jit(solution)/shard_map/ppermute | solution.py:701
  131.1 18.3 %collective-permute-start.37 = (bf16[256,768]{1,0:T(8,128)(2,1)S(1)}, bf16[256,768]{1,0:T(8,128)(2,1)S(1)}, u32[]{:S(2)}, u32[]{:S(2)}) collective-permute-start(bf16[256,768]{1,0:T(8,128)(2,1)S(1)} %get-tuple-element.240), channel_id=1, source_target_pairs={{0,1},{1,0},{2,3},{3,2},{4,5},{5,4},{6,7},{7,6},{8,9},{9,8},{10,11... | collective-permute-start | bytes 1179656 | tf_op jit(solution)/shard_map/ppermute | solution.py:705
  132.3 17.1 %collective-permute-start.38 = (bf16[256,768]{1,0:T(8,128)(2,1)S(1)}, bf16[256,768]{1,0:T(8,128)(2,1)S(1)}, u32[]{:S(2)}, u32[]{:S(2)}) collective-permute-start(bf16[256,768]{1,0:T(8,128)(2,1)S(1)} %get-tuple-element.242), channel_id=1, source_target_pairs={{0,2},{1,3},{2,0},{3,1},{4,6},{5,7},{6,4},{7,5},{8,10},{9,11},{10,... | collective-permute-start | bytes 1179656 | tf_op jit(solution)/shard_map/ppermute | solution.py:705
  133.3 16.1 %collective-permute-start.40 = (bf16[96,1536]{1,0:T(8,128)(2,1)S(1)}, bf16[96,1536]{1,0:T(8,128)(2,1)S(1)}, u32[]{:S(2)}, u32[]{:S(2)}) collective-permute-start(bf16[96,1536]{1,0:T(8,128)(2,1)S(1)} %get-tuple-element.251), channel_id=1, source_target_pairs={{0,16},{8,24},{16,0},{24,8},{1,17},{9,25},{17,1},{25,9},{2,18},{10... | collective-permute-start | bytes 884744 | tf_op jit(solution)/shard_map/ppermute | solution.py:710
  151.8 16.1 %collective-permute-start.42 = (bf16[256,768]{1,0:T(8,128)(2,1)S(1)}, bf16[256,768]{1,0:T(8,128)(2,1)S(1)}, u32[]{:S(2)}, u32[]{:S(2)}) collective-permute-start(bf16[256,768]{1,0:T(8,128)(2,1)S(1)} %get-tuple-element.253), channel_id=1, source_target_pairs={{0,3},{1,2},{2,1},{3,0},{4,7},{5,6},{6,5},{7,4},{8,11},{9,10},{10,... | collective-permute-start | bytes 1179656 | tf_op jit(solution)/shard_map/ppermute | solution.py:705
  153.9 13.2 %collective-permute-start.43 = (bf16[96,768]{1,0:T(8,128)(2,1)S(1)}, bf16[96,768]{1,0:T(8,128)(2,1)S(1)}, u32[]{:S(2)}, u32[]{:S(2)}) collective-permute-start(bf16[96,768]{1,0:T(8,128)(2,1)S(1)} %get-tuple-element.267), channel_id=1, source_target_pairs={{0,8},{8,16},{16,24},{24,0},{1,9},{9,17},{17,25},{25,1},{2,10},{10... | collective-permute-start | bytes 442376 | tf_op jit(solution)/shard_map/ppermute | solution.py:710
  154.0 13.9 %collective-permute-start.44 = (bf16[96,768]{1,0:T(8,128)(2,1)S(1)}, bf16[96,768]{1,0:T(8,128)(2,1)S(1)}, u32[]{:S(2)}, u32[]{:S(2)}) collective-permute-start(bf16[96,768]{1,0:T(8,128)(2,1)S(1)} %get-tuple-element.268), channel_id=1, source_target_pairs={{0,16},{8,24},{16,0},{24,8},{1,17},{9,25},{17,1},{25,9},{2,18},{10... | collective-permute-start | bytes 442376 | tf_op jit(solution)/shard_map/ppermute | solution.py:710
  156.2 11.6 %collective-permute-start.45 = (bf16[96,768]{1,0:T(8,128)(2,1)S(1)}, bf16[96,768]{1,0:T(8,128)(2,1)S(1)}, u32[]{:S(2)}, u32[]{:S(2)}) collective-permute-start(bf16[96,768]{1,0:T(8,128)(2,1)S(1)} %get-tuple-element.257), channel_id=1, source_target_pairs={{0,24},{8,0},{16,8},{24,16},{1,25},{9,1},{17,9},{25,17},{2,26},{10... | collective-permute-start | bytes 442376 | tf_op jit(solution)/shard_map/ppermute | solution.py:710
  168.6 7.2 %collective-permute-start.46 = (bf16[4,96,640]{2,1,0:T(8,128)(2,1)}, bf16[4,96,640]{2,1,0:T(8,128)(2,1)}, u32[]{:S(2)}, u32[]{:S(2)}) collective-permute-start(bf16[4,96,640]{2,1,0:T(8,128)(2,1)} %get-tuple-element.269), channel_id=1, source_target_pairs={{0,4},{4,0},{1,5},{5,1},{2,6},{6,2},{3,7},{7,3},{8,12},{12,8},{9,1... | collective-permute-start | bytes 1474568 | tf_op jit(solution)/shard_map/ppermute | solution.py:701
  169.9 26.4 %all-to-all-start = ((bf16[4,256,768]{2,1,0:T(8,128)(2,1)}), bf16[4,256,768]{2,1,0:T(8,128)(2,1)S(1)}, u32[]{:S(2)}, u32[]{:S(2)}) async-start(bf16[4,256,768]{2,1,0:T(8,128)(2,1)} %spread_grad.1), calls=%async_computation | async-start | bytes 3145728 | tf_op jit(solution)/shard_map/all_to_all | solution.py:1070
  177.1 8.1 %collective-permute-start.47 = (bf16[96,640]{1,0:T(8,128)(2,1)S(1)}, bf16[96,640]{1,0:T(8,128)(2,1)S(1)}, u32[]{:S(2)}, u32[]{:S(2)}) collective-permute-start(bf16[96,640]{1,0:T(8,128)(2,1)S(1)} %get-tuple-element.273), channel_id=1, source_target_pairs={{0,8},{8,16},{16,24},{24,0},{1,9},{9,17},{17,25},{25,1},{2,10},{10... | collective-permute-start | bytes 368648 | tf_op jit(solution)/shard_map/ppermute | solution.py:710
  179.9 10.1 %collective-permute-start.48 = (bf16[96,640]{1,0:T(8,128)(2,1)S(1)}, bf16[96,640]{1,0:T(8,128)(2,1)S(1)}, u32[]{:S(2)}, u32[]{:S(2)}) collective-permute-start(bf16[96,640]{1,0:T(8,128)(2,1)S(1)} %get-tuple-element.274), channel_id=1, source_target_pairs={{0,16},{8,24},{16,0},{24,8},{1,17},{9,25},{17,1},{25,9},{2,18},{10... | collective-permute-start | bytes 368648 | tf_op jit(solution)/shard_map/ppermute | solution.py:710
  180.2 9.8 %collective-permute-start.49 = (bf16[96,640]{1,0:T(8,128)(2,1)S(1)}, bf16[96,640]{1,0:T(8,128)(2,1)S(1)}, u32[]{:S(2)}, u32[]{:S(2)}) collective-permute-start(bf16[96,640]{1,0:T(8,128)(2,1)S(1)} %get-tuple-element.270), channel_id=1, source_target_pairs={{0,24},{8,0},{16,8},{24,16},{1,25},{9,1},{17,9},{25,17},{2,26},{10... | collective-permute-start | bytes 368648 | tf_op jit(solution)/shard_map/ppermute | solution.py:710
  190.8 7.5 %collective-permute-start.50 = (bf16[112,192]{1,0:T(8,128)(2,1)S(1)}, bf16[112,192]{1,0:T(8,128)(2,1)S(1)}, u32[]{:S(2)}, u32[]{:S(2)}) collective-permute-start(bf16[112,192]{1,0:T(8,128)(2,1)S(1)} %get-tuple-element.283), channel_id=1, source_target_pairs={{0,1},{1,0},{2,3},{3,2},{4,5},{5,4},{6,7},{7,6},{8,9},{9,8},{10,11... | collective-permute-start | bytes 129032 | tf_op jit(solution)/shard_map/ppermute | solution.py:705
  192.6 5.7 %collective-permute-start.51 = (bf16[112,192]{1,0:T(8,128)(2,1)S(1)}, bf16[112,192]{1,0:T(8,128)(2,1)S(1)}, u32[]{:S(2)}, u32[]{:S(2)}) collective-permute-start(bf16[112,192]{1,0:T(8,128)(2,1)S(1)} %get-tuple-element.284), channel_id=1, source_target_pairs={{0,2},{1,3},{2,0},{3,1},{4,6},{5,7},{6,4},{7,5},{8,10},{9,11},{10,... | collective-permute-start | bytes 129032 | tf_op jit(solution)/shard_map/ppermute | solution.py:705
  194.0 5.1 %collective-permute-start.52 = (bf16[112,192]{1,0:T(8,128)(2,1)S(1)}, bf16[112,192]{1,0:T(8,128)(2,1)S(1)}, u32[]{:S(2)}, u32[]{:S(2)}) collective-permute-start(bf16[112,192]{1,0:T(8,128)(2,1)S(1)} %get-tuple-element.276), channel_id=1, source_target_pairs={{0,3},{1,2},{2,1},{3,0},{4,7},{5,6},{6,5},{7,4},{8,11},{9,10},{10,... | collective-permute-start | bytes 129032 | tf_op jit(solution)/shard_map/ppermute | solution.py:705
  (47 other events, 429.5 us)

commit v3 on v2

--- a/solution.py
+++ b/solution.py
@@ -30,7 +30,7 @@
 F32 = jnp.float32
 BF16 = jnp.bfloat16
 VMEM_LIMIT = {}
-FROM_HBM = ('prepare', 'prepare_rest')
+FROM_HBM = ('prepare',)
 SMEM = pl.BlockSpec(memory_space=pltpu.SMEM)
 VMEM = pl.BlockSpec(memory_space=pltpu.VMEM)
 
@@ -87,7 +87,17 @@
     return lax.rsqrt(jnp.mean(values * values, axis=-1, keepdims=True) + EPSILON)
 
 
-def prepare_body(meta, query, keyvalue, gain, first):
+def wide_places(rows):
+    places = []
+    for index in range(0, -(-rows // 32)):
+        size = min(32, rows - index * 32)
+        source = slice(index * 32, index * 32 + size)
+        tail = (3 + index // 2) * TILE + (index % 2) * HD
+        places.append((source, size, index * TILE, tail))
+    return places
+
+
+def prepare_body(meta, query, keyvalue, gain, output, tokens, first, payload):
     rows, width = query.shape
     first[:, :width] = query[...]
     gains = jnp.concatenate([gain[...].astype(F32), jnp.zeros((HD - 2, rows), F32)], axis=0)
@@ -98,82 +108,87 @@
         first[:, start : start + TILE] = jnp.concatenate(
             [keyvalue[0, :, lanes], keyvalue[1, :, lanes]], axis=1
         )
-
-
-def prepare_rest_body(meta, output, gateup, down, turned, rest):
-    turned[...] = output[...].astype(F32).T.astype(BF16)
-    hidden = down.shape[1]
-    rest[:, :hidden] = gateup[0]
-    rest[:, hidden : 2 * hidden] = gateup[1]
-    rest[:, 2 * hidden :] = down[...]
-
-
-def join_body(meta, p0, p1, p2, p3, out):
-    for index, piece in enumerate((p0, p1, p2, p3)):
-        out[:, index * TILE : (index + 1) * TILE] = piece[:, :TILE]
-    for index, pair in enumerate(((p0, p1), (p2, p3))):
-        start = (PARTS + index) * TILE
-        out[:, start : start + TILE] = jnp.concatenate(
-            [pair[0][:, TILE:], pair[1][:, TILE:]], axis=1
-        )
+    count = tokens.shape[0]
+    payload[:count, :] = tokens[...]
+    payload[count:, :] = jnp.zeros((32, tokens.shape[1]), BF16)
+    turned = output[...].astype(F32).T.astype(BF16)
+    for source, size, head, tail in wide_places(rows):
+        payload[count : count + size, head : head + TILE] = turned[source, :TILE]
+        payload[count : count + size, tail : tail + HD] = turned[source, TILE:]
+
+
+def join_body(meta, p0, p1, p2, p3, gateup, down, out):
+    rows, hidden = down.shape
+    for source, size, head, tail in wide_places(rows):
+        for index, piece in enumerate((p0, p1, p2, p3)):
+            start = piece.shape[0] - 32
+            lanes = slice(index * TILE, (index + 1) * TILE)
+            out[source, lanes] = piece[start : start + size, head : head + TILE]
+            rest = PARTS * TILE + index * HD
+            out[source, rest : rest + HD] = piece[start : start + size, tail : tail + HD]
+    width = PARTS * (TILE + HD)
+    out[:, width : width + hidden] = gateup[0]
+    out[:, width + hidden : width + 2 * hidden] = gateup[1]
+    out[:, width + 2 * hidden :] = down[...]
 
 
 def stack_body(meta, *refs):
-    pieces, out = refs[:-1], refs[-1]
-    count = len(pieces)
+    count = next(k for k in range(1, len(refs)) if refs[k].ndim == 3)
+    pieces, outs = refs[:count], refs[count:]
+    size = outs[0].shape[0]
     for shift, piece in enumerate(pieces):
-        out[lax.rem(meta[2] + count - shift, count)] = piece[...]
-
-
-def assemble(meta, own, other, target, low, high):
+        index = lax.rem(meta[2] + count - shift, count)
+        for number, out in enumerate(outs):
+            if len(outs) == 1:
+                out[index] = piece[...]
+            else:
+
+                @pl.when(index // size == number)
+                def _(out=out, piece=piece, index=index):
+                    out[lax.rem(index, size)] = piece[...]
+
+
+def assemble(meta, own, other, target, low, high, first=0):
     context = meta[1]
     count, rows, _ = own.shape
     for index in range(count):
-        target[rows_at((2 * index + context) * rows, rows, 16), :] = own[index, :, low:high]
-        target[rows_at((2 * index + 1 - context) * rows, rows, 16), :] = other[index, :, low:high]
-
-
-def assemble_second_body(meta, wide_own, wide_other, rest_own, rest_other, out):
-    split = wide_own.shape[2]
-    context = meta[1]
-    count, rows, _ = wide_own.shape
-    for pair, lanes in (
-        ((wide_own, wide_other), slice(0, split)),
-        ((rest_own, rest_other), slice(split, out.shape[1])),
-    ):
-        for index in range(count):
-            first = rows_at((2 * index + context) * rows, rows, 16)
-            second = rows_at((2 * index + 1 - context) * rows, rows, 16)
-            out[first, lanes] = pair[0][index]
-            out[second, lanes] = pair[1][index]
-
-
-def assemble_first_body(meta, own, other, weight, gains):
-    assemble(meta, own, other, weight, 0, QKV)
+        start = 2 * (first + index)
+        target[rows_at((start + context) * rows, rows, 16), :] = own[index, :, low:high]
+        target[rows_at((start + 1 - context) * rows, rows, 16), :] = other[index, :, low:high]
+
+
+def assemble_second_body(meta, own, other, out):
+    assemble(meta, own, other, out, 0, out.shape[1])
+
+
+def assemble_first_body(meta, *refs):
+    *parts, weight, gains = refs
+    half = len(parts) // 2
+    first = 0
+    for own, other in zip(parts[:half], parts[half:]):
+        assemble(meta, own, other, weight, 0, QKV, first)
+        first += own.shape[0]
     tile = weight[:, TILE : 2 * TILE].astype(F32)
     gains[...] = tile.T[HD : HD + 8, :]
     weight[:, TILE : 2 * TILE] = jnp.where(lanes_of(tile.shape) < HD, tile, 0.0).astype(BF16)
 
 
-def project_body(
-    meta, x0, x1, x2, x3, x4, gains, weight, cosine, sine, hidden, normed, query, keyval
-):
+def project_body(meta, x0, x1, x2, x3, gains, weight, cosine, sine, hidden, normed, query, keyval):
     part = meta[0]
-    blocks = x0.shape[0] // 64
+    blocks = hidden.shape[0] // 256
     gain = gains[0:1, :]
-    pieces = ((x0, 0, 0), (x1, 1, 0), (x2, 2, 0), (x3, 3, 0), (x4, 3, blocks // 2))
-    for piece, offset, start in pieces:
+    for offset, piece in enumerate((x0, x1, x2, x3)):
         place = jnp.bitwise_xor(part, offset)
 
-        def spread(block, carry, piece=piece, place=place, start=start):
+        def spread(block, carry, piece=piece, place=place):
             source = piece[rows_at(block * 64, 64, 64), :]
             values = source.astype(F32)
-            target = rows_at((start + block) * 256 + place * 64, 64, 64)
+            target = rows_at(block * 256 + place * 64, 64, 64)
             hidden[target, :] = source
             normed[target, :] = (values * root_mean(values) * gain).astype(BF16)
             return carry
 
-        lax.fori_loop(0, piece.shape[0] // 64, spread, 0)
+        lax.fori_loop(0, blocks, spread, 0)
 
     def rotate(block, carry):
         rows = rows_at(block * 256, 256, 256)
@@ -292,7 +307,7 @@
 
 
 def feed_body(
-    meta, ends, hidden, h0, h1, h2, h3, h4, c0, c1, c2, c3, c4, gains, wide,
+    meta, ends, hidden, h0, h1, h2, h3, c0, c1, c2, c3, c4, gains, wide,
     o0, o1, o2, o3, second, active, grads, spread, middle_own, heads_own,
     joined, block_grad, block_middle,
 ):
@@ -308,9 +323,7 @@
     for row in range(row_count):
         far = row >= row_count // 2
         shift = row_count // 2 if far else 0
-        heads = [piece.at[row * 768 : row * 768 + 768, :] for piece in (h0, h1, h2)]
-        start = (row - shift) * 768
-        heads.append((h4 if far else h3).at[start : start + 768, :])
+        heads = [piece.at[row * 768 : row * 768 + 768, :] for piece in (h0, h1, h2, h3)]
         for side in range(2):
             block = 2 * row + side
             rows = slice(block * 256, block * 256 + 256)
@@ -539,24 +552,23 @@
     lax.fori_loop(0, grad_query.shape[0] // 256, one, 0)
 
 
-def spread_grad_body(meta, grads, weight, out, block_grad):
-    def one(block, carry):
-        rows = rows_at(block * 256, 256, 256)
-        block_grad[...] = dot_nt(grads[rows, :], weight[...]).astype(BF16)
-        for place in range(PARTS):
-            target = rows_at(block * 64, 64, 64)
-            out[place, target, :] = block_grad[place * 64 : place * 64 + 64, :]
-        return carry
-
-    lax.fori_loop(0, grads.shape[0] // 256, one, 0)
+def spread_grad_body(meta, grads, weight, o0, o1, o2, o3, turned, block_grad):
+    part = meta[0]
+    turned[...] = weight[...].T
+    for block in range(grads.shape[0] // 256):
+        rows = slice(block * 256, block * 256 + 256)
+        block_grad[...] = dot(grads[rows, :], turned[...]).astype(BF16)
+        for offset, piece in enumerate((o0, o1, o2, o3)):
+            place = jnp.bitwise_xor(part, offset)
+            piece[block * 64 : block * 64 + 64, :] = block_grad[rows_at(place * 64, 64, 64), :]
 
 
 def first_weights_body(meta, normed, grads, weight, gains, gain_two, *refs):
     outs, total, turned = refs[:-2], refs[-2], refs[-1]
     turned[...] = normed[...].T
     width = total.shape[1]
-    for start in range(0, width, TILE):
-        lanes = slice(start, start + TILE)
+    for start, size in ((0, 256), (256, 384)):
+        lanes = slice(start, start + size)
         total[:, lanes] = dot(turned[...], grads[:, lanes])
     product = total[...] * weight[...].astype(F32)
     column = jnp.sum(product, axis=1, keepdims=True)
@@ -571,10 +583,10 @@
         outs[0][...] = total[...].astype(BF16)
 
 
-def input_body(meta, landed, tokens, grad_middle, gains, out):
-    total = landed[0].astype(F32)
-    for index in range(1, PARTS):
-        total = total + landed[index].astype(F32)
+def input_body(meta, g0, g1, g2, g3, tokens, grad_middle, gains, out):
+    total = g0[...].astype(F32)
+    for piece in (g1, g2, g3):
+        total = total + piece[...].astype(F32)
     values = tokens[...].astype(F32)
     scale = root_mean(values)
     scaled = gains[0:1, :] * total
@@ -584,11 +596,14 @@
 
 def collect_body(meta, *refs):
     pieces, first, packed = refs[: -1 - PARTS], refs[-1 - PARTS], refs[-PARTS:]
-    count = len(pieces) // 2
-    total, wide = pieces[0][...].astype(F32), pieces[count][...].astype(F32)
-    for index in range(1, count):
-        total = total + pieces[index][...].astype(F32)
-        wide = wide + pieces[count + index][...].astype(F32)
+    total, wide = None, None
+    for piece in pieces:
+        value = piece[...].astype(F32)
+        if value.shape[1] != H * HD:
+            total = value[:, :QKV] if total is None else total + value[:, :QKV]
+            value = value[:, QKV:]
+        if value.shape[1]:
+            wide = value if wide is None else wide + value
     first[...] = total
     rows, width = total.shape[0], packed[0].shape[1]
     turned = total[:, TILE : 2 * TILE].T
@@ -630,14 +645,15 @@
         out[...] = value
 
 
-def context_sum_body(meta, *refs):
-    count = refs[0].shape[0]
-    pairs, outs = refs[:-count], refs[-count:]
-    for shift, out in enumerate(outs):
-        index = lax.rem(meta[2] + shift, count)
+def context_sum_body(offsets, meta, *refs):
+    pairs, outs = refs[: -len(offsets)], refs[-len(offsets) :]
+    for offset, out in zip(offsets, outs):
+        index = lax.rem(meta[2] + offset, pairs[0].shape[0])
         start = 0
         for keep, arrived in zip(pairs[::2], pairs[1::2]):
             width = keep.shape[2]
+            if start + width > out.shape[1]:
+                break
             total = keep[index] + arrived[index].astype(F32)
             out[:, start : start + width] = total.astype(out.dtype)
             start += width
@@ -743,16 +759,20 @@
     return [block] + [shift_dp(block, shift) for shift in range(1, count)]
 
 
-def stack_blocks(chain, pieces):
-    shape = (len(pieces), *pieces[0].shape)
-    return chain.call("stack", stack_body, [(shape, BF16)], (), pieces)[0]
-
-
-def context_sums(chain, *pairs):
-    count, rows, _ = pairs[0].shape
+def stack_blocks(chain, pieces, split=1):
+    shape = (len(pieces) // split, *pieces[0].shape)
+    return chain.call("stack", stack_body, [(shape, BF16)] * split, (), pieces)
+
+
+def context_sums(chain, *pairs, offsets=(0, 1, 2, 3), narrow=()):
+    _, rows, first = pairs[0].shape
     width = sum(value.shape[2] for value in pairs[::2])
-    outs = [((rows, width), F32)] + [((rows, width), BF16)] * (count - 1)
-    return chain.call("context_sum", context_sum_body, outs, (), pairs)
+    outs = []
+    for offset in offsets:
+        size = first if offset in narrow else width
+        outs.append(((rows, size), BF16 if offset else F32))
+    body = functools.partial(context_sum_body, offsets)
+    return chain.call("context_sum", body, outs, (), pairs)
 
 
 def landed_blocks(sums):
@@ -806,84 +826,68 @@
     own_grad = cotangent.reshape(own_rows, features)
     by_hand = block_rows % 32 == 0 and block_count == 4
     half = own_rows // 2
-    first_block = chain.call(
+    first_block, payload = chain.call(
         "prepare",
         prepare_body,
-        [((block_rows, QKV), BF16)],
+        [((block_rows, QKV), BF16), ((own_rows + 32, features), BF16)],
         (),
-        (query_weight, keyvalue_weight, norm_gain),
-    )[0]
-    turned_output, rest_block = chain.call(
-        "prepare_rest",
-        prepare_rest_body,
-        [(output_weight.shape[::-1], BF16), ((block_rows, 3 * hidden_width), BF16)],
-        (),
-        (output_weight, gateup_weight, down_weight.T),
+        (query_weight, keyvalue_weight, norm_gain, output_weight, own_tokens),
     )
     ends, cosine, sine = rotary_tables(chain.meta, document_lengths, dealing)
 
-    tokens_x, tokens_y = across(own_tokens, 1), across(own_tokens, 2)
+    token_pieces = spread_all(payload)
     if by_hand:
         first_pieces = [first_block] + [shift_dp(first_block, shift) for shift in (1, 2, 3)]
-    else:
-        first_pieces = [lax.all_gather(first_block, ("dp", "ctx"), axis=0, tiled=True)]
-    done = (tokens_x, tokens_y, first_pieces[1:], cosine)
-
-    tokens_d = [
-        across(after(tokens_y, done)[:half], 1),
-        across(after(tokens_x, done)[half:], 2),
-    ]
-    rest_pieces = [rest_block]
-    if by_hand:
-        rest_pieces.append(shift_dp(after(rest_block, done), 1))
-        first_own = stack_blocks(chain, after(first_pieces, done))
+        first_own = stack_blocks(chain, after(first_pieces, cosine), 2)
         weight, gains = chain.call(
             "assemble_first",
             assemble_first_body,
             [((features, QKV), BF16), ((8, features), F32)],
             (),
-            (first_own, swap_ctx(first_own)),
+            (*first_own, *[swap_ctx(value) for value in first_own]),
         )
     else:
-        first_full = first_pieces[0]
+        first_full = lax.all_gather(first_block, ("dp", "ctx"), axis=0, tiled=True)
         gains = jnp.pad(first_full[:, 3 * HD : 3 * HD + 2].T.astype(F32), ((0, 6), (0, 0)))
         lane = jnp.arange(QKV)
         weight = jnp.where((lane >= 3 * HD) & (lane < 4 * HD), 0, first_full).astype(BF16)
-    done = (tokens_d, rest_pieces[1:], weight)
+    second_block = chain.call(
+        "join",
+        join_body,
+        [((block_rows, features + 3 * hidden_width), BF16)],
+        (),
+        (*token_pieces, gateup_weight, down_weight.T),
+    )[0]
+    done = (token_pieces[1:], weight)
 
     grads_x = across(after(own_grad, done), 1)
     grads_y = across(after(own_grad, done), 2)
-    wide_y = across(after(turned_output, done), 2)
+    second_pieces = [second_block]
     if by_hand:
-        rest_pieces.append(shift_dp(after(rest_block, done), 2))
+        second_pieces.append(shift_dp(after(second_block, done), 1))
     hidden, normed, query, keyval = chain.call(
         "project",
         project_body,
         [((count, features), BF16)] * 2 + [((count, 2 * TILE), BF16), ((count, 3 * TILE), BF16)],
         (),
         (
-            own_tokens,
-            tokens_x,
-            tokens_y,
-            *tokens_d,
+            *token_pieces,
             gains,
             after(weight, done),
             cosine,
             sine,
         ),
     )
-    done = (grads_x, grads_y, wide_y, rest_pieces[1:])
+    done = (grads_x, grads_y, second_pieces[1:])
     keyval_other = swap_ctx(after(keyval, done))
-    wide_x = across(after(turned_output, keyval, done), 1)
-    wide_d = across(after(turned_output, keyval, done), 3)
-    done = (keyval_other, wide_x, wide_d)
+    done = (keyval_other,)
 
     grads_d = [
         across(after(grads_y, done)[:half], 1),
         across(after(grads_x, done)[half:], 2),
     ]
     if by_hand:
-        rest_pieces.append(shift_dp(after(rest_block, done), 3))
+        second_third = shift_dp(after(second_block, done), 3)
     key_scratch = [((4, 256, 3 * TILE), BF16), ((4, 3 * TILE, 256), BF16), ((3, 256, 256), F32)]
     mixed, logs = chain.call(
         "attend",
@@ -893,42 +897,21 @@
         (after(query, done), keyval, keyval_other),
         key_scratch + [((3, 256, 256), F32)],
     )
-    done = (grads_d, rest_pieces[1:])
-
-    heads_x = across(after(mixed, done), 1)
-    heads_y = across(after(mixed, done), 2)
-    wide_block = chain.call(
-        "join",
-        join_body,
-        [((block_rows, features), BF16)],
-        (),
-        (turned_output, wide_x, wide_y, wide_d),
-    )[0]
+    done = (grads_d, [second_third] if by_hand else [])
+
+    head_pieces = spread_all(after(mixed, done))
     if by_hand:
-        wide_pieces = [wide_block] + [
-            shift_dp(after(wide_block, done), shift) for shift in (1, 2, 3)
-        ]
-        rest_own = stack_blocks(chain, after(rest_pieces, done))
-        done = (heads_x, heads_y, wide_pieces[1:], rest_own)
-        rest_other = swap_ctx(after(rest_own, done))
-        wide_own = stack_blocks(chain, after(wide_pieces, done))
+        second_pieces += [shift_dp(after(second_block, done, mixed), 2), second_third]
+        second_own = stack_blocks(chain, after(second_pieces, head_pieces))[0]
         second_full = chain.call(
             "assemble_second",
             assemble_second_body,
             [((features, features + 3 * hidden_width), BF16)],
             (),
-            (wide_own, swap_ctx(wide_own), rest_own, rest_other),
+            (second_own, swap_ctx(second_own)),
         )[0]
     else:
-        done = (heads_x, heads_y)
-        second_full = lax.all_gather(
-            jnp.concatenate([wide_block, rest_block], axis=1), ("dp", "ctx"), axis=0, tiled=True
-        )
-    half_heads = mixed.shape[0] // 2
-    heads_d = [
-        across(after(heads_y, done)[:half_heads], 1),
-        across(after(heads_x, done)[half_heads:], 2),
-    ]
+        second_full = lax.all_gather(second_block, ("dp", "ctx"), axis=0, tiled=True)
     piece_shape = ((own_rows, features), BF16)
     feed = chain.call(
         "feed",
@@ -945,10 +928,7 @@
         (ends,),
         (
             hidden,
-            mixed,
-            heads_x,
-            heads_y,
-            *heads_d,
+            *head_pieces,
             own_grad,
             grads_x,
             grads_y,
@@ -988,7 +968,7 @@
     feed_landed = []
     if by_hand:
         feed_landed = [feed_parts[0]]
-        feed_landed += [shift_dp(after(feed_parts[k], fed[0]), k) for k in (1, 3)]
+        feed_landed.append(shift_dp(after(feed_parts[2], fed[0]), 2))
         middle_own = after(middle_own, feed_landed[1:])
     sends = chain.call(
         "middle",
@@ -1012,7 +992,7 @@
 
     fed_near = [across(after(fed[offset], done), offset) for offset in (1, 2)]
     if by_hand:
-        feed_landed.append(shift_dp(after(feed_parts[2], done), 2))
+        feed_landed.append(shift_dp(after(feed_parts[1], done), 1))
         arrived_output = swap_ctx(after(output_sums[1], done))
     else:
         arrived_output = grad_low
@@ -1030,18 +1010,14 @@
             ((4, 256, 3 * TILE), F32),
         ],
     )
-    done = (fed_near, arrived_output, feed_landed[3:])
+    done = (fed_near, arrived_output, feed_landed[2:])
     arrived = swap_ctx(after(grad_other, done))
 
     fed_far = across(after(fed[3], arrived), 3)
-    output_landed = []
     if by_hand:
-        output_parts = context_sums(chain, output_sums[0], after(arrived_output, arrived))
-        output_landed = [output_parts[0]] + [shift_dp(output_parts[k], k) for k in (1, 2, 3)]
-    block_output = middle_own
-    for piece in (fed[0], *fed_near, fed_far):
-        block_output = block_output + piece.astype(F32)
-    block_output = block_output.astype(BF16).reshape(tokens.shape)
+        feed_landed.append(shift_dp(after(feed_parts[3], arrived), 3))
+        pair = (output_sums[0], after(arrived_output, arrived))
+        output_far = shift_dp(context_sums(chain, *pair, offsets=(2,))[0], 2)
     grads = chain.call(
         "first",
         first_body,
@@ -1060,50 +1036,58 @@
     spread_grads = chain.call(
         "spread_grad",
         spread_grad_body,
-        [((PARTS, own_rows, features), BF16)],
+        [piece_shape] * PARTS,
         (),
         (grads, weight),
-        [((256, features), BF16)],
-    )[0]
-    done = (fed_far, output_landed[1:])
+        [((QKV, features), BF16), ((256, features), BF16)],
+    )
+    done = (fed_far, feed_landed[3:], [output_far] if by_hand else [])
+    first_grads = exchange(after(spread_grads, done))
     arrived_first = swap_ctx(after(first_sums[1], spread_grads, done)) if by_hand else grads
-    first_grads = lax.all_to_all(after(spread_grads, done), "tensor", 0, 0)
     if by_hand:
-        feed_total = feed_landed[0]
+        last_parts = context_sums(
+            chain, first_sums[0], arrived_first, output_sums[0], arrived_output, narrow=(2,)
+        )
+        feed_total = after(feed_landed[0], last_parts)
         for piece in feed_landed[1:]:
             feed_total = feed_total + piece.astype(F32)
-        last_parts = context_sums(chain, first_sums[0], arrived_first)
-        last_landed = [last_parts[0]] + [shift_dp(last_parts[k], k) for k in (1, 2, 3)]
+        last_landed = [last_parts[0]] + [shift_dp(last_parts[k], k) for k in (2, 1)]
+        last_landed.append(shift_dp(after(last_parts[3], first_grads[1]), 3))
+        last_landed.append(output_far)
     else:
         scatter = functools.partial(
             lax.psum_scatter, axis_name=("dp", "ctx"), scatter_dimension=0, tiled=True
         )
-        last_landed = [scatter(first_sums[0])]
-        output_landed = [scatter(output_sums[0])]
+        last_landed = [scatter(jnp.concatenate([first_sums[0], output_sums[0]], axis=1))]
         feed_total = scatter(feed_sums[0]).astype(F32)
+    input_grad = chain.call(
+        "input",
+        input_body,
+        [((own_rows, features), F32)],
+        (),
+        (*first_grads, own_tokens, grad_middle, gains),
+    )[0].reshape(tokens.shape)
     packed_shape = (block_rows + 16, HEADS * HD)
     first_total, *packed = chain.call(
         "collect",
         collect_body,
         [((block_rows, QKV), F32)] + [(packed_shape, BF16)] * PARTS,
         (),
-        (*last_landed, *output_landed),
-    )
-    packed = exchange(packed)
-    input_grad = chain.call(
-        "input",
-        input_body,
-        [((own_rows, features), F32)],
-        (),
-        (first_grads, own_tokens, grad_middle, gains),
-    )[0].reshape(tokens.shape)
+        last_landed,
+    )
+    landed = exchange(packed)
+    block_output = after(middle_own, last_landed[0])
+    fed_all = (fed[0], *fed_near, fed_far)
+    for piece in fed_all:
+        block_output = block_output + piece.astype(F32)
+    block_output = block_output.astype(BF16).reshape(tokens.shape)
     output_results = chain.call(
         "finish",
         finish_body,
         [(output_weight.shape, F32)] * 4 + [(gain_master.shape, F32)] * 4,
         (),
         (
-            *packed,
+            *landed,
             output_master,
             output_moment,
             output_variance,

time: 201 us -> 194 us (0.965)
  starting transfers between devices: 60.6 us -> 52.1 us
  waiting for transfers between devices: 67 us -> 75.2 us
  Pallas kernels: 62.1 us -> 57.4 us
    ppermute x27 -> x25, waiting for transfers between devices: 20.1 us -> 35.3 us  [across(): lax.ppermute(value, 'tensor', [(i, i ^ offset) for i in range(PARTS)])]
    ppermute x18 -> x13, waiting for transfers between devices: 44 us -> 30.3 us  [shift_dp(): lax.ppermute(value, 'dp', [(i, (i + shift) % size) for i in range(size)])]
    ppermute x8, waiting for transfers between devices: 2.87 us -> 9.59 us  [swap_ctx(): return lax.ppermute(value, 'ctx', [(0, 1), (1, 0)])]
    pallas_call x25 -> x23, Pallas kernels: 59.2 us -> 54.6 us  [call(): pl.pallas_call(body, out_shape=out_shape, in_specs=[SMEM] * len(scalars)...]
    all_to_all x1 -> x0, starting transfers between devices: 3.57 us -> none  [per_device(): first_grads = lax.all_to_all(after(spread_grads, done), 'tensor', 0, 0)]
    ppermute x18 -> x13, starting transfers between devices: 25.3 us -> 22.2 us  [shift_dp(): lax.ppermute(value, 'dp', [(i, (i + shift) % size) for i in range(size)])]
    ppermute x27 -> x25, starting transfers between devices: 30.8 us -> 29 us  [across(): lax.ppermute(value, 'tensor', [(i, i ^ offset) for i in range(PARTS)])]
  transfers between devices with their start and end apart: 54 -> 46, of which waited for: 24 -> 24; matrix products, arithmetic and copies ran while one was open for 3% -> 3% of each run, Pallas kernels for 23% -> 20%
where the time goes in v3:
time: 194 us
  waiting for transfers between devices  75.2 us (39%)
  Pallas kernels  57.4 us (30%)
  starting transfers between devices  52.1 us (27%)
  other arithmetic  5.18 us (3%)
  local copies, waits for them, and re-layouts  2.37 us (1%)
    pallas_call x23, Pallas kernels, call(): pl.pallas_call(body, out_shape=out_shape, in_specs=[SMEM] * len(scalars)...  54.6 us
    ppermute x25, waiting for transfers between devices, across(): lax.ppermute(value, 'tensor', [(i, i ^ offset) for i in range(PARTS)])  35.3 us
    ppermute x13, waiting for transfers between devices, shift_dp(): lax.ppermute(value, 'dp', [(i, (i + shift) % size) for i in range(size)])  30.3 us
    ppermute x25, starting transfers between devices, across(): lax.ppermute(value, 'tensor', [(i, i ^ offset) for i in range(PARTS)])  29 us
    ppermute x13, starting transfers between devices, shift_dp(): lax.ppermute(value, 'dp', [(i, (i + shift) % size) for i in range(size)])  22.2 us
    ppermute x8, waiting for transfers between devices, swap_ctx(): return lax.ppermute(value, 'ctx', [(0, 1), (1, 0)])  9.59 us
  transfers between devices with their start and end apart: 46, of which 24 were waited for; matrix products, arithmetic and copies ran while one was open for 3% of the time, Pallas kernels for 20%

profile of v3, /device:TPU:0, one launch (start us, length us, event | category | flops | bytes accessed | tf_op | source)
XLA Modules:
  0.0 193.5 jit_solution(12690003888088421293)
XLA Ops:
  0.8 1.5 prepare.1
  2.2 5.1 %collective-permute-start.2 = (bf16[96,640]{1,0:T(8,128)(2,1)S(1)}, bf16[96,640]{1,0:T(8,128)(2,1)S(1)}, u32[]{:S(2)}, u32[]{:S(2)}) collective-permute-start(bf16[96,640]{1,0:T(8,128)(2,1)S(1)} %get-tuple-element.158.refs_0_), channel_id=1, source_target_pairs={{0,24},{8,0},{16,8},{24,16},{1,25},{9,1},{17,9},{25,17},{2,26},{10... | collective-permute-start | bytes 368648 | tf_op jit(solution)/shard_map/ppermute | solution.py:726
  7.3 2.4 %collective-permute-start.7 = (bf16[288,768]{1,0:T(8,128)(2,1)S(1)}, bf16[288,768]{1,0:T(8,128)(2,1)S(1)}, u32[]{:S(2)}, u32[]{:S(2)}) collective-permute-start(bf16[288,768]{1,0:T(8,128)(2,1)S(1)} %get-tuple-element.154.p0.x0), channel_id=1, source_target_pairs={{0,3},{1,2},{2,1},{3,0},{4,7},{5,6},{6,5},{7,4},{8,11},{9,10},{10,... | collective-permute-start | bytes 1327112 | tf_op jit(solution)/shard_map/ppermute | solution.py:721
  13.9 2.9 %tables.1 = (s32[2,7]{1,0:T(2,128)S(1)}, f32[1024,128]{1,0:T(8,128)S(1)}, f32[1024,128]{1,0:T(8,128)S(1)}) custom-call(s32[4]{0:T(128)S(1)} %pad_add_fusion.meta, s32[2,8]{1,0:T(2,128)S(1)} %copy-done.10, s32[2,7]{1,0:T(2,128)S(1)} %copy-done.11, f32[1,128]{1,0:T(1,128)S(1)} %copy-done.12), custom_call_target="tpu_custom_call" | custom-call | tf_op jit(solution)/shard_map/tables/pallas_call | solution.py:694
  16.8 2.6 %collective-permute-done.1.refs_2_ = bf16[96,640]{1,0:T(8,128)(2,1)S(1)} collective-permute-done((bf16[96,640]{1,0:T(8,128)(2,1)S(1)}, bf16[96,640]{1,0:T(8,128)(2,1)S(1)}, u32[]{:S(2)}, u32[]{:S(2)}) %collective-permute-start.1) | collective-permute-done | bytes 122912 | tf_op jit(solution)/shard_map/ppermute | solution.py:726
  22.7 6.6 %collective-permute-done.6.p2.x2 = bf16[288,768]{1,0:T(8,128)(2,1)S(1)} collective-permute-done((bf16[288,768]{1,0:T(8,128)(2,1)S(1)}, bf16[288,768]{1,0:T(8,128)(2,1)S(1)}, u32[]{:S(2)}, u32[]{:S(2)}) %collective-permute-start.6) | collective-permute-done | bytes 442400 | tf_op jit(solution)/shard_map/ppermute | solution.py:721
  30.2 1.5 collective-permute-start.9
  32.4 5.1 %project.1 = (bf16[1024,768]{1,0:T(8,128)(2,1)S(1)}, bf16[1024,768]{1,0:T(8,128)(2,1)S(1)}, bf16[1024,256]{1,0:T(8,128)(2,1)S(1)}, bf16[1024,384]{1,0:T(8,128)(2,1)S(1)}) custom-call(s32[4]{0:T(128)S(1)} %pad_add_fusion.meta, bf16[288,768]{1,0:T(8,128)(2,1)S(1)} %get-tuple-element.154.p0.x0, bf16[288,768]{1,0:T(8,128)(2,1)S(1)} %collective-permute-done.5.p1.x1, ...), custom_call_target="tpu_custom_call" | custom-call | tf_op jit(solution)/shard_map/project/pallas_call | solution.py:49
  37.6 3.6 %collective-permute-done.9.c2 = bf16[256,768]{1,0:T(8,128)(2,1)S(1)} collective-permute-done((bf16[256,768]{1,0:T(8,128)(2,1)S(1)}, bf16[256,768]{1,0:T(8,128)(2,1)S(1)}, u32[]{:S(2)}, u32[]{:S(2)}) %collective-permute-start.9) | collective-permute-done | bytes 393248 | tf_op jit(solution)/shard_map/ppermute | solution.py:721
  42.4 1.5 collective-permute-done.10.refs_1_
  43.9 2.3 %collective-permute-done.11.other = bf16[1024,384]{1,0:T(8,128)(2,1)S(1)} collective-permute-done((bf16[1024,384]{1,0:T(8,128)(2,1)S(1)}, bf16[1024,384]{1,0:T(8,128)(2,1)S(1)}, u32[]{:S(2)}, u32[]{:S(2)}) %collective-permute-start.11) | collective-permute-done | bytes 786464 | tf_op jit(solution)/shard_map/ppermute | solution.py:717
  46.2 1.9 %collective-permute-start.14 = (bf16[96,2304]{1,0:T(8,128)(2,1)S(1)}, bf16[96,2304]{1,0:T(8,128)(2,1)S(1)}, u32[]{:S(2)}, u32[]{:S(2)}) collective-permute-start(bf16[96,2304]{1,0:T(8,128)(2,1)S(1)} %join.1.refs_0_), channel_id=1, source_target_pairs={{0,24},{8,0},{16,8},{24,16},{1,25},{9,1},{17,9},{25,17},{2,26},{10... | collective-permute-start | bytes 1327112 | tf_op jit(solution)/shard_map/ppermute | solution.py:726
  48.8 1.5 collective-permute-start.12
  50.3 6.7 %attend.1 = (bf16[1536,128]{1,0:T(8,128)(2,1)S(1)}, f32[4,8,256]{2,1,0:T(8,128)S(1)}) custom-call(s32[4]{0:T(128)S(1)} %pad_add_fusion.meta, s32[2,7]{1,0:T(2,128)S(1)} %get-tuple-element.173.ends, bf16[1024,256]{1,0:T(8,128)(2,1)S(1)} %get-tuple-element.178.query, bf16[1024,384]{1,0:T(8,128)(2,1)S(1)} %get-tuple-element.177.own, ...), custom_call_target="tpu_custom_call" | custom-call | tf_op jit(solution)/shard_map/attend/pallas_call | solution.py:49
  57.0 1.4 collective-permute-done.14.refs_3_
  59.2 1.4 collective-permute-start.18
  62.7 9.5 %collective-permute-done.18.h3 = bf16[1536,128]{1,0:T(8,128)(2,1)S(1)} collective-permute-done((bf16[1536,128]{1,0:T(8,128)(2,1)S(1)}, bf16[1536,128]{1,0:T(8,128)(2,1)S(1)}, u32[]{:S(2)}, u32[]{:S(2)}) %collective-permute-start.18) | collective-permute-done | bytes 393248 | tf_op jit(solution)/shard_map/ppermute | solution.py:721
  72.2 6.7 %collective-permute-done.17.h2 = bf16[1536,128]{1,0:T(8,128)(2,1)S(1)} collective-permute-done((bf16[1536,128]{1,0:T(8,128)(2,1)S(1)}, bf16[1536,128]{1,0:T(8,128)(2,1)S(1)}, u32[]{:S(2)}, u32[]{:S(2)}) %collective-permute-start.17) | collective-permute-done | bytes 393248 | tf_op jit(solution)/shard_map/ppermute | solution.py:721
  78.9 1.3 collective-permute-done.15.refs_2_
  80.9 3.7 %collective-permute-done.19.other = bf16[4,96,2304]{2,1,0:T(8,128)(2,1)S(1)} collective-permute-done((bf16[4,96,2304]{2,1,0:T(8,128)(2,1)S(1)}, bf16[4,96,2304]{2,1,0:T(8,128)(2,1)S(1)}, u32[]{:S(2)}, u32[]{:S(2)}) %collective-permute-start.19) | collective-permute-done | bytes 1769504 | tf_op jit(solution)/shard_map/ppermute | solution.py:717
  85.4 8.0 %feed.1 = (bf16[256,768]{1,0:T(8,128)(2,1)S(1)}, bf16[256,768]{1,0:T(8,128)(2,1)S(1)}, bf16[256,768]{1,0:T(8,128)(2,1)S(1)}, bf16[256,768]{1,0:T(8,128)(2,1)S(1)...) custom-call(s32[4]{0:T(128)S(1)} %pad_add_fusion.meta, ...), custom_call_target="tpu_custom_call" | custom-call | tf_op jit(solution)/shard_map/feed/pallas_call | solution.py:49
  93.4 3.6 %feed_weights.1 = (f32[4,96,1536]{2,1,0:T(8,128)S(1)}, bf16[4,96,1536]{2,1,0:T(8,128)(2,1)S(1)}) custom-call(s32[4]{0:T(128)S(1)} %pad_add_fusion.meta, bf16[1024,768]{1,0:T(8,128)(2,1)S(1)} %get-tuple-element.197.second, bf16[1024,1024]{1,0:T(8,128)(2,1)S(1)} %get-tuple-element.198.grads, bf16[1024,512]{1,0:T(8,128)(2,1)S(1)} %get-tuple-element.199.active, ...), custom_call_target="tpu_custom_call" | custom-call | tf_op jit(solution)/shard_map/feed_weights/pallas_call | solution.py:49
  97.2 1.4 collective-permute-start.22
  98.8 1.9 %collective-permute-start.24 = (bf16[256,768]{1,0:T(8,128)(2,1)S(1)}, bf16[256,768]{1,0:T(8,128)(2,1)S(1)}, u32[]{:S(2)}, u32[]{:S(2)}) collective-permute-start(bf16[256,768]{1,0:T(8,128)(2,1)S(1)} %get-tuple-element.215), channel_id=1, source_target_pairs={{0,3},{1,2},{2,1},{3,0},{4,7},{5,6},{6,5},{7,4},{8,11},{9,10},{10,... | collective-permute-start | bytes 1179656 | tf_op jit(solution)/shard_map/ppermute | solution.py:721
  101.5 1.6 fed.1
  103.8 15.0 %collective-permute-done.21 = bf16[96,1536]{1,0:T(8,128)(2,1)S(1)} collective-permute-done((bf16[96,1536]{1,0:T(8,128)(2,1)S(1)}, bf16[96,1536]{1,0:T(8,128)(2,1)S(1)}, u32[]{:S(2)}, u32[]{:S(2)}) %collective-permute-start.21) | collective-permute-done | bytes 294944 | tf_op jit(solution)/shard_map/ppermute | solution.py:726
  118.8 1.6 middle.1
  120.4 1.4 collective-permute-start.25
  122.3 1.7 collective-permute-start.27
  125.5 2.7 %collective-permute-done.26.g2 = bf16[384,128]{1,0:T(8,128)(2,1)S(1)} collective-permute-done((bf16[384,128]{1,0:T(8,128)(2,1)S(1)}, bf16[384,128]{1,0:T(8,128)(2,1)S(1)}, u32[]{:S(2)}, u32[]{:S(2)}) %collective-permute-start.26) | collective-permute-done | bytes 98336 | tf_op jit(solution)/shard_map/ppermute | solution.py:721
  128.2 1.4 collective-permute-start.29
  130.7 9.4 %attend_back.1 = (bf16[1024,256]{1,0:T(8,128)(2,1)S(1)}, f32[1024,384]{1,0:T(8,128)S(1)}, bf16[1024,384]{1,0:T(8,128)(2,1)S(1)}) custom-call(s32[4]{0:T(128)S(1)} %pad_add_fusion.meta, s32[2,7]{1,0:T(2,128)S(1)} %get-tuple-element.173.ends, bf16[1024,256]{1,0:T(8,128)(2,1)S(1)} %get-tuple-element.178.query, bf16[1024,384]{1,0:T(8,128)(2,1)S(1)} %get-tuple-element.177.own, ...), custom_call_target="tpu_custom_call" | custom-call | tf_op jit(solution)/shard_map/attend_back/pallas_call | solution.py:49
  141.1 2.3 %collective-permute-done.32.arrived = bf16[1024,384]{1,0:T(8,128)(2,1)S(1)} collective-permute-done((bf16[1024,384]{1,0:T(8,128)(2,1)S(1)}, bf16[1024,384]{1,0:T(8,128)(2,1)S(1)}, u32[]{:S(2)}, u32[]{:S(2)}) %collective-permute-start.32) | collective-permute-done | bytes 786464 | tf_op jit(solution)/shard_map/ppermute | solution.py:717
  143.3 1.4 collective-permute-start.33
  144.7 2.6 %collective-permute-start.34 = (bf16[96,1536]{1,0:T(8,128)(2,1)S(1)}, bf16[96,1536]{1,0:T(8,128)(2,1)S(1)}, u32[]{:S(2)}, u32[]{:S(2)}) collective-permute-start(bf16[96,1536]{1,0:T(8,128)(2,1)S(1)} %get-tuple-element.251), channel_id=1, source_target_pairs={{0,24},{8,0},{16,8},{24,16},{1,25},{9,1},{17,9},{25,17},{2,26},{10... | collective-permute-start | bytes 884744 | tf_op jit(solution)/shard_map/ppermute | solution.py:726
  148.0 1.7 first.1.grads
  149.6 2.2 %first_weights.1 = (f32[4,96,640]{2,1,0:T(8,128)S(1)}, bf16[4,96,640]{2,1,0:T(8,128)(2,1)S(1)}) custom-call(s32[4]{0:T(128)S(1)} %pad_add_fusion.meta, bf16[1024,768]{1,0:T(8,128)(2,1)S(1)} %get-tuple-element.241.normed, bf16[1024,640]{1,0:T(8,128)(2,1)S(1)} %first.1.grads, bf16[768,640]{1,0:T(8,128)(2,1)S(1)} %get-tuple-element.169.weight, ...), custom_call_target="tpu_custom_call" | custom-call | tf_op jit(solution)/shard_map/first_weights/pallas_call | solution.py:49
  151.9 2.1 %spread_grad.1 = (bf16[256,768]{1,0:T(8,128)(2,1)S(1)}, bf16[256,768]{1,0:T(8,128)(2,1)S(1)}, bf16[256,768]{1,0:T(8,128)(2,1)S(1)}, bf16[256,768]{1,0:T(8,128)(2,1)S(1)}) custom-call(s32[4]{0:T(128)S(1)} %pad_add_fusion.meta, bf16[1024,640]{1,0:T(8,128)(2,1)S(1)} %first.1.grads, bf16[768,640]{1,0:T(8,128)(2,1)S(1)} %get-tuple-element.169.weight), custom_call_target="tpu_custom_call" | custom-call | tf_op jit(solution)/shard_map/spread_grad/pallas_call | solution.py:49
  154.0 5.5 %collective-permute-done.35.refs_4_ = bf16[96,768]{1,0:T(8,128)(2,1)S(1)} collective-permute-done((bf16[96,768]{1,0:T(8,128)(2,1)S(1)}, bf16[96,768]{1,0:T(8,128)(2,1)S(1)}, u32[]{:S(2)}, u32[]{:S(2)}) %collective-permute-start.35) | collective-permute-done | bytes 147488 | tf_op jit(solution)/shard_map/ppermute | solution.py:726
  161.5 1.5 collective-permute-start.39
  164.7 4.3 %collective-permute-start.41 = (bf16[96,1408]{1,0:T(8,128)(2,1)S(1)}, bf16[96,1408]{1,0:T(8,128)(2,1)S(1)}, u32[]{:S(2)}, u32[]{:S(2)}) collective-permute-start(bf16[96,1408]{1,0:T(8,128)(2,1)S(1)} %get-tuple-element.264), channel_id=1, source_target_pairs={{0,8},{8,16},{16,24},{24,0},{1,9},{9,17},{17,25},{25,1},{2,10},{10... | collective-permute-start | bytes 811016 | tf_op jit(solution)/shard_map/ppermute | solution.py:726
  168.9 2.5 %collective-permute-done.37.g1 = bf16[256,768]{1,0:T(8,128)(2,1)S(1)} collective-permute-done((bf16[256,768]{1,0:T(8,128)(2,1)S(1)}, bf16[256,768]{1,0:T(8,128)(2,1)S(1)}, u32[]{:S(2)}, u32[]{:S(2)}) %collective-permute-start.37) | collective-permute-done | bytes 393248 | tf_op jit(solution)/shard_map/ppermute | solution.py:721
  171.4 4.5 %collective-permute-start.42 = (bf16[96,1408]{1,0:T(8,128)(2,1)S(1)}, bf16[96,1408]{1,0:T(8,128)(2,1)S(1)}, u32[]{:S(2)}, u32[]{:S(2)}) collective-permute-start(bf16[96,1408]{1,0:T(8,128)(2,1)S(1)} %get-tuple-element.265), channel_id=1, source_target_pairs={{0,24},{8,0},{16,8},{24,16},{1,25},{9,1},{17,9},{25,17},{2,26},{10... | collective-permute-start | bytes 811016 | tf_op jit(solution)/shard_map/ppermute | solution.py:726
  179.9 1.9 input.1
  181.8 2.1 %collective-permute-done.42.refs_3_ = bf16[96,1408]{1,0:T(8,128)(2,1)S(1)} collective-permute-done((bf16[96,1408]{1,0:T(8,128)(2,1)S(1)}, bf16[96,1408]{1,0:T(8,128)(2,1)S(1)}, u32[]{:S(2)}, u32[]{:S(2)}) %collective-permute-start.42) | collective-permute-done | bytes 270368 | tf_op jit(solution)/shard_map/ppermute | solution.py:726
  186.7 1.5 collective-permute-start.45
  190.2 1.6 collective-permute-done.45.p3
  191.8 1.7 finish.1
  (130 shorter events, 34.1 us)
Async XLA Ops:
  0.7 28.8 %copy-start.3 = (bf16[512,96]{0,1:T(8,128)(2,1)S(1)}, bf16[512,96]{0,1:T(8,128)(2,1)}, u32[]{:S(2)}) copy-start(bf16[512,96]{0,1:T(8,128)(2,1)} %param.49) | copy-start | bytes 294916
  0.7 28.8 %copy-start.2 = (bf16[2,96,512]{2,1,0:T(8,128)(2,1)S(1)}, bf16[2,96,512]{2,1,0:T(8,128)(2,1)}, u32[]{:S(2)}) copy-start(bf16[2,96,512]{2,1,0:T(8,128)(2,1)} %gateup.1) | copy-start | bytes 589828
  2.2 8.6 %collective-permute-start.2 = (bf16[96,640]{1,0:T(8,128)(2,1)S(1)}, bf16[96,640]{1,0:T(8,128)(2,1)S(1)}, u32[]{:S(2)}, u32[]{:S(2)}) collective-permute-start(bf16[96,640]{1,0:T(8,128)(2,1)S(1)} %get-tuple-element.158.refs_0_), channel_id=1, source_target_pairs={{0,24},{8,0},{16,8},{24,16},{1,25},{9,1},{17,9},{25,17},{2,26},{10... | collective-permute-start | bytes 368648 | tf_op jit(solution)/shard_map/ppermute | solution.py:726
  7.3 15.4 %collective-permute-start.7 = (bf16[288,768]{1,0:T(8,128)(2,1)S(1)}, bf16[288,768]{1,0:T(8,128)(2,1)S(1)}, u32[]{:S(2)}, u32[]{:S(2)}) collective-permute-start(bf16[288,768]{1,0:T(8,128)(2,1)S(1)} %get-tuple-element.154.p0.x0), channel_id=1, source_target_pairs={{0,3},{1,2},{2,1},{3,0},{4,7},{5,6},{6,5},{7,4},{8,11},{9,10},{10,... | collective-permute-start | bytes 1327112 | tf_op jit(solution)/shard_map/ppermute | solution.py:721
  9.8 19.6 %collective-permute-start.6 = (bf16[288,768]{1,0:T(8,128)(2,1)S(1)}, bf16[288,768]{1,0:T(8,128)(2,1)S(1)}, u32[]{:S(2)}, u32[]{:S(2)}) collective-permute-start(bf16[288,768]{1,0:T(8,128)(2,1)S(1)} %get-tuple-element.154.p0.x0), channel_id=1, source_target_pairs={{0,2},{1,3},{2,0},{3,1},{4,6},{5,7},{6,4},{7,5},{8,10},{9,11},{10,... | collective-permute-start | bytes 1327112 | tf_op jit(solution)/shard_map/ppermute | solution.py:721
  10.3 19.2 %collective-permute-start.5 = (bf16[288,768]{1,0:T(8,128)(2,1)S(1)}, bf16[288,768]{1,0:T(8,128)(2,1)S(1)}, u32[]{:S(2)}, u32[]{:S(2)}) collective-permute-start(bf16[288,768]{1,0:T(8,128)(2,1)S(1)} %get-tuple-element.154.p0.x0), channel_id=1, source_target_pairs={{0,1},{1,0},{2,3},{3,2},{4,5},{5,4},{6,7},{7,6},{8,9},{9,8},{10,11... | collective-permute-start | bytes 1327112 | tf_op jit(solution)/shard_map/ppermute | solution.py:721
  10.8 8.6 %collective-permute-start.1 = (bf16[96,640]{1,0:T(8,128)(2,1)S(1)}, bf16[96,640]{1,0:T(8,128)(2,1)S(1)}, u32[]{:S(2)}, u32[]{:S(2)}) collective-permute-start(bf16[96,640]{1,0:T(8,128)(2,1)S(1)} %get-tuple-element.158.refs_0_), channel_id=1, source_target_pairs={{0,16},{8,24},{16,0},{24,8},{1,17},{9,25},{17,1},{25,9},{2,18},{10... | collective-permute-start | bytes 368648 | tf_op jit(solution)/shard_map/ppermute | solution.py:726
  10.8 8.6 %collective-permute-start = (bf16[96,640]{1,0:T(8,128)(2,1)S(1)}, bf16[96,640]{1,0:T(8,128)(2,1)S(1)}, u32[]{:S(2)}, u32[]{:S(2)}) collective-permute-start(bf16[96,640]{1,0:T(8,128)(2,1)S(1)} %get-tuple-element.158.refs_0_), channel_id=1, source_target_pairs={{0,8},{8,16},{16,24},{24,0},{1,9},{9,17},{17,25},{25,1},{2,10},{10... | collective-permute-start | bytes 368648 | tf_op jit(solution)/shard_map/ppermute | solution.py:726
  20.1 1.6 collective-permute-start.3
  20.2 1.8 collective-permute-start.4
  30.1 13.8 %collective-permute-start.10 = (bf16[96,2304]{1,0:T(8,128)(2,1)S(1)}, bf16[96,2304]{1,0:T(8,128)(2,1)S(1)}, u32[]{:S(2)}, u32[]{:S(2)}) collective-permute-start(bf16[96,2304]{1,0:T(8,128)(2,1)S(1)} %join.1.refs_0_), channel_id=1, source_target_pairs={{0,8},{8,16},{16,24},{24,0},{1,9},{9,17},{17,25},{25,1},{2,10},{10... | collective-permute-start | bytes 1327112 | tf_op jit(solution)/shard_map/ppermute | solution.py:726
  30.2 11.0 %collective-permute-start.9 = (bf16[256,768]{1,0:T(8,128)(2,1)S(1)}, bf16[256,768]{1,0:T(8,128)(2,1)S(1)}, u32[]{:S(2)}, u32[]{:S(2)}) collective-permute-start(bf16[256,768]{1,0:T(8,128)(2,1)S(1)} %bitcast.25), channel_id=1, source_target_pairs={{0,2},{1,3},{2,0},{3,1},{4,6},{5,7},{6,4},{7,5},{8,10},{9,11},{10,... | collective-permute-start | bytes 1179656 | tf_op jit(solution)/shard_map/ppermute | solution.py:721
  31.6 10.8 %collective-permute-start.8 = (bf16[256,768]{1,0:T(8,128)(2,1)S(1)}, bf16[256,768]{1,0:T(8,128)(2,1)S(1)}, u32[]{:S(2)}, u32[]{:S(2)}) collective-permute-start(bf16[256,768]{1,0:T(8,128)(2,1)S(1)} %bitcast.26), channel_id=1, source_target_pairs={{0,1},{1,0},{2,3},{3,2},{4,5},{5,4},{6,7},{7,6},{8,9},{9,8},{10,11... | collective-permute-start | bytes 1179656 | tf_op jit(solution)/shard_map/ppermute | solution.py:721
  43.9 2.3 %collective-permute-start.11 = (bf16[1024,384]{1,0:T(8,128)(2,1)S(1)}, bf16[1024,384]{1,0:T(8,128)(2,1)S(1)}, u32[]{:S(2)}, u32[]{:S(2)}) collective-permute-start(bf16[1024,384]{1,0:T(8,128)(2,1)S(1)} %get-tuple-element.177.own), channel_id=1, source_target_pairs={{0,4},{4,0},{1,5},{5,1},{2,6},{6,2},{3,7},{7,3},{8,12},{12,8},{9,1... | collective-permute-start | bytes 2359304 | tf_op jit(solution)/shard_map/ppermute | solution.py:717
  46.2 12.2 %collective-permute-start.14 = (bf16[96,2304]{1,0:T(8,128)(2,1)S(1)}, bf16[96,2304]{1,0:T(8,128)(2,1)S(1)}, u32[]{:S(2)}, u32[]{:S(2)}) collective-permute-start(bf16[96,2304]{1,0:T(8,128)(2,1)S(1)} %join.1.refs_0_), channel_id=1, source_target_pairs={{0,24},{8,0},{16,8},{24,16},{1,25},{9,1},{17,9},{25,17},{2,26},{10... | collective-permute-start | bytes 1327112 | tf_op jit(solution)/shard_map/ppermute | solution.py:726
  48.2 8.8 %collective-permute-start.13 = (bf16[128,768]{1,0:T(8,128)(2,1)S(1)}, bf16[128,768]{1,0:T(8,128)(2,1)S(1)}, u32[]{:S(2)}, u32[]{:S(2)}) collective-permute-start(bf16[128,768]{1,0:T(8,128)(2,1)S(1)} %slice.46), channel_id=1, source_target_pairs={{0,2},{1,3},{2,0},{3,1},{4,6},{5,7},{6,4},{7,5},{8,10},{9,11},{10,... | collective-permute-start | bytes 589832 | tf_op jit(solution)/shard_map/ppermute | solution.py:721
  48.8 8.3 %collective-permute-start.12 = (bf16[128,768]{1,0:T(8,128)(2,1)S(1)}, bf16[128,768]{1,0:T(8,128)(2,1)S(1)}, u32[]{:S(2)}, u32[]{:S(2)}) collective-permute-start(bf16[128,768]{1,0:T(8,128)(2,1)S(1)} %slice.45), channel_id=1, source_target_pairs={{0,1},{1,0},{2,3},{3,2},{4,5},{5,4},{6,7},{7,6},{8,9},{9,8},{10,11... | collective-permute-start | bytes 589832 | tf_op jit(solution)/shard_map/ppermute | solution.py:721
  58.4 21.8 %collective-permute-start.15 = (bf16[96,2304]{1,0:T(8,128)(2,1)S(1)}, bf16[96,2304]{1,0:T(8,128)(2,1)S(1)}, u32[]{:S(2)}, u32[]{:S(2)}) collective-permute-start(bf16[96,2304]{1,0:T(8,128)(2,1)S(1)} %join.1.refs_0_), channel_id=1, source_target_pairs={{0,16},{8,24},{16,0},{24,8},{1,17},{9,25},{17,1},{25,9},{2,18},{10... | collective-permute-start | bytes 1327112 | tf_op jit(solution)/shard_map/ppermute | solution.py:726
  59.2 13.0 %collective-permute-start.18 = (bf16[1536,128]{1,0:T(8,128)(2,1)S(1)}, bf16[1536,128]{1,0:T(8,128)(2,1)S(1)}, u32[]{:S(2)}, u32[]{:S(2)}) collective-permute-start(bf16[1536,128]{1,0:T(8,128)(2,1)S(1)} %get-tuple-element.186.h0), channel_id=1, source_target_pairs={{0,3},{1,2},{2,1},{3,0},{4,7},{5,6},{6,5},{7,4},{8,11},{9,10},{10,... | collective-permute-start | bytes 1179656 | tf_op jit(solution)/shard_map/ppermute | solution.py:721
  60.6 18.3 %collective-permute-start.17 = (bf16[1536,128]{1,0:T(8,128)(2,1)S(1)}, bf16[1536,128]{1,0:T(8,128)(2,1)S(1)}, u32[]{:S(2)}, u32[]{:S(2)}) collective-permute-start(bf16[1536,128]{1,0:T(8,128)(2,1)S(1)} %get-tuple-element.186.h0), channel_id=1, source_target_pairs={{0,2},{1,3},{2,0},{3,1},{4,6},{5,7},{6,4},{7,5},{8,10},{9,11},{10,... | collective-permute-start | bytes 1179656 | tf_op jit(solution)/shard_map/ppermute | solution.py:721
  61.4 17.5 %collective-permute-start.16 = (bf16[1536,128]{1,0:T(8,128)(2,1)S(1)}, bf16[1536,128]{1,0:T(8,128)(2,1)S(1)}, u32[]{:S(2)}, u32[]{:S(2)}) collective-permute-start(bf16[1536,128]{1,0:T(8,128)(2,1)S(1)} %get-tuple-element.186.h0), channel_id=1, source_target_pairs={{0,1},{1,0},{2,3},{3,2},{4,5},{5,4},{6,7},{7,6},{8,9},{9,8},{10,11... | collective-permute-start | bytes 1179656 | tf_op jit(solution)/shard_map/ppermute | solution.py:721
  80.9 3.8 %collective-permute-start.19 = (bf16[4,96,2304]{2,1,0:T(8,128)(2,1)S(1)}, bf16[4,96,2304]{2,1,0:T(8,128)(2,1)S(1)}, u32[]{:S(2)}, u32[]{:S(2)}) collective-permute-start(bf16[4,96,2304]{2,1,0:T(8,128)(2,1)S(1)} %stack.43.own), channel_id=1, source_target_pairs={{0,4},{4,0},{1,5},{5,1},{2,6},{6,2},{3,7},{7,3},{8,12},{12,8},{9,1... | collective-permute-start | bytes 5308424 | tf_op jit(solution)/shard_map/ppermute | solution.py:717
  97.0 3.7 %collective-permute-start.20 = (bf16[4,96,1536]{2,1,0:T(8,128)(2,1)S(1)}, bf16[4,96,1536]{2,1,0:T(8,128)(2,1)S(1)}, u32[]{:S(2)}, u32[]{:S(2)}) collective-permute-start(bf16[4,96,1536]{2,1,0:T(8,128)(2,1)S(1)} %get-tuple-element.201), channel_id=1, source_target_pairs={{0,4},{4,0},{1,5},{5,1},{2,6},{6,2},{3,7},{7,3},{8,12},{12,8},{9,1... | collective-permute-start | bytes 3538952 | tf_op jit(solution)/shard_map/ppermute | solution.py:717
  97.2 21.6 %collective-permute-start.22 = (bf16[256,768]{1,0:T(8,128)(2,1)S(1)}, bf16[256,768]{1,0:T(8,128)(2,1)S(1)}, u32[]{:S(2)}, u32[]{:S(2)}) collective-permute-start(bf16[256,768]{1,0:T(8,128)(2,1)S(1)} %get-tuple-element.213), channel_id=1, source_target_pairs={{0,1},{1,0},{2,3},{3,2},{4,5},{5,4},{6,7},{7,6},{8,9},{9,8},{10,11... | collective-permute-start | bytes 1179656 | tf_op jit(solution)/shard_map/ppermute | solution.py:721
  98.6 20.2 %collective-permute-start.23 = (bf16[256,768]{1,0:T(8,128)(2,1)S(1)}, bf16[256,768]{1,0:T(8,128)(2,1)S(1)}, u32[]{:S(2)}, u32[]{:S(2)}) collective-permute-start(bf16[256,768]{1,0:T(8,128)(2,1)S(1)} %get-tuple-element.214), channel_id=1, source_target_pairs={{0,2},{1,3},{2,0},{3,1},{4,6},{5,7},{6,4},{7,5},{8,10},{9,11},{10,... | collective-permute-start | bytes 1179656 | tf_op jit(solution)/shard_map/ppermute | solution.py:721
  98.8 20.1 %collective-permute-start.24 = (bf16[256,768]{1,0:T(8,128)(2,1)S(1)}, bf16[256,768]{1,0:T(8,128)(2,1)S(1)}, u32[]{:S(2)}, u32[]{:S(2)}) collective-permute-start(bf16[256,768]{1,0:T(8,128)(2,1)S(1)} %get-tuple-element.215), channel_id=1, source_target_pairs={{0,3},{1,2},{2,1},{3,0},{4,7},{5,6},{6,5},{7,4},{8,11},{9,10},{10,... | collective-permute-start | bytes 1179656 | tf_op jit(solution)/shard_map/ppermute | solution.py:721
  103.1 15.7 %collective-permute-start.21 = (bf16[96,1536]{1,0:T(8,128)(2,1)S(1)}, bf16[96,1536]{1,0:T(8,128)(2,1)S(1)}, u32[]{:S(2)}, u32[]{:S(2)}) collective-permute-start(bf16[96,1536]{1,0:T(8,128)(2,1)S(1)} %get-tuple-element.208), channel_id=1, source_target_pairs={{0,16},{8,24},{16,0},{24,8},{1,17},{9,25},{17,1},{25,9},{2,18},{10... | collective-permute-start | bytes 884744 | tf_op jit(solution)/shard_map/ppermute | solution.py:726
  120.4 5.1 %collective-permute-start.25 = (bf16[384,128]{1,0:T(8,128)(2,1)S(1)}, bf16[384,128]{1,0:T(8,128)(2,1)S(1)}, u32[]{:S(2)}, u32[]{:S(2)}) collective-permute-start(bf16[384,128]{1,0:T(8,128)(2,1)S(1)} %get-tuple-element.222), channel_id=1, source_target_pairs={{0,1},{1,0},{2,3},{3,2},{4,5},{5,4},{6,7},{7,6},{8,9},{9,8},{10,11... | collective-permute-start | bytes 294920 | tf_op jit(solution)/shard_map/ppermute | solution.py:721
  121.9 6.3 %collective-permute-start.26 = (bf16[384,128]{1,0:T(8,128)(2,1)S(1)}, bf16[384,128]{1,0:T(8,128)(2,1)S(1)}, u32[]{:S(2)}, u32[]{:S(2)}) collective-permute-start(bf16[384,128]{1,0:T(8,128)(2,1)S(1)} %get-tuple-element.223), channel_id=1, source_target_pairs={{0,2},{1,3},{2,0},{3,1},{4,6},{5,7},{6,4},{7,5},{8,10},{9,11},{10,... | collective-permute-start | bytes 294920 | tf_op jit(solution)/shard_map/ppermute | solution.py:721
  122.3 5.9 %collective-permute-start.27 = (bf16[384,128]{1,0:T(8,128)(2,1)S(1)}, bf16[384,128]{1,0:T(8,128)(2,1)S(1)}, u32[]{:S(2)}, u32[]{:S(2)}) collective-permute-start(bf16[384,128]{1,0:T(8,128)(2,1)S(1)} %get-tuple-element.224), channel_id=1, source_target_pairs={{0,3},{1,2},{2,1},{3,0},{4,7},{5,6},{6,5},{7,4},{8,11},{9,10},{10,... | collective-permute-start | bytes 294920 | tf_op jit(solution)/shard_map/ppermute | solution.py:721
  128.2 12.8 %collective-permute-start.28 = (bf16[4,96,768]{2,1,0:T(8,128)(2,1)S(1)}, bf16[4,96,768]{2,1,0:T(8,128)(2,1)S(1)}, u32[]{:S(2)}, u32[]{:S(2)}) collective-permute-start(bf16[4,96,768]{2,1,0:T(8,128)(2,1)S(1)} %get-tuple-element.228), channel_id=1, source_target_pairs={{0,4},{4,0},{1,5},{5,1},{2,6},{6,2},{3,7},{7,3},{8,12},{12,8},{9,1... | collective-permute-start | bytes 1769480 | tf_op jit(solution)/shard_map/ppermute | solution.py:717
  128.2 12.8 %collective-permute-start.29 = (bf16[256,768]{1,0:T(8,128)(2,1)S(1)}, bf16[256,768]{1,0:T(8,128)(2,1)S(1)}, u32[]{:S(2)}, u32[]{:S(2)}) collective-permute-start(bf16[256,768]{1,0:T(8,128)(2,1)S(1)} %get-tuple-element.230), channel_id=1, source_target_pairs={{0,1},{1,0},{2,3},{3,2},{4,5},{5,4},{6,7},{7,6},{8,9},{9,8},{10,11... | collective-permute-start | bytes 1179656 | tf_op jit(solution)/shard_map/ppermute | solution.py:721
  129.6 11.4 %collective-permute-start.30 = (bf16[256,768]{1,0:T(8,128)(2,1)S(1)}, bf16[256,768]{1,0:T(8,128)(2,1)S(1)}, u32[]{:S(2)}, u32[]{:S(2)}) collective-permute-start(bf16[256,768]{1,0:T(8,128)(2,1)S(1)} %get-tuple-element.232), channel_id=1, source_target_pairs={{0,2},{1,3},{2,0},{3,1},{4,6},{5,7},{6,4},{7,5},{8,10},{9,11},{10,... | collective-permute-start | bytes 1179656 | tf_op jit(solution)/shard_map/ppermute | solution.py:721
  130.3 10.7 %collective-permute-start.31 = (bf16[96,1536]{1,0:T(8,128)(2,1)S(1)}, bf16[96,1536]{1,0:T(8,128)(2,1)S(1)}, u32[]{:S(2)}, u32[]{:S(2)}) collective-permute-start(bf16[96,1536]{1,0:T(8,128)(2,1)S(1)} %get-tuple-element.234), channel_id=1, source_target_pairs={{0,8},{8,16},{16,24},{24,0},{1,9},{9,17},{17,25},{25,1},{2,10},{10... | collective-permute-start | bytes 884744 | tf_op jit(solution)/shard_map/ppermute | solution.py:726
  141.0 2.4 %collective-permute-start.32 = (bf16[1024,384]{1,0:T(8,128)(2,1)S(1)}, bf16[1024,384]{1,0:T(8,128)(2,1)S(1)}, u32[]{:S(2)}, u32[]{:S(2)}) collective-permute-start(bf16[1024,384]{1,0:T(8,128)(2,1)S(1)} %get-tuple-element.235), channel_id=1, source_target_pairs={{0,4},{4,0},{1,5},{5,1},{2,6},{6,2},{3,7},{7,3},{8,12},{12,8},{9,1... | collective-permute-start | bytes 2359304 | tf_op jit(solution)/shard_map/ppermute | solution.py:717
  143.3 16.1 %collective-permute-start.33 = (bf16[256,768]{1,0:T(8,128)(2,1)S(1)}, bf16[256,768]{1,0:T(8,128)(2,1)S(1)}, u32[]{:S(2)}, u32[]{:S(2)}) collective-permute-start(bf16[256,768]{1,0:T(8,128)(2,1)S(1)} %get-tuple-element.250), channel_id=1, source_target_pairs={{0,3},{1,2},{2,1},{3,0},{4,7},{5,6},{6,5},{7,4},{8,11},{9,10},{10,... | collective-permute-start | bytes 1179656 | tf_op jit(solution)/shard_map/ppermute | solution.py:721
  144.7 14.7 %collective-permute-start.34 = (bf16[96,1536]{1,0:T(8,128)(2,1)S(1)}, bf16[96,1536]{1,0:T(8,128)(2,1)S(1)}, u32[]{:S(2)}, u32[]{:S(2)}) collective-permute-start(bf16[96,1536]{1,0:T(8,128)(2,1)S(1)} %get-tuple-element.251), channel_id=1, source_target_pairs={{0,24},{8,0},{16,8},{24,16},{1,25},{9,1},{17,9},{25,17},{2,26},{10... | collective-permute-start | bytes 884744 | tf_op jit(solution)/shard_map/ppermute | solution.py:726
  147.9 11.6 %collective-permute-start.35 = (bf16[96,768]{1,0:T(8,128)(2,1)S(1)}, bf16[96,768]{1,0:T(8,128)(2,1)S(1)}, u32[]{:S(2)}, u32[]{:S(2)}) collective-permute-start(bf16[96,768]{1,0:T(8,128)(2,1)S(1)} %context_sum.4), channel_id=1, source_target_pairs={{0,16},{8,24},{16,0},{24,8},{1,17},{9,25},{17,1},{25,9},{2,18},{10... | collective-permute-start | bytes 442376 | tf_op jit(solution)/shard_map/ppermute | solution.py:726
  159.5 3.6 %collective-permute-start.36 = (bf16[4,96,640]{2,1,0:T(8,128)(2,1)S(1)}, bf16[4,96,640]{2,1,0:T(8,128)(2,1)S(1)}, u32[]{:S(2)}, u32[]{:S(2)}) collective-permute-start(bf16[4,96,640]{2,1,0:T(8,128)(2,1)S(1)} %get-tuple-element.252), channel_id=1, source_target_pairs={{0,4},{4,0},{1,5},{5,1},{2,6},{6,2},{3,7},{7,3},{8,12},{12,8},{9,1... | collective-permute-start | bytes 1474568 | tf_op jit(solution)/shard_map/ppermute | solution.py:717
  159.5 12.0 %collective-permute-start.37 = (bf16[256,768]{1,0:T(8,128)(2,1)S(1)}, bf16[256,768]{1,0:T(8,128)(2,1)S(1)}, u32[]{:S(2)}, u32[]{:S(2)}) collective-permute-start(bf16[256,768]{1,0:T(8,128)(2,1)S(1)} %get-tuple-element.258), channel_id=1, source_target_pairs={{0,1},{1,0},{2,3},{3,2},{4,5},{5,4},{6,7},{7,6},{8,9},{9,8},{10,11... | collective-permute-start | bytes 1179656 | tf_op jit(solution)/shard_map/ppermute | solution.py:721
  160.3 19.6 %collective-permute-start.38 = (bf16[256,768]{1,0:T(8,128)(2,1)S(1)}, bf16[256,768]{1,0:T(8,128)(2,1)S(1)}, u32[]{:S(2)}, u32[]{:S(2)}) collective-permute-start(bf16[256,768]{1,0:T(8,128)(2,1)S(1)} %get-tuple-element.259), channel_id=1, source_target_pairs={{0,2},{1,3},{2,0},{3,1},{4,6},{5,7},{6,4},{7,5},{8,10},{9,11},{10,... | collective-permute-start | bytes 1179656 | tf_op jit(solution)/shard_map/ppermute | solution.py:721
  161.5 18.4 %collective-permute-start.39 = (bf16[256,768]{1,0:T(8,128)(2,1)S(1)}, bf16[256,768]{1,0:T(8,128)(2,1)S(1)}, u32[]{:S(2)}, u32[]{:S(2)}) collective-permute-start(bf16[256,768]{1,0:T(8,128)(2,1)S(1)} %get-tuple-element.260), channel_id=1, source_target_pairs={{0,3},{1,2},{2,1},{3,0},{4,7},{5,6},{6,5},{7,4},{8,11},{9,10},{10,... | collective-permute-start | bytes 1179656 | tf_op jit(solution)/shard_map/ppermute | solution.py:721
  163.8 18.0 %collective-permute-start.40 = (bf16[96,640]{1,0:T(8,128)(2,1)S(1)}, bf16[96,640]{1,0:T(8,128)(2,1)S(1)}, u32[]{:S(2)}, u32[]{:S(2)}) collective-permute-start(bf16[96,640]{1,0:T(8,128)(2,1)S(1)} %get-tuple-element.263), channel_id=1, source_target_pairs={{0,16},{8,24},{16,0},{24,8},{1,17},{9,25},{17,1},{25,9},{2,18},{10... | collective-permute-start | bytes 368648 | tf_op jit(solution)/shard_map/ppermute | solution.py:726
  164.7 19.2 %collective-permute-start.41 = (bf16[96,1408]{1,0:T(8,128)(2,1)S(1)}, bf16[96,1408]{1,0:T(8,128)(2,1)S(1)}, u32[]{:S(2)}, u32[]{:S(2)}) collective-permute-start(bf16[96,1408]{1,0:T(8,128)(2,1)S(1)} %get-tuple-element.264), channel_id=1, source_target_pairs={{0,8},{8,16},{16,24},{24,0},{1,9},{9,17},{17,25},{25,1},{2,10},{10... | collective-permute-start | bytes 811016 | tf_op jit(solution)/shard_map/ppermute | solution.py:726
  171.4 12.4 %collective-permute-start.42 = (bf16[96,1408]{1,0:T(8,128)(2,1)S(1)}, bf16[96,1408]{1,0:T(8,128)(2,1)S(1)}, u32[]{:S(2)}, u32[]{:S(2)}) collective-permute-start(bf16[96,1408]{1,0:T(8,128)(2,1)S(1)} %get-tuple-element.265), channel_id=1, source_target_pairs={{0,24},{8,0},{16,8},{24,16},{1,25},{9,1},{17,9},{25,17},{2,26},{10... | collective-permute-start | bytes 811016 | tf_op jit(solution)/shard_map/ppermute | solution.py:726
  184.6 5.6 %collective-permute-start.43 = (bf16[112,192]{1,0:T(8,128)(2,1)S(1)}, bf16[112,192]{1,0:T(8,128)(2,1)S(1)}, u32[]{:S(2)}, u32[]{:S(2)}) collective-permute-start(bf16[112,192]{1,0:T(8,128)(2,1)S(1)} %get-tuple-element.270), channel_id=1, source_target_pairs={{0,1},{1,0},{2,3},{3,2},{4,5},{5,4},{6,7},{7,6},{8,9},{9,8},{10,11... | collective-permute-start | bytes 129032 | tf_op jit(solution)/shard_map/ppermute | solution.py:721
  185.5 4.8 %collective-permute-start.44 = (bf16[112,192]{1,0:T(8,128)(2,1)S(1)}, bf16[112,192]{1,0:T(8,128)(2,1)S(1)}, u32[]{:S(2)}, u32[]{:S(2)}) collective-permute-start(bf16[112,192]{1,0:T(8,128)(2,1)S(1)} %get-tuple-element.271), channel_id=1, source_target_pairs={{0,2},{1,3},{2,0},{3,1},{4,6},{5,7},{6,4},{7,5},{8,10},{9,11},{10,... | collective-permute-start | bytes 129032 | tf_op jit(solution)/shard_map/ppermute | solution.py:721
  186.7 5.1 %collective-permute-start.45 = (bf16[112,192]{1,0:T(8,128)(2,1)S(1)}, bf16[112,192]{1,0:T(8,128)(2,1)S(1)}, u32[]{:S(2)}, u32[]{:S(2)}) collective-permute-start(bf16[112,192]{1,0:T(8,128)(2,1)S(1)} %get-tuple-element.267), channel_id=1, source_target_pairs={{0,3},{1,2},{2,1},{3,0},{4,7},{5,6},{6,5},{7,4},{8,11},{9,10},{10,... | collective-permute-start | bytes 129032 | tf_op jit(solution)/shard_map/ppermute | solution.py:721
  (23 other events, 110.0 us)

commit v4 on v3

--- a/solution.py
+++ b/solution.py
@@ -957,18 +957,10 @@
     )
     if by_hand:
         feed_parts = context_sums(chain, feed_sums[0], swap_ctx(feed_sums[1]))
-    fed = chain.call(
-        "fed",
-        fed_body,
-        [piece_shape] * 4,
-        (),
-        (active, second_full),
-        [((256, features), BF16)],
-    )
     feed_landed = []
     if by_hand:
         feed_landed = [feed_parts[0]]
-        feed_landed.append(shift_dp(after(feed_parts[2], fed[0]), 2))
+        feed_landed.append(shift_dp(feed_parts[2], 2))
         middle_own = after(middle_own, feed_landed[1:])
     sends = chain.call(
         "middle",
@@ -980,6 +972,14 @@
     )
     grad_middle, grad_low, gain_two = sends[4:]
     grad_heads = exchange(sends[:4])
+    fed = chain.call(
+        "fed",
+        fed_body,
+        [piece_shape] * 4,
+        (),
+        (active, second_full),
+        [((256, features), BF16)],
+    )
     output_sums = chain.call(
         "output_weights",
         output_weights_body,
@@ -989,6 +989,9 @@
         [((features, 256), F32)],
     )
     done = (grad_heads,)
+    if by_hand:
+        feed_landed.append(shift_dp(after(feed_parts[3], grad_low), 3))
+        done = (grad_heads, feed_landed[2:])
 
     fed_near = [across(after(fed[offset], done), offset) for offset in (1, 2)]
     if by_hand:
@@ -1010,12 +1013,11 @@
             ((4, 256, 3 * TILE), F32),
         ],
     )
-    done = (fed_near, arrived_output, feed_landed[2:])
+    done = (fed_near, arrived_output, feed_landed[3:])
     arrived = swap_ctx(after(grad_other, done))
 
     fed_far = across(after(fed[3], arrived), 3)
     if by_hand:
-        feed_landed.append(shift_dp(after(feed_parts[3], arrived), 3))
         pair = (output_sums[0], after(arrived_output, arrived))
         output_far = shift_dp(context_sums(chain, *pair, offsets=(2,))[0], 2)
     grads = chain.call(
@@ -1041,7 +1043,7 @@
         (grads, weight),
         [((QKV, features), BF16), ((256, features), BF16)],
     )
-    done = (fed_far, feed_landed[3:], [output_far] if by_hand else [])
+    done = (fed_far, [output_far] if by_hand else [])
     first_grads = exchange(after(spread_grads, done))
     arrived_first = swap_ctx(after(first_sums[1], spread_grads, done)) if by_hand else grads
     if by_hand:

time: 194 us -> 190 us (0.979)
  starting transfers between devices: 52.1 us -> 49.2 us
    ppermute x13, waiting for transfers between devices: 30.3 us -> 25.7 us  [shift_dp(): lax.ppermute(value, 'dp', [(i, (i + shift) % size) for i in range(size)])]
    ppermute x25, waiting for transfers between devices: 35.3 us -> 39.3 us  [across(): lax.ppermute(value, 'tensor', [(i, i ^ offset) for i in range(PARTS)])]
    ppermute x13, starting transfers between devices: 22.2 us -> 19.5 us  [shift_dp(): lax.ppermute(value, 'dp', [(i, (i + shift) % size) for i in range(size)])]
  transfers between devices with their start and end apart: 46 -> 46, of which waited for: 24 -> 27; matrix products, arithmetic and copies ran while one was open for 3% -> 3% of each run, Pallas kernels for 20% -> 20%
where the time goes in v4:
time: 190 us
  waiting for transfers between devices  74.6 us (39%)
  Pallas kernels  57.4 us (30%)
  starting transfers between devices  49.2 us (26%)
  other arithmetic  5.18 us (3%)
  local copies, waits for them, and re-layouts  2.38 us (1%)
    pallas_call x23, Pallas kernels, call(): pl.pallas_call(body, out_shape=out_shape, in_specs=[SMEM] * len(scalars)...  54.5 us
    ppermute x25, waiting for transfers between devices, across(): lax.ppermute(value, 'tensor', [(i, i ^ offset) for i in range(PARTS)])  39.3 us
    ppermute x25, starting transfers between devices, across(): lax.ppermute(value, 'tensor', [(i, i ^ offset) for i in range(PARTS)])  28.8 us
    ppermute x13, waiting for transfers between devices, shift_dp(): lax.ppermute(value, 'dp', [(i, (i + shift) % size) for i in range(size)])  25.7 us
    ppermute x13, starting transfers between devices, shift_dp(): lax.ppermute(value, 'dp', [(i, (i + shift) % size) for i in range(size)])  19.5 us
    ppermute x8, waiting for transfers between devices, swap_ctx(): return lax.ppermute(value, 'ctx', [(0, 1), (1, 0)])  9.59 us
    sub x4, other arithmetic, adam_step(): return (gradient, master - rate * stepped, moment_new, variance_new)  3.87 us
  transfers between devices with their start and end apart: 46, of which 27 were waited for; matrix products, arithmetic and copies ran while one was open for 3% of the time, Pallas kernels for 20%

profile of v4, /device:TPU:0, one launch (start us, length us, event | category | flops | bytes accessed | tf_op | source)
XLA Modules:
  0.0 190.0 jit_solution(14165045897031288578)
XLA Ops:
  0.8 1.5 prepare.1
  2.2 5.1 %collective-permute-start.2 = (bf16[96,640]{1,0:T(8,128)(2,1)S(1)}, bf16[96,640]{1,0:T(8,128)(2,1)S(1)}, u32[]{:S(2)}, u32[]{:S(2)}) collective-permute-start(bf16[96,640]{1,0:T(8,128)(2,1)S(1)} %get-tuple-element.157.refs_0_), channel_id=1, source_target_pairs={{0,24},{8,0},{16,8},{24,16},{1,25},{9,1},{17,9},{25,17},{2,26},{10... | collective-permute-start | bytes 368648 | tf_op jit(solution)/shard_map/ppermute | solution.py:726
  7.3 2.4 %collective-permute-start.7 = (bf16[288,768]{1,0:T(8,128)(2,1)S(1)}, bf16[288,768]{1,0:T(8,128)(2,1)S(1)}, u32[]{:S(2)}, u32[]{:S(2)}) collective-permute-start(bf16[288,768]{1,0:T(8,128)(2,1)S(1)} %get-tuple-element.153.p0.x0), channel_id=1, source_target_pairs={{0,3},{1,2},{2,1},{3,0},{4,7},{5,6},{6,5},{7,4},{8,11},{9,10},{10,... | collective-permute-start | bytes 1327112 | tf_op jit(solution)/shard_map/ppermute | solution.py:721
  13.9 2.9 %tables.1 = (s32[2,7]{1,0:T(2,128)S(1)}, f32[1024,128]{1,0:T(8,128)S(1)}, f32[1024,128]{1,0:T(8,128)S(1)}) custom-call(s32[4]{0:T(128)S(1)} %pad_add_fusion.meta, s32[2,8]{1,0:T(2,128)S(1)} %copy-done.10, s32[2,7]{1,0:T(2,128)S(1)} %copy-done.11, f32[1,128]{1,0:T(1,128)S(1)} %copy-done.12), custom_call_target="tpu_custom_call" | custom-call | tf_op jit(solution)/shard_map/tables/pallas_call | solution.py:694
  16.8 2.6 %collective-permute-done.1.refs_2_ = bf16[96,640]{1,0:T(8,128)(2,1)S(1)} collective-permute-done((bf16[96,640]{1,0:T(8,128)(2,1)S(1)}, bf16[96,640]{1,0:T(8,128)(2,1)S(1)}, u32[]{:S(2)}, u32[]{:S(2)}) %collective-permute-start.1) | collective-permute-done | bytes 122912 | tf_op jit(solution)/shard_map/ppermute | solution.py:726
  22.7 6.6 %collective-permute-done.6.p2.x2 = bf16[288,768]{1,0:T(8,128)(2,1)S(1)} collective-permute-done((bf16[288,768]{1,0:T(8,128)(2,1)S(1)}, bf16[288,768]{1,0:T(8,128)(2,1)S(1)}, u32[]{:S(2)}, u32[]{:S(2)}) %collective-permute-start.6) | collective-permute-done | bytes 442400 | tf_op jit(solution)/shard_map/ppermute | solution.py:721
  30.2 1.5 collective-permute-start.9
  32.4 5.1 %project.1 = (bf16[1024,768]{1,0:T(8,128)(2,1)S(1)}, bf16[1024,768]{1,0:T(8,128)(2,1)S(1)}, bf16[1024,256]{1,0:T(8,128)(2,1)S(1)}, bf16[1024,384]{1,0:T(8,128)(2,1)S(1)}) custom-call(s32[4]{0:T(128)S(1)} %pad_add_fusion.meta, bf16[288,768]{1,0:T(8,128)(2,1)S(1)} %get-tuple-element.153.p0.x0, bf16[288,768]{1,0:T(8,128)(2,1)S(1)} %collective-permute-done.5.p1.x1, ...), custom_call_target="tpu_custom_call" | custom-call | tf_op jit(solution)/shard_map/project/pallas_call | solution.py:49
  37.6 3.6 %collective-permute-done.9.c2 = bf16[256,768]{1,0:T(8,128)(2,1)S(1)} collective-permute-done((bf16[256,768]{1,0:T(8,128)(2,1)S(1)}, bf16[256,768]{1,0:T(8,128)(2,1)S(1)}, u32[]{:S(2)}, u32[]{:S(2)}) %collective-permute-start.9) | collective-permute-done | bytes 393248 | tf_op jit(solution)/shard_map/ppermute | solution.py:721
  42.4 1.5 collective-permute-done.10.refs_1_
  43.9 2.3 %collective-permute-done.11.other = bf16[1024,384]{1,0:T(8,128)(2,1)S(1)} collective-permute-done((bf16[1024,384]{1,0:T(8,128)(2,1)S(1)}, bf16[1024,384]{1,0:T(8,128)(2,1)S(1)}, u32[]{:S(2)}, u32[]{:S(2)}) %collective-permute-start.11) | collective-permute-done | bytes 786464 | tf_op jit(solution)/shard_map/ppermute | solution.py:717
  46.2 1.9 %collective-permute-start.14 = (bf16[96,2304]{1,0:T(8,128)(2,1)S(1)}, bf16[96,2304]{1,0:T(8,128)(2,1)S(1)}, u32[]{:S(2)}, u32[]{:S(2)}) collective-permute-start(bf16[96,2304]{1,0:T(8,128)(2,1)S(1)} %join.1.refs_0_), channel_id=1, source_target_pairs={{0,24},{8,0},{16,8},{24,16},{1,25},{9,1},{17,9},{25,17},{2,26},{10... | collective-permute-start | bytes 1327112 | tf_op jit(solution)/shard_map/ppermute | solution.py:726
  48.8 1.5 collective-permute-start.12
  50.3 6.7 %attend.1 = (bf16[1536,128]{1,0:T(8,128)(2,1)S(1)}, f32[4,8,256]{2,1,0:T(8,128)S(1)}) custom-call(s32[4]{0:T(128)S(1)} %pad_add_fusion.meta, s32[2,7]{1,0:T(2,128)S(1)} %get-tuple-element.172.ends, bf16[1024,256]{1,0:T(8,128)(2,1)S(1)} %get-tuple-element.177.query, bf16[1024,384]{1,0:T(8,128)(2,1)S(1)} %get-tuple-element.176.own, ...), custom_call_target="tpu_custom_call" | custom-call | tf_op jit(solution)/shard_map/attend/pallas_call | solution.py:49
  57.0 1.4 collective-permute-done.14.refs_3_
  59.2 1.4 collective-permute-start.18
  62.7 9.5 %collective-permute-done.18.h3 = bf16[1536,128]{1,0:T(8,128)(2,1)S(1)} collective-permute-done((bf16[1536,128]{1,0:T(8,128)(2,1)S(1)}, bf16[1536,128]{1,0:T(8,128)(2,1)S(1)}, u32[]{:S(2)}, u32[]{:S(2)}) %collective-permute-start.18) | collective-permute-done | bytes 393248 | tf_op jit(solution)/shard_map/ppermute | solution.py:721
  72.2 6.7 %collective-permute-done.17.h2 = bf16[1536,128]{1,0:T(8,128)(2,1)S(1)} collective-permute-done((bf16[1536,128]{1,0:T(8,128)(2,1)S(1)}, bf16[1536,128]{1,0:T(8,128)(2,1)S(1)}, u32[]{:S(2)}, u32[]{:S(2)}) %collective-permute-start.17) | collective-permute-done | bytes 393248 | tf_op jit(solution)/shard_map/ppermute | solution.py:721
  80.9 3.7 %collective-permute-done.19.other = bf16[4,96,2304]{2,1,0:T(8,128)(2,1)S(1)} collective-permute-done((bf16[4,96,2304]{2,1,0:T(8,128)(2,1)S(1)}, bf16[4,96,2304]{2,1,0:T(8,128)(2,1)S(1)}, u32[]{:S(2)}, u32[]{:S(2)}) %collective-permute-start.19) | collective-permute-done | bytes 1769504 | tf_op jit(solution)/shard_map/ppermute | solution.py:717
  85.4 8.0 %feed.1 = (bf16[256,768]{1,0:T(8,128)(2,1)S(1)}, bf16[256,768]{1,0:T(8,128)(2,1)S(1)}, bf16[256,768]{1,0:T(8,128)(2,1)S(1)}, bf16[256,768]{1,0:T(8,128)(2,1)S(1)...) custom-call(s32[4]{0:T(128)S(1)} %pad_add_fusion.meta, ...), custom_call_target="tpu_custom_call" | custom-call | tf_op jit(solution)/shard_map/feed/pallas_call | solution.py:49
  93.4 3.6 %feed_weights.1 = (f32[4,96,1536]{2,1,0:T(8,128)S(1)}, bf16[4,96,1536]{2,1,0:T(8,128)(2,1)S(1)}) custom-call(s32[4]{0:T(128)S(1)} %pad_add_fusion.meta, bf16[1024,768]{1,0:T(8,128)(2,1)S(1)} %get-tuple-element.196.second, bf16[1024,1024]{1,0:T(8,128)(2,1)S(1)} %get-tuple-element.197.grads, bf16[1024,512]{1,0:T(8,128)(2,1)S(1)} %get-tuple-element.198.active, ...), custom_call_target="tpu_custom_call" | custom-call | tf_op jit(solution)/shard_map/feed_weights/pallas_call | solution.py:49
  97.2 1.4 collective-permute-start.22
  98.8 1.9 %collective-permute-start.24 = (bf16[256,768]{1,0:T(8,128)(2,1)S(1)}, bf16[256,768]{1,0:T(8,128)(2,1)S(1)}, u32[]{:S(2)}, u32[]{:S(2)}) collective-permute-start(bf16[256,768]{1,0:T(8,128)(2,1)S(1)} %get-tuple-element.210), channel_id=1, source_target_pairs={{0,3},{1,2},{2,1},{3,0},{4,7},{5,6},{6,5},{7,4},{8,11},{9,10},{10,... | collective-permute-start | bytes 1179656 | tf_op jit(solution)/shard_map/ppermute | solution.py:721
  102.2 15.0 %collective-permute-done.21 = bf16[96,1536]{1,0:T(8,128)(2,1)S(1)} collective-permute-done((bf16[96,1536]{1,0:T(8,128)(2,1)S(1)}, bf16[96,1536]{1,0:T(8,128)(2,1)S(1)}, u32[]{:S(2)}, u32[]{:S(2)}) %collective-permute-start.21) | collective-permute-done | bytes 294944 | tf_op jit(solution)/shard_map/ppermute | solution.py:726
  118.1 1.6 middle.1
  119.7 1.6 collective-permute-start.28
  123.4 1.4 collective-permute-start.27
  124.8 1.6 fed.1
  131.6 9.4 %attend_back.1 = (bf16[1024,256]{1,0:T(8,128)(2,1)S(1)}, f32[1024,384]{1,0:T(8,128)S(1)}, bf16[1024,384]{1,0:T(8,128)(2,1)S(1)}) custom-call(s32[4]{0:T(128)S(1)} %pad_add_fusion.meta, s32[2,7]{1,0:T(2,128)S(1)} %get-tuple-element.172.ends, bf16[1024,256]{1,0:T(8,128)(2,1)S(1)} %get-tuple-element.177.query, bf16[1024,384]{1,0:T(8,128)(2,1)S(1)} %get-tuple-element.176.own, ...), custom_call_target="tpu_custom_call" | custom-call | tf_op jit(solution)/shard_map/attend_back/pallas_call | solution.py:49
  141.6 2.3 %collective-permute-done.33.arrived = bf16[1024,384]{1,0:T(8,128)(2,1)S(1)} collective-permute-done((bf16[1024,384]{1,0:T(8,128)(2,1)S(1)}, bf16[1024,384]{1,0:T(8,128)(2,1)S(1)}, u32[]{:S(2)}, u32[]{:S(2)}) %collective-permute-start.33) | collective-permute-done | bytes 786464 | tf_op jit(solution)/shard_map/ppermute | solution.py:717
  143.9 1.5 collective-permute-start.34
  146.0 1.8 collective-permute-start.35
  147.8 1.7 first.1.grads
  149.5 2.2 %first_weights.1 = (f32[4,96,640]{2,1,0:T(8,128)S(1)}, bf16[4,96,640]{2,1,0:T(8,128)(2,1)S(1)}) custom-call(s32[4]{0:T(128)S(1)} %pad_add_fusion.meta, bf16[1024,768]{1,0:T(8,128)(2,1)S(1)} %get-tuple-element.239.normed, bf16[1024,640]{1,0:T(8,128)(2,1)S(1)} %first.1.grads, bf16[768,640]{1,0:T(8,128)(2,1)S(1)} %get-tuple-element.168.weight, ...), custom_call_target="tpu_custom_call" | custom-call | tf_op jit(solution)/shard_map/first_weights/pallas_call | solution.py:49
  151.7 2.1 %spread_grad.1 = (bf16[256,768]{1,0:T(8,128)(2,1)S(1)}, bf16[256,768]{1,0:T(8,128)(2,1)S(1)}, bf16[256,768]{1,0:T(8,128)(2,1)S(1)}, bf16[256,768]{1,0:T(8,128)(2,1)S(1)}) custom-call(s32[4]{0:T(128)S(1)} %pad_add_fusion.meta, bf16[1024,640]{1,0:T(8,128)(2,1)S(1)} %first.1.grads, bf16[768,640]{1,0:T(8,128)(2,1)S(1)} %get-tuple-element.168.weight), custom_call_target="tpu_custom_call" | custom-call | tf_op jit(solution)/shard_map/spread_grad/pallas_call | solution.py:49
  153.9 1.9 collective-permute-done.35.refs_4_
  156.0 1.3 collective-permute-start.37
  158.0 1.4 collective-permute-start.39
  160.2 1.9 collective-permute-start.40
  162.1 1.3 collective-permute-start.41
  163.4 4.4 %collective-permute-done.37.g1 = bf16[256,768]{1,0:T(8,128)(2,1)S(1)} collective-permute-done((bf16[256,768]{1,0:T(8,128)(2,1)S(1)}, bf16[256,768]{1,0:T(8,128)(2,1)S(1)}, u32[]{:S(2)}, u32[]{:S(2)}) %collective-permute-start.37) | collective-permute-done | bytes 393248 | tf_op jit(solution)/shard_map/ppermute | solution.py:721
  167.9 2.6 %collective-permute-start.42 = (bf16[96,1408]{1,0:T(8,128)(2,1)S(1)}, bf16[96,1408]{1,0:T(8,128)(2,1)S(1)}, u32[]{:S(2)}, u32[]{:S(2)}) collective-permute-start(bf16[96,1408]{1,0:T(8,128)(2,1)S(1)} %get-tuple-element.263), channel_id=1, source_target_pairs={{0,24},{8,0},{16,8},{24,16},{1,25},{9,1},{17,9},{25,17},{2,26},{10... | collective-permute-start | bytes 811016 | tf_op jit(solution)/shard_map/ppermute | solution.py:726
  173.9 3.0 %collective-permute-done.38.g2 = bf16[256,768]{1,0:T(8,128)(2,1)S(1)} collective-permute-done((bf16[256,768]{1,0:T(8,128)(2,1)S(1)}, bf16[256,768]{1,0:T(8,128)(2,1)S(1)}, u32[]{:S(2)}, u32[]{:S(2)}) %collective-permute-start.38) | collective-permute-done | bytes 393248 | tf_op jit(solution)/shard_map/ppermute | solution.py:721
  177.0 1.9 %input.1 = f32[256,768]{1,0:T(8,128)} custom-call(s32[4]{0:T(128)S(1)} %pad_add_fusion.meta, bf16[256,768]{1,0:T(8,128)(2,1)S(1)} %get-tuple-element.255.g0, bf16[256,768]{1,0:T(8,128)(2,1)S(1)} %collective-permute-done.37.g1, bf16[256,768]{1,0:T(8,128)(2,1)S(1)} %collective-permute-done.38.g2, bf16[256,768]{1,0:T(8,128)(2,1)S(1)} %collective-permute-done.39.g3, ...), custom_call_target="tpu_custom_call" | custom-call | tf_op jit(solution)/shard_map/input/pallas_call | solution.py:49
  178.9 1.4 collective-permute-done.42.refs_3_
  181.1 1.4 collective-permute-start.43
  183.2 1.4 collective-permute-start.45
  188.3 1.7 finish.1
  (130 shorter events, 37.9 us)
Async XLA Ops:
  0.7 28.8 %copy-start.3 = (bf16[512,96]{0,1:T(8,128)(2,1)S(1)}, bf16[512,96]{0,1:T(8,128)(2,1)}, u32[]{:S(2)}) copy-start(bf16[512,96]{0,1:T(8,128)(2,1)} %param.49) | copy-start | bytes 294916
  0.7 28.8 %copy-start.2 = (bf16[2,96,512]{2,1,0:T(8,128)(2,1)S(1)}, bf16[2,96,512]{2,1,0:T(8,128)(2,1)}, u32[]{:S(2)}) copy-start(bf16[2,96,512]{2,1,0:T(8,128)(2,1)} %gateup.1) | copy-start | bytes 589828
  2.2 8.6 %collective-permute-start.2 = (bf16[96,640]{1,0:T(8,128)(2,1)S(1)}, bf16[96,640]{1,0:T(8,128)(2,1)S(1)}, u32[]{:S(2)}, u32[]{:S(2)}) collective-permute-start(bf16[96,640]{1,0:T(8,128)(2,1)S(1)} %get-tuple-element.157.refs_0_), channel_id=1, source_target_pairs={{0,24},{8,0},{16,8},{24,16},{1,25},{9,1},{17,9},{25,17},{2,26},{10... | collective-permute-start | bytes 368648 | tf_op jit(solution)/shard_map/ppermute | solution.py:726
  7.3 15.4 %collective-permute-start.7 = (bf16[288,768]{1,0:T(8,128)(2,1)S(1)}, bf16[288,768]{1,0:T(8,128)(2,1)S(1)}, u32[]{:S(2)}, u32[]{:S(2)}) collective-permute-start(bf16[288,768]{1,0:T(8,128)(2,1)S(1)} %get-tuple-element.153.p0.x0), channel_id=1, source_target_pairs={{0,3},{1,2},{2,1},{3,0},{4,7},{5,6},{6,5},{7,4},{8,11},{9,10},{10,... | collective-permute-start | bytes 1327112 | tf_op jit(solution)/shard_map/ppermute | solution.py:721
  9.8 19.6 %collective-permute-start.6 = (bf16[288,768]{1,0:T(8,128)(2,1)S(1)}, bf16[288,768]{1,0:T(8,128)(2,1)S(1)}, u32[]{:S(2)}, u32[]{:S(2)}) collective-permute-start(bf16[288,768]{1,0:T(8,128)(2,1)S(1)} %get-tuple-element.153.p0.x0), channel_id=1, source_target_pairs={{0,2},{1,3},{2,0},{3,1},{4,6},{5,7},{6,4},{7,5},{8,10},{9,11},{10,... | collective-permute-start | bytes 1327112 | tf_op jit(solution)/shard_map/ppermute | solution.py:721
  10.3 19.2 %collective-permute-start.5 = (bf16[288,768]{1,0:T(8,128)(2,1)S(1)}, bf16[288,768]{1,0:T(8,128)(2,1)S(1)}, u32[]{:S(2)}, u32[]{:S(2)}) collective-permute-start(bf16[288,768]{1,0:T(8,128)(2,1)S(1)} %get-tuple-element.153.p0.x0), channel_id=1, source_target_pairs={{0,1},{1,0},{2,3},{3,2},{4,5},{5,4},{6,7},{7,6},{8,9},{9,8},{10,11... | collective-permute-start | bytes 1327112 | tf_op jit(solution)/shard_map/ppermute | solution.py:721
  10.8 8.6 %collective-permute-start.1 = (bf16[96,640]{1,0:T(8,128)(2,1)S(1)}, bf16[96,640]{1,0:T(8,128)(2,1)S(1)}, u32[]{:S(2)}, u32[]{:S(2)}) collective-permute-start(bf16[96,640]{1,0:T(8,128)(2,1)S(1)} %get-tuple-element.157.refs_0_), channel_id=1, source_target_pairs={{0,16},{8,24},{16,0},{24,8},{1,17},{9,25},{17,1},{25,9},{2,18},{10... | collective-permute-start | bytes 368648 | tf_op jit(solution)/shard_map/ppermute | solution.py:726
  10.8 8.6 %collective-permute-start = (bf16[96,640]{1,0:T(8,128)(2,1)S(1)}, bf16[96,640]{1,0:T(8,128)(2,1)S(1)}, u32[]{:S(2)}, u32[]{:S(2)}) collective-permute-start(bf16[96,640]{1,0:T(8,128)(2,1)S(1)} %get-tuple-element.157.refs_0_), channel_id=1, source_target_pairs={{0,8},{8,16},{16,24},{24,0},{1,9},{9,17},{17,25},{25,1},{2,10},{10... | collective-permute-start | bytes 368648 | tf_op jit(solution)/shard_map/ppermute | solution.py:726
  20.1 1.6 collective-permute-start.3
  20.2 1.8 collective-permute-start.4
  30.1 13.8 %collective-permute-start.10 = (bf16[96,2304]{1,0:T(8,128)(2,1)S(1)}, bf16[96,2304]{1,0:T(8,128)(2,1)S(1)}, u32[]{:S(2)}, u32[]{:S(2)}) collective-permute-start(bf16[96,2304]{1,0:T(8,128)(2,1)S(1)} %join.1.refs_0_), channel_id=1, source_target_pairs={{0,8},{8,16},{16,24},{24,0},{1,9},{9,17},{17,25},{25,1},{2,10},{10... | collective-permute-start | bytes 1327112 | tf_op jit(solution)/shard_map/ppermute | solution.py:726
  30.2 11.0 %collective-permute-start.9 = (bf16[256,768]{1,0:T(8,128)(2,1)S(1)}, bf16[256,768]{1,0:T(8,128)(2,1)S(1)}, u32[]{:S(2)}, u32[]{:S(2)}) collective-permute-start(bf16[256,768]{1,0:T(8,128)(2,1)S(1)} %bitcast.25), channel_id=1, source_target_pairs={{0,2},{1,3},{2,0},{3,1},{4,6},{5,7},{6,4},{7,5},{8,10},{9,11},{10,... | collective-permute-start | bytes 1179656 | tf_op jit(solution)/shard_map/ppermute | solution.py:721
  31.6 10.8 %collective-permute-start.8 = (bf16[256,768]{1,0:T(8,128)(2,1)S(1)}, bf16[256,768]{1,0:T(8,128)(2,1)S(1)}, u32[]{:S(2)}, u32[]{:S(2)}) collective-permute-start(bf16[256,768]{1,0:T(8,128)(2,1)S(1)} %bitcast.26), channel_id=1, source_target_pairs={{0,1},{1,0},{2,3},{3,2},{4,5},{5,4},{6,7},{7,6},{8,9},{9,8},{10,11... | collective-permute-start | bytes 1179656 | tf_op jit(solution)/shard_map/ppermute | solution.py:721
  43.9 2.3 %collective-permute-start.11 = (bf16[1024,384]{1,0:T(8,128)(2,1)S(1)}, bf16[1024,384]{1,0:T(8,128)(2,1)S(1)}, u32[]{:S(2)}, u32[]{:S(2)}) collective-permute-start(bf16[1024,384]{1,0:T(8,128)(2,1)S(1)} %get-tuple-element.176.own), channel_id=1, source_target_pairs={{0,4},{4,0},{1,5},{5,1},{2,6},{6,2},{3,7},{7,3},{8,12},{12,8},{9,1... | collective-permute-start | bytes 2359304 | tf_op jit(solution)/shard_map/ppermute | solution.py:717
  46.2 12.2 %collective-permute-start.14 = (bf16[96,2304]{1,0:T(8,128)(2,1)S(1)}, bf16[96,2304]{1,0:T(8,128)(2,1)S(1)}, u32[]{:S(2)}, u32[]{:S(2)}) collective-permute-start(bf16[96,2304]{1,0:T(8,128)(2,1)S(1)} %join.1.refs_0_), channel_id=1, source_target_pairs={{0,24},{8,0},{16,8},{24,16},{1,25},{9,1},{17,9},{25,17},{2,26},{10... | collective-permute-start | bytes 1327112 | tf_op jit(solution)/shard_map/ppermute | solution.py:726
  48.2 8.8 %collective-permute-start.13 = (bf16[128,768]{1,0:T(8,128)(2,1)S(1)}, bf16[128,768]{1,0:T(8,128)(2,1)S(1)}, u32[]{:S(2)}, u32[]{:S(2)}) collective-permute-start(bf16[128,768]{1,0:T(8,128)(2,1)S(1)} %slice.46), channel_id=1, source_target_pairs={{0,2},{1,3},{2,0},{3,1},{4,6},{5,7},{6,4},{7,5},{8,10},{9,11},{10,... | collective-permute-start | bytes 589832 | tf_op jit(solution)/shard_map/ppermute | solution.py:721
  48.8 8.3 %collective-permute-start.12 = (bf16[128,768]{1,0:T(8,128)(2,1)S(1)}, bf16[128,768]{1,0:T(8,128)(2,1)S(1)}, u32[]{:S(2)}, u32[]{:S(2)}) collective-permute-start(bf16[128,768]{1,0:T(8,128)(2,1)S(1)} %slice.45), channel_id=1, source_target_pairs={{0,1},{1,0},{2,3},{3,2},{4,5},{5,4},{6,7},{7,6},{8,9},{9,8},{10,11... | collective-permute-start | bytes 589832 | tf_op jit(solution)/shard_map/ppermute | solution.py:721
  58.4 21.8 %collective-permute-start.15 = (bf16[96,2304]{1,0:T(8,128)(2,1)S(1)}, bf16[96,2304]{1,0:T(8,128)(2,1)S(1)}, u32[]{:S(2)}, u32[]{:S(2)}) collective-permute-start(bf16[96,2304]{1,0:T(8,128)(2,1)S(1)} %join.1.refs_0_), channel_id=1, source_target_pairs={{0,16},{8,24},{16,0},{24,8},{1,17},{9,25},{17,1},{25,9},{2,18},{10... | collective-permute-start | bytes 1327112 | tf_op jit(solution)/shard_map/ppermute | solution.py:726
  59.2 13.0 %collective-permute-start.18 = (bf16[1536,128]{1,0:T(8,128)(2,1)S(1)}, bf16[1536,128]{1,0:T(8,128)(2,1)S(1)}, u32[]{:S(2)}, u32[]{:S(2)}) collective-permute-start(bf16[1536,128]{1,0:T(8,128)(2,1)S(1)} %get-tuple-element.185.h0), channel_id=1, source_target_pairs={{0,3},{1,2},{2,1},{3,0},{4,7},{5,6},{6,5},{7,4},{8,11},{9,10},{10,... | collective-permute-start | bytes 1179656 | tf_op jit(solution)/shard_map/ppermute | solution.py:721
  60.6 18.3 %collective-permute-start.17 = (bf16[1536,128]{1,0:T(8,128)(2,1)S(1)}, bf16[1536,128]{1,0:T(8,128)(2,1)S(1)}, u32[]{:S(2)}, u32[]{:S(2)}) collective-permute-start(bf16[1536,128]{1,0:T(8,128)(2,1)S(1)} %get-tuple-element.185.h0), channel_id=1, source_target_pairs={{0,2},{1,3},{2,0},{3,1},{4,6},{5,7},{6,4},{7,5},{8,10},{9,11},{10,... | collective-permute-start | bytes 1179656 | tf_op jit(solution)/shard_map/ppermute | solution.py:721
  61.4 17.5 %collective-permute-start.16 = (bf16[1536,128]{1,0:T(8,128)(2,1)S(1)}, bf16[1536,128]{1,0:T(8,128)(2,1)S(1)}, u32[]{:S(2)}, u32[]{:S(2)}) collective-permute-start(bf16[1536,128]{1,0:T(8,128)(2,1)S(1)} %get-tuple-element.185.h0), channel_id=1, source_target_pairs={{0,1},{1,0},{2,3},{3,2},{4,5},{5,4},{6,7},{7,6},{8,9},{9,8},{10,11... | collective-permute-start | bytes 1179656 | tf_op jit(solution)/shard_map/ppermute | solution.py:721
  80.9 3.8 %collective-permute-start.19 = (bf16[4,96,2304]{2,1,0:T(8,128)(2,1)S(1)}, bf16[4,96,2304]{2,1,0:T(8,128)(2,1)S(1)}, u32[]{:S(2)}, u32[]{:S(2)}) collective-permute-start(bf16[4,96,2304]{2,1,0:T(8,128)(2,1)S(1)} %stack.43.own), channel_id=1, source_target_pairs={{0,4},{4,0},{1,5},{5,1},{2,6},{6,2},{3,7},{7,3},{8,12},{12,8},{9,1... | collective-permute-start | bytes 5308424 | tf_op jit(solution)/shard_map/ppermute | solution.py:717
  97.0 3.7 %collective-permute-start.20 = (bf16[4,96,1536]{2,1,0:T(8,128)(2,1)S(1)}, bf16[4,96,1536]{2,1,0:T(8,128)(2,1)S(1)}, u32[]{:S(2)}, u32[]{:S(2)}) collective-permute-start(bf16[4,96,1536]{2,1,0:T(8,128)(2,1)S(1)} %get-tuple-element.200), channel_id=1, source_target_pairs={{0,4},{4,0},{1,5},{5,1},{2,6},{6,2},{3,7},{7,3},{8,12},{12,8},{9,1... | collective-permute-start | bytes 3538952 | tf_op jit(solution)/shard_map/ppermute | solution.py:717
  97.2 20.0 %collective-permute-start.22 = (bf16[256,768]{1,0:T(8,128)(2,1)S(1)}, bf16[256,768]{1,0:T(8,128)(2,1)S(1)}, u32[]{:S(2)}, u32[]{:S(2)}) collective-permute-start(bf16[256,768]{1,0:T(8,128)(2,1)S(1)} %get-tuple-element.208), channel_id=1, source_target_pairs={{0,1},{1,0},{2,3},{3,2},{4,5},{5,4},{6,7},{7,6},{8,9},{9,8},{10,11... | collective-permute-start | bytes 1179656 | tf_op jit(solution)/shard_map/ppermute | solution.py:721
  98.6 19.5 %collective-permute-start.23 = (bf16[256,768]{1,0:T(8,128)(2,1)S(1)}, bf16[256,768]{1,0:T(8,128)(2,1)S(1)}, u32[]{:S(2)}, u32[]{:S(2)}) collective-permute-start(bf16[256,768]{1,0:T(8,128)(2,1)S(1)} %get-tuple-element.209), channel_id=1, source_target_pairs={{0,2},{1,3},{2,0},{3,1},{4,6},{5,7},{6,4},{7,5},{8,10},{9,11},{10,... | collective-permute-start | bytes 1179656 | tf_op jit(solution)/shard_map/ppermute | solution.py:721
  98.8 19.4 %collective-permute-start.24 = (bf16[256,768]{1,0:T(8,128)(2,1)S(1)}, bf16[256,768]{1,0:T(8,128)(2,1)S(1)}, u32[]{:S(2)}, u32[]{:S(2)}) collective-permute-start(bf16[256,768]{1,0:T(8,128)(2,1)S(1)} %get-tuple-element.210), channel_id=1, source_target_pairs={{0,3},{1,2},{2,1},{3,0},{4,7},{5,6},{6,5},{7,4},{8,11},{9,10},{10,... | collective-permute-start | bytes 1179656 | tf_op jit(solution)/shard_map/ppermute | solution.py:721
  101.5 15.7 %collective-permute-start.21 = (bf16[96,1536]{1,0:T(8,128)(2,1)S(1)}, bf16[96,1536]{1,0:T(8,128)(2,1)S(1)}, u32[]{:S(2)}, u32[]{:S(2)}) collective-permute-start(bf16[96,1536]{1,0:T(8,128)(2,1)S(1)} %get-tuple-element.203), channel_id=1, source_target_pairs={{0,16},{8,24},{16,0},{24,8},{1,17},{9,25},{17,1},{25,9},{2,18},{10... | collective-permute-start | bytes 884744 | tf_op jit(solution)/shard_map/ppermute | solution.py:726
  119.7 9.1 %collective-permute-start.28 = (bf16[96,1536]{1,0:T(8,128)(2,1)S(1)}, bf16[96,1536]{1,0:T(8,128)(2,1)S(1)}, u32[]{:S(2)}, u32[]{:S(2)}) collective-permute-start(bf16[96,1536]{1,0:T(8,128)(2,1)S(1)} %get-tuple-element.225), channel_id=1, source_target_pairs={{0,24},{8,0},{16,8},{24,16},{1,25},{9,1},{17,9},{25,17},{2,26},{10... | collective-permute-start | bytes 884744 | tf_op jit(solution)/shard_map/ppermute | solution.py:726
  121.3 6.3 %collective-permute-start.25 = (bf16[384,128]{1,0:T(8,128)(2,1)S(1)}, bf16[384,128]{1,0:T(8,128)(2,1)S(1)}, u32[]{:S(2)}, u32[]{:S(2)}) collective-permute-start(bf16[384,128]{1,0:T(8,128)(2,1)S(1)} %get-tuple-element.219), channel_id=1, source_target_pairs={{0,1},{1,0},{2,3},{3,2},{4,5},{5,4},{6,7},{7,6},{8,9},{9,8},{10,11... | collective-permute-start | bytes 294920 | tf_op jit(solution)/shard_map/ppermute | solution.py:721
  122.6 5.1 %collective-permute-start.26 = (bf16[384,128]{1,0:T(8,128)(2,1)S(1)}, bf16[384,128]{1,0:T(8,128)(2,1)S(1)}, u32[]{:S(2)}, u32[]{:S(2)}) collective-permute-start(bf16[384,128]{1,0:T(8,128)(2,1)S(1)} %get-tuple-element.220), channel_id=1, source_target_pairs={{0,2},{1,3},{2,0},{3,1},{4,6},{5,7},{6,4},{7,5},{8,10},{9,11},{10,... | collective-permute-start | bytes 294920 | tf_op jit(solution)/shard_map/ppermute | solution.py:721
  123.4 5.5 %collective-permute-start.27 = (bf16[384,128]{1,0:T(8,128)(2,1)S(1)}, bf16[384,128]{1,0:T(8,128)(2,1)S(1)}, u32[]{:S(2)}, u32[]{:S(2)}) collective-permute-start(bf16[384,128]{1,0:T(8,128)(2,1)S(1)} %get-tuple-element.221), channel_id=1, source_target_pairs={{0,3},{1,2},{2,1},{3,0},{4,7},{5,6},{6,5},{7,4},{8,11},{9,10},{10,... | collective-permute-start | bytes 294920 | tf_op jit(solution)/shard_map/ppermute | solution.py:721
  128.9 12.7 %collective-permute-start.29 = (bf16[4,96,768]{2,1,0:T(8,128)(2,1)S(1)}, bf16[4,96,768]{2,1,0:T(8,128)(2,1)S(1)}, u32[]{:S(2)}, u32[]{:S(2)}) collective-permute-start(bf16[4,96,768]{2,1,0:T(8,128)(2,1)S(1)} %get-tuple-element.226), channel_id=1, source_target_pairs={{0,4},{4,0},{1,5},{5,1},{2,6},{6,2},{3,7},{7,3},{8,12},{12,8},{9,1... | collective-permute-start | bytes 1769480 | tf_op jit(solution)/shard_map/ppermute | solution.py:717
  128.9 12.7 %collective-permute-start.30 = (bf16[256,768]{1,0:T(8,128)(2,1)S(1)}, bf16[256,768]{1,0:T(8,128)(2,1)S(1)}, u32[]{:S(2)}, u32[]{:S(2)}) collective-permute-start(bf16[256,768]{1,0:T(8,128)(2,1)S(1)} %get-tuple-element.228), channel_id=1, source_target_pairs={{0,1},{1,0},{2,3},{3,2},{4,5},{5,4},{6,7},{7,6},{8,9},{9,8},{10,11... | collective-permute-start | bytes 1179656 | tf_op jit(solution)/shard_map/ppermute | solution.py:721
  130.2 11.4 %collective-permute-start.31 = (bf16[256,768]{1,0:T(8,128)(2,1)S(1)}, bf16[256,768]{1,0:T(8,128)(2,1)S(1)}, u32[]{:S(2)}, u32[]{:S(2)}) collective-permute-start(bf16[256,768]{1,0:T(8,128)(2,1)S(1)} %get-tuple-element.230), channel_id=1, source_target_pairs={{0,2},{1,3},{2,0},{3,1},{4,6},{5,7},{6,4},{7,5},{8,10},{9,11},{10,... | collective-permute-start | bytes 1179656 | tf_op jit(solution)/shard_map/ppermute | solution.py:721
  130.9 10.7 %collective-permute-start.32 = (bf16[96,1536]{1,0:T(8,128)(2,1)S(1)}, bf16[96,1536]{1,0:T(8,128)(2,1)S(1)}, u32[]{:S(2)}, u32[]{:S(2)}) collective-permute-start(bf16[96,1536]{1,0:T(8,128)(2,1)S(1)} %get-tuple-element.232), channel_id=1, source_target_pairs={{0,8},{8,16},{16,24},{24,0},{1,9},{9,17},{17,25},{25,1},{2,10},{10... | collective-permute-start | bytes 884744 | tf_op jit(solution)/shard_map/ppermute | solution.py:726
  141.6 2.4 %collective-permute-start.33 = (bf16[1024,384]{1,0:T(8,128)(2,1)S(1)}, bf16[1024,384]{1,0:T(8,128)(2,1)S(1)}, u32[]{:S(2)}, u32[]{:S(2)}) collective-permute-start(bf16[1024,384]{1,0:T(8,128)(2,1)S(1)} %get-tuple-element.233), channel_id=1, source_target_pairs={{0,4},{4,0},{1,5},{5,1},{2,6},{6,2},{3,7},{7,3},{8,12},{12,8},{9,1... | collective-permute-start | bytes 2359304 | tf_op jit(solution)/shard_map/ppermute | solution.py:717
  143.9 12.1 %collective-permute-start.34 = (bf16[256,768]{1,0:T(8,128)(2,1)S(1)}, bf16[256,768]{1,0:T(8,128)(2,1)S(1)}, u32[]{:S(2)}, u32[]{:S(2)}) collective-permute-start(bf16[256,768]{1,0:T(8,128)(2,1)S(1)} %get-tuple-element.248), channel_id=1, source_target_pairs={{0,3},{1,2},{2,1},{3,0},{4,7},{5,6},{6,5},{7,4},{8,11},{9,10},{10,... | collective-permute-start | bytes 1179656 | tf_op jit(solution)/shard_map/ppermute | solution.py:721
  146.0 9.7 %collective-permute-start.35 = (bf16[96,768]{1,0:T(8,128)(2,1)S(1)}, bf16[96,768]{1,0:T(8,128)(2,1)S(1)}, u32[]{:S(2)}, u32[]{:S(2)}) collective-permute-start(bf16[96,768]{1,0:T(8,128)(2,1)S(1)} %context_sum.4), channel_id=1, source_target_pairs={{0,16},{8,24},{16,0},{24,8},{1,17},{9,25},{17,1},{25,9},{2,18},{10... | collective-permute-start | bytes 442376 | tf_op jit(solution)/shard_map/ppermute | solution.py:726
  156.0 3.5 %collective-permute-start.36 = (bf16[4,96,640]{2,1,0:T(8,128)(2,1)S(1)}, bf16[4,96,640]{2,1,0:T(8,128)(2,1)S(1)}, u32[]{:S(2)}, u32[]{:S(2)}) collective-permute-start(bf16[4,96,640]{2,1,0:T(8,128)(2,1)S(1)} %get-tuple-element.249), channel_id=1, source_target_pairs={{0,4},{4,0},{1,5},{5,1},{2,6},{6,2},{3,7},{7,3},{8,12},{12,8},{9,1... | collective-permute-start | bytes 1474568 | tf_op jit(solution)/shard_map/ppermute | solution.py:717
  156.0 11.9 %collective-permute-start.37 = (bf16[256,768]{1,0:T(8,128)(2,1)S(1)}, bf16[256,768]{1,0:T(8,128)(2,1)S(1)}, u32[]{:S(2)}, u32[]{:S(2)}) collective-permute-start(bf16[256,768]{1,0:T(8,128)(2,1)S(1)} %get-tuple-element.256), channel_id=1, source_target_pairs={{0,1},{1,0},{2,3},{3,2},{4,5},{5,4},{6,7},{7,6},{8,9},{9,8},{10,11... | collective-permute-start | bytes 1179656 | tf_op jit(solution)/shard_map/ppermute | solution.py:721
  157.3 19.7 %collective-permute-start.38 = (bf16[256,768]{1,0:T(8,128)(2,1)S(1)}, bf16[256,768]{1,0:T(8,128)(2,1)S(1)}, u32[]{:S(2)}, u32[]{:S(2)}) collective-permute-start(bf16[256,768]{1,0:T(8,128)(2,1)S(1)} %get-tuple-element.257), channel_id=1, source_target_pairs={{0,2},{1,3},{2,0},{3,1},{4,6},{5,7},{6,4},{7,5},{8,10},{9,11},{10,... | collective-permute-start | bytes 1179656 | tf_op jit(solution)/shard_map/ppermute | solution.py:721
  158.0 19.0 %collective-permute-start.39 = (bf16[256,768]{1,0:T(8,128)(2,1)S(1)}, bf16[256,768]{1,0:T(8,128)(2,1)S(1)}, u32[]{:S(2)}, u32[]{:S(2)}) collective-permute-start(bf16[256,768]{1,0:T(8,128)(2,1)S(1)} %get-tuple-element.258), channel_id=1, source_target_pairs={{0,3},{1,2},{2,1},{3,0},{4,7},{5,6},{6,5},{7,4},{8,11},{9,10},{10,... | collective-permute-start | bytes 1179656 | tf_op jit(solution)/shard_map/ppermute | solution.py:721
  160.2 18.6 %collective-permute-start.40 = (bf16[96,640]{1,0:T(8,128)(2,1)S(1)}, bf16[96,640]{1,0:T(8,128)(2,1)S(1)}, u32[]{:S(2)}, u32[]{:S(2)}) collective-permute-start(bf16[96,640]{1,0:T(8,128)(2,1)S(1)} %get-tuple-element.261), channel_id=1, source_target_pairs={{0,16},{8,24},{16,0},{24,8},{1,17},{9,25},{17,1},{25,9},{2,18},{10... | collective-permute-start | bytes 368648 | tf_op jit(solution)/shard_map/ppermute | solution.py:726
  162.1 18.2 %collective-permute-start.41 = (bf16[96,1408]{1,0:T(8,128)(2,1)S(1)}, bf16[96,1408]{1,0:T(8,128)(2,1)S(1)}, u32[]{:S(2)}, u32[]{:S(2)}) collective-permute-start(bf16[96,1408]{1,0:T(8,128)(2,1)S(1)} %get-tuple-element.262), channel_id=1, source_target_pairs={{0,8},{8,16},{16,24},{24,0},{1,9},{9,17},{17,25},{25,1},{2,10},{10... | collective-permute-start | bytes 811016 | tf_op jit(solution)/shard_map/ppermute | solution.py:726
  167.9 12.4 %collective-permute-start.42 = (bf16[96,1408]{1,0:T(8,128)(2,1)S(1)}, bf16[96,1408]{1,0:T(8,128)(2,1)S(1)}, u32[]{:S(2)}, u32[]{:S(2)}) collective-permute-start(bf16[96,1408]{1,0:T(8,128)(2,1)S(1)} %get-tuple-element.263), channel_id=1, source_target_pairs={{0,24},{8,0},{16,8},{24,16},{1,25},{9,1},{17,9},{25,17},{2,26},{10... | collective-permute-start | bytes 811016 | tf_op jit(solution)/shard_map/ppermute | solution.py:726
  181.1 5.6 %collective-permute-start.43 = (bf16[112,192]{1,0:T(8,128)(2,1)S(1)}, bf16[112,192]{1,0:T(8,128)(2,1)S(1)}, u32[]{:S(2)}, u32[]{:S(2)}) collective-permute-start(bf16[112,192]{1,0:T(8,128)(2,1)S(1)} %get-tuple-element.268), channel_id=1, source_target_pairs={{0,1},{1,0},{2,3},{3,2},{4,5},{5,4},{6,7},{7,6},{8,9},{9,8},{10,11... | collective-permute-start | bytes 129032 | tf_op jit(solution)/shard_map/ppermute | solution.py:721
  182.5 4.8 %collective-permute-start.44 = (bf16[112,192]{1,0:T(8,128)(2,1)S(1)}, bf16[112,192]{1,0:T(8,128)(2,1)S(1)}, u32[]{:S(2)}, u32[]{:S(2)}) collective-permute-start(bf16[112,192]{1,0:T(8,128)(2,1)S(1)} %get-tuple-element.269), channel_id=1, source_target_pairs={{0,2},{1,3},{2,0},{3,1},{4,6},{5,7},{6,4},{7,5},{8,10},{9,11},{10,... | collective-permute-start | bytes 129032 | tf_op jit(solution)/shard_map/ppermute | solution.py:721
  183.2 5.1 %collective-permute-start.45 = (bf16[112,192]{1,0:T(8,128)(2,1)S(1)}, bf16[112,192]{1,0:T(8,128)(2,1)S(1)}, u32[]{:S(2)}, u32[]{:S(2)}) collective-permute-start(bf16[112,192]{1,0:T(8,128)(2,1)S(1)} %get-tuple-element.265), channel_id=1, source_target_pairs={{0,3},{1,2},{2,1},{3,0},{4,7},{5,6},{6,5},{7,4},{8,11},{9,10},{10,... | collective-permute-start | bytes 129032 | tf_op jit(solution)/shard_map/ppermute | solution.py:721
  (23 other events, 105.3 us)
